TPU v7x, 256 devices: a whole 4x4x8 slice. The times are simulated.
256 devices in a mesh: seq: 32 (over x, z), dp: 8 (over y, core).
Axes of the slice: x: 4, y: 4, z: 8, core: 2. Of those that a mesh axis runs over, the one named last changes fastest.
Arguments:
- inputs: bfloat16 [8, 4096, 2048], P('dp', 'seq')
- step_sizes: float32 [8, 64, 4096], P('dp', None, 'seq'), may hold values from 0.02 to 0.1
- gate: float32 [8, 4096], P('dp', 'seq')
- decay_rate: float32 [64], replicated
- skip: float32 [64], replicated, may hold values from 0.5 to 1.5
- keys: bfloat16 [8, 4096, 512], P('dp', 'seq'), may hold values from -1.1953125 to 1.1953125
- queries: bfloat16 [8, 4096, 512], P('dp', 'seq'), may hold values from -1.1953125 to 1.1953125
- grads: bfloat16 [8, 4096, 2048], P('dp', 'seq')
Outputs:
- d_inputs: bfloat16 [8, 4096, 2048], P('dp', 'seq')
- d_step_sizes: float32 [8, 64, 4096], P('dp', None, 'seq')
- d_keys: bfloat16 [8, 4096, 512], P('dp', 'seq')
- d_queries: bfloat16 [8, 4096, 512], P('dp', 'seq')
- d_log_rate: float32 [64], replicated
- d_skip: float32 [64], replicated
All inputs are finite; a program needn't handle non-finite values.
Results may differ from a plain program's by a relative error of at most 0.0057.
Values sent between devices are 32-bit elements; how exact they have to be, the bound alone decides.
No kernel may reach another device: no remote copies, remote signals or barrier semaphores. Data moves between devices by JAX's collectives and lax.ppermute only.
A program may use at most 192 MiB of HBM per device.

v0:
```python
import jax
import jax.numpy as jnp
from jax import lax
from jax.sharding import PartitionSpec as P

H = 64
P_SIZE = 32
N = 128
G = 4
K = 16


highest = lax.Precision.HIGHEST


def prefix(value, axis, join, neutral, backward):
    count, mine = (lax.axis_size(axis), lax.axis_index(axis))
    pieces = jax.tree.map(lambda part: lax.all_gather(part, axis), value)
    if backward:
        pieces = jax.tree.map(lambda part: part[::-1], pieces)
        mine = count - 1 - mine
    so_far = jax.tree.map(
        lambda part, zero: jnp.full_like(part, 0) + jnp.asarray(zero, part.dtype), value, neutral
    )

    def hop(position, so_far):
        longer = join(so_far, jax.tree.map(lambda part: part[position], pieces))
        return jax.tree.map(lambda new, old: jnp.where(position < mine, new, old), longer, so_far)

    return lax.fori_loop(0, count - 1, hop, so_far)


def lower_ones(length):
    row_index = lax.broadcasted_iota(jnp.int32, (length, length), 0)
    col_index = lax.broadcasted_iota(jnp.int32, (length, length), 1)
    return (row_index >= col_index).astype(jnp.float32)


def block_logs(step_rows, gate_row, rate_slice, lower_mask):
    log_decay = gate_row[None, :] - rate_slice[:, None] * step_rows
    return jnp.dot(log_decay, lower_mask.T, precision=highest)


def block_state(input_rows, step_rows, cumulative, key_rows):
    tail_decay = jnp.exp(cumulative[:, -1:] - cumulative)
    weighted_inputs = (
        input_rows.astype(jnp.float32) * (tail_decay * step_rows).T[:, :, None]
    ).astype(jnp.bfloat16)
    local_state = jnp.einsum(
        "tkp,tn->kpn", weighted_inputs, key_rows, preferred_element_type=jnp.float32
    )
    return (jnp.exp(cumulative[:, -1]), local_state)


def block_seed(grad_rows, cumulative, query_rows):
    weighted_grads = (grad_rows.astype(jnp.float32) * jnp.exp(cumulative).T[:, :, None]).astype(
        jnp.bfloat16
    )
    return jnp.einsum("tkp,tn->kpn", weighted_grads, query_rows, preferred_element_type=jnp.float32)


def block_grads(
    input_rows,
    grad_rows,
    step_rows,
    cumulative,
    lower_mask,
    rate_slice,
    skip_slice,
    key_rows,
    query_rows,
    state_in,
    adjoint_out,
):
    length = cumulative.shape[1]
    input_full = input_rows.astype(jnp.float32)
    grad_full = grad_rows.astype(jnp.float32)
    tail_decay = jnp.exp(cumulative[:, -1:] - cumulative)
    growth = jnp.exp(cumulative)
    causal = (lower_mask > 0)[None]
    gaps = cumulative[:, :, None] - cumulative[:, None, :]
    decays = jnp.where(causal, jnp.exp(jnp.where(causal, gaps, 0.0)), 0.0)
    scores = jnp.dot(query_rows, key_rows.T, preferred_element_type=jnp.float32)
    mixing = decays * scores[None]
    mixing_low = mixing.astype(jnp.bfloat16)
    state_low = state_in.astype(jnp.bfloat16)
    adjoint_low = adjoint_out.astype(jnp.bfloat16)
    intra_term = jnp.einsum(
        "kts,tkp->skp", mixing_low, grad_rows, preferred_element_type=jnp.float32
    )
    state_term = jnp.einsum(
        "kpn,sn->skp", adjoint_low, key_rows, preferred_element_type=jnp.float32
    )
    d_scaled = intra_term + tail_decay.T[:, :, None] * state_term
    d_inputs = d_scaled * step_rows.T[:, :, None] + skip_slice[None, :, None] * grad_full
    head_dots = jnp.einsum(
        "tkp,skp->kts", grad_rows, input_rows, preferred_element_type=jnp.float32
    )
    pair_dots = head_dots * step_rows[:, None, :]
    weighted = mixing * pair_dots
    shared_low = jnp.sum(decays * pair_dots, axis=0).astype(jnp.bfloat16)
    carried = jnp.einsum("kpn,tn->tkp", state_low, query_rows, preferred_element_type=jnp.float32)
    entry_products = jnp.einsum(
        "tkp,kpn->tkn", grad_rows, state_low, preferred_element_type=jnp.float32
    )
    d_queries = jnp.dot(shared_low, key_rows, preferred_element_type=jnp.float32) + jnp.sum(
        entry_products * growth.T[:, :, None], axis=1
    )
    exit_products = jnp.einsum(
        "skp,kpn->skn", input_rows, adjoint_low, preferred_element_type=jnp.float32
    )
    exit_weight = step_rows * tail_decay
    d_keys = jnp.dot(shared_low.T, query_rows, preferred_element_type=jnp.float32) + jnp.sum(
        exit_products * exit_weight.T[:, :, None], axis=1
    )
    entry_term = growth * jnp.sum(grad_full * carried, axis=2).T
    exit_term = exit_weight * jnp.sum(input_full * state_term, axis=2).T
    final_slot = (lax.broadcasted_iota(jnp.int32, (1, length), 1) == length - 1).astype(jnp.float32)
    closing = jnp.exp(cumulative[:, -1]) * jnp.sum(adjoint_out * state_in, axis=(1, 2)) + jnp.sum(
        exit_term, axis=1
    )
    d_cumulative = (
        jnp.sum(weighted, axis=2)
        - jnp.sum(weighted, axis=1)
        + entry_term
        - exit_term
        + closing[:, None] * final_slot
    )
    d_logs = jnp.dot(d_cumulative, lower_mask, precision=highest)
    d_steps = jnp.sum(d_scaled * input_full, axis=2).T - rate_slice[:, None] * d_logs
    rate_part = -rate_slice * jnp.sum(step_rows * d_logs, axis=1)
    return (
        d_inputs.astype(jnp.bfloat16),
        d_steps,
        d_keys.astype(jnp.bfloat16),
        d_queries.astype(jnp.bfloat16),
        rate_part,
    )


def chain_link(earlier, later):
    return (earlier[0] * later[0], later[0][:, None, None] * earlier[1] + later[1])


def on_device(inputs, step_sizes, gate, decay_rate, skip, keys, queries, grads):
    length_dev = inputs.shape[1]
    input_heads = inputs[0].reshape(length_dev, H, P_SIZE)
    grad_heads = grads[0].reshape(length_dev, H, P_SIZE)
    step_rows = step_sizes[0]
    gate_row = gate[0]
    key_groups = keys[0].reshape(length_dev, G, N)
    query_groups = queries[0].reshape(length_dev, G, N)
    lower_mask = lower_ones(length_dev)
    tokens_all = length_dev * lax.axis_size("seq") * lax.axis_size("dp")
    skip_part = jnp.einsum(
        "tkp,tkp->k", input_heads, grad_heads, preferred_element_type=jnp.float32
    )

    def prepare(group_index):
        head_span = slice(group_index * K, (group_index + 1) * K)
        cumulative = block_logs(step_rows[head_span], gate_row, decay_rate[head_span], lower_mask)
        block_decay, local_state = block_state(
            input_heads[:, head_span], step_rows[head_span], cumulative, key_groups[:, group_index]
        )
        adjoint_seed = block_seed(
            grad_heads[:, head_span], cumulative, query_groups[:, group_index]
        )
        return (cumulative, block_decay, local_state, adjoint_seed)

    results = []
    prepared = [prepare(group_index) for group_index in range(G)]
    all_decay = jnp.concatenate([prepared_set[1] for prepared_set in prepared])
    all_local = jnp.concatenate([prepared_set[2] for prepared_set in prepared])
    all_seed = jnp.concatenate([prepared_set[3] for prepared_set in prepared])
    identity = (jnp.ones_like(all_decay), jnp.zeros_like(all_local))
    state_all = prefix((all_decay, all_local), "seq", chain_link, identity, False)[1]
    adjoint_all = prefix((all_decay, all_seed), "seq", chain_link, identity, True)[1]
    for group_index in range(G):
        head_span = slice(group_index * K, (group_index + 1) * K)
        finish_cumulative = prepared[group_index][0]
        state_in = state_all[head_span]
        adjoint_out = adjoint_all[head_span]
        finish_head_span = slice(group_index * K, (group_index + 1) * K)
        results.append(
            block_grads(
                input_heads[:, finish_head_span],
                grad_heads[:, finish_head_span],
                step_rows[finish_head_span],
                finish_cumulative,
                lower_mask,
                decay_rate[finish_head_span],
                skip[finish_head_span],
                key_groups[:, group_index],
                query_groups[:, group_index],
                state_in,
                adjoint_out,
            )
        )
    d_inputs = jnp.concatenate([outcome[0] for outcome in results], axis=1).reshape(
        1, length_dev, H * P_SIZE
    )
    d_steps = jnp.concatenate([outcome[1] for outcome in results], axis=0)[None]
    d_keys = jnp.stack([outcome[2] for outcome in results], axis=1).reshape(1, length_dev, G * N)
    d_queries = jnp.stack([outcome[3] for outcome in results], axis=1).reshape(1, length_dev, G * N)
    rate_part = jnp.concatenate([outcome[4] for outcome in results])
    rate_total_sum, skip_total_sum = lax.psum((rate_part, skip_part), ("seq", "dp"))
    return (
        d_inputs,
        d_steps,
        d_keys,
        d_queries,
        rate_total_sum / tokens_all,
        skip_total_sum / tokens_all,
    )


def solution(mesh):
    placed = (
        P("dp", "seq", None),
        P("dp", None, "seq"),
        P("dp", "seq"),
        P(),
        P(),
        P("dp", "seq", None),
        P("dp", "seq", None),
        P("dp", "seq", None),
    )
    return jax.shard_map(
        on_device,
        mesh=mesh,
        in_specs=placed,
        out_specs=(
            P("dp", "seq", None),
            P("dp", None, "seq"),
            P("dp", "seq", None),
            P("dp", "seq", None),
            P(),
            P(),
        ),
        check_vma=False,
    )
```

profile of v0, /device:TPU:16, one launch (start us, length us, event | category | flops | bytes accessed | tf_op | source)
XLA Modules:
  0.0 727.4 jit_solution(4083711294071486645)
XLA Ops:
  19.1 79.9 %all-reduce = f32[2048]{0:T(1024)S(1)} all-reduce(f32[2048]{0:T(1024)S(1)} %maximum_dynamic-update-slice_fusion), channel_id=2, replica_groups=mesh['seq'=32,'dp'=8] {'seq'}, use_global_device_ids=true, to_apply=%add | all-reduce | flops 2048 | bytes 16384
  104.5 150.3 %all-gather.6.cloned.1.call-done = f32[2048,32,128]{2,1,0:T(8,128)} async-done(((f32[64,32,128]{2,1,0:T(8,128)}), f32[2048,32,128]{2,1,0:T(8,128)}) %all-gather.6.cloned.1.call-update) | async-done | bytes 33554448 | tf_op jit(solution)/shard_map/all_gather | solution.py:18
  254.9 22.9 %rev.7 = f32[32,64,32,128]{3,2,1,0:T(8,128)} reverse(f32[32,64,32,128]{3,2,1,0:T(8,128)} %bitcast.468), dimensions={0} | reverse | bytes 67108864 | tf_op jit(solution)/shard_map/rev | solution.py:20
  277.7 47.4 %while.28 = (s32[]{:T(128)}, f32[64,32,128]{2,1,0:T(8,128)S(1)}, s32[]{:T(128)}, f32[32,64]{1,0:T(8,128)S(1)}, f32[32,64,32,128]{3,2,1,0:T(8,128)}, /*index=5*/s32[]{:T(128)}, s32[]{:T(128)}) while((s32[]{:T(128)}, f32[64,32,128]{2,1,0:T(8,128)S(1)}, s32[]{:T(128)}, f32[32,64]{1,0:T(8,128)S(1)}, f32[32,64,32,128]{3,2,1,0:T(8,128)}, ...), condition=%wide.region_1.2_spmd.clone, body=%wide.region_0.1_spmd.clone.sunk | while | flops 1048580 | bytes 3146601 | solution.py:30
  279.3 1.5 fusion.339
  280.8 1.5 fusion.339
  282.3 1.5 fusion.339
  283.9 1.5 fusion.339
  285.4 1.5 fusion.339
  286.9 1.5 fusion.339
  288.5 1.5 fusion.339
  290.0 1.5 fusion.339
  291.5 1.5 fusion.339
  293.0 1.5 fusion.339
  294.6 1.5 fusion.339
  296.1 1.5 fusion.339
  297.6 1.5 fusion.339
  299.2 1.5 fusion.339
  300.7 1.5 fusion.339
  302.2 1.5 fusion.339
  305.3 1.5 fusion.339
  309.9 1.5 fusion.339
  314.5 1.5 fusion.339
  316.0 1.5 fusion.339
  319.0 1.5 fusion.339
  320.6 1.5 fusion.339
  323.6 1.5 fusion.339
  327.9 2.0 fusion.93
  337.6 4.0 fusion.59
  350.7 212.3 %all-gather.8.cloned.1.call-done = f32[2048,32,128]{2,1,0:T(8,128)} async-done(((f32[64,32,128]{2,1,0:T(8,128)}), f32[2048,32,128]{2,1,0:T(8,128)}) %all-gather.8.cloned.1.call-update) | async-done | bytes 33554448 | tf_op jit(solution)/shard_map/all_gather | solution.py:18
  563.0 68.1 %while.29 = (s32[]{:T(128)}, f32[64,32,128]{2,1,0:T(8,128)S(1)}, s32[]{:T(128)}, f32[32,64]{1,0:T(8,128)}, f32[32,64,32,128]{3,2,1,0:T(8,128)}, /*index=5*/s32[]{:T(128)}, s32[]{:T(128)}) while((s32[]{:T(128)}, f32[64,32,128]{2,1,0:T(8,128)S(1)}, s32[]{:T(128)}, f32[32,64]{1,0:T(8,128)}, f32[32,64,32,128]{3,2,1,0:T(8,128)}, ...), condition=%wide.region_6.7_spmd.clone, body=%wide.region_5.6_spmd.clone.sunk | while | flops 1048580 | bytes 3146601 | solution.py:30
  644.5 73.0 %all-reduce.1 = (f32[64]{0:T(128)S(1)}, f32[64]{0:T(128)S(1)}) all-reduce(f32[64]{0:T(128)S(1)} %pad_maximum_fusion.5, f32[64]{0:T(128)} %fusion.46), channel_id=1, replica_groups=mesh['seq'=32,'dp'=8] {'seq','dp'}, use_global_device_ids=true, to_apply=%region_48.49 | all-reduce | flops 128 | bytes 1024 | tf_op jit(solution)/shard_map/psum | solution.py:206
  (275 shorter events, 131.7 us)
Async XLA Ops:
  7.2 247.7 %all-gather.6.cloned.1.call-start = ((), (), s32[]{:S(2)}) async-start(), calls=%async_computation | async-start | bytes 34603008 | tf_op jit(solution)/shard_map/all_gather | solution.py:18
  8.1 7.1 copy-start.29
  8.1 7.1 copy-start.30
  8.1 7.4 %copy-start.31 = (f32[16]{0:T(128)}, f32[16]{0:T(128)S(1)}, u32[]{:S(2)}) copy-start(f32[16]{0:T(128)S(1)} %get-tuple-element.360) | copy-start | bytes 196
  8.1 7.4 %copy-start.32 = (f32[16]{0:T(128)}, f32[16]{0:T(128)S(1)}, u32[]{:S(2)}) copy-start(f32[16]{0:T(128)S(1)} %get-tuple-element.357) | copy-start | bytes 196
  9.9 319.9 %copy-start.1 = (f32[16,128]{1,0:T(8,128)}, f32[16,128]{1,0:T(8,128)S(1)}, u32[]{:S(2)}) copy-start(f32[16,128]{1,0:T(8,128)S(1)} %fusion.168) | copy-start | bytes 24580
  10.2 319.7 %copy-start.26 = (f32[16]{0:T(128)}, f32[16]{0:T(128)S(1)}, u32[]{:S(2)}) copy-start(f32[16]{0:T(128)S(1)} %get-tuple-element.362) | copy-start | bytes 196
  10.2 319.7 %copy-start.27 = (f32[16]{0:T(128)}, f32[16]{0:T(128)S(1)}, u32[]{:S(2)}) copy-start(f32[16]{0:T(128)S(1)} %get-tuple-element.363) | copy-start | bytes 196
  10.3 8.8 %copy-start.14 = (f32[128,16]{0,1:T(8,128)}, f32[128,16]{0,1:T(8,128)S(1)}, u32[]{:S(2)}) copy-start(f32[128,16]{0,1:T(8,128)S(1)} %get-tuple-element.348) | copy-start | bytes 24580
  12.7 6.4 copy-start.15
  14.9 315.0 %copy-start.3 = (f32[16,128]{1,0:T(8,128)}, f32[16,128]{1,0:T(8,128)S(1)}, u32[]{:S(2)}) copy-start(f32[16,128]{1,0:T(8,128)S(1)} %fusion.170) | copy-start | bytes 24580
  15.2 314.7 %copy-start.25 = (f32[16]{0:T(128)}, f32[16]{0:T(128)S(1)}, u32[]{:S(2)}) copy-start(f32[16]{0:T(128)S(1)} %get-tuple-element.364) | copy-start | bytes 196
  15.2 314.7 %copy-start.28 = (f32[16]{0:T(128)}, f32[16]{0:T(128)S(1)}, u32[]{:S(2)}) copy-start(f32[16]{0:T(128)S(1)} %get-tuple-element.365) | copy-start | bytes 196
  15.3 239.6 %copy-start.16 = (f32[128,16]{0,1:T(8,128)}, f32[128,16]{0,1:T(8,128)S(1)}, u32[]{:S(2)}) copy-start(f32[128,16]{0,1:T(8,128)S(1)} %get-tuple-element.344) | copy-start | bytes 24580
  15.6 239.3 %copy-start.17 = (f32[128,16]{0,1:T(8,128)}, f32[128,16]{0,1:T(8,128)S(1)}, u32[]{:S(2)}) copy-start(f32[128,16]{0,1:T(8,128)S(1)} %get-tuple-element.342) | copy-start | bytes 24580
  16.9 546.2 %all-gather.8.cloned.1.call-start = ((), (), s32[]{:S(2)}) async-start(), calls=%async_computation.1 | async-start | bytes 34603008 | tf_op jit(solution)/shard_map/all_gather | solution.py:18
  99.1 155.8 %copy-start.13 = (f32[32,64]{1,0:T(8,128)}, f32[32,64]{1,0:T(8,128)S(1)}, u32[]{:S(2)}) copy-start(f32[32,64]{1,0:T(8,128)S(1)} %reshape.98) | copy-start | bytes 24580
  101.5 226.4 %copy-start.22 = (pred[128,128]{1,0:T(8,128)(4,1)}, pred[128,128]{1,0:T(8,128)(4,1)S(1)}, u32[]{:S(2)}) copy-start(pred[128,128]{1,0:T(8,128)(4,1)S(1)} %convert_compare_fusion) | copy-start | bytes 49156
  103.9 221.9 %copy-start.5 = (f32[128,128]{1,0:T(8,128)}, f32[128,128]{1,0:T(8,128)S(1)}, u32[]{:S(2)}) copy-start(f32[128,128]{1,0:T(8,128)S(1)} %fusion.188) | copy-start | bytes 196612
  104.1 222.2 %copy-start.7 = (f32[128,128]{1,0:T(8,128)}, f32[128,128]{1,0:T(8,128)S(1)}, u32[]{:S(2)}) copy-start(f32[128,128]{1,0:T(8,128)S(1)} %fusion.174) | copy-start | bytes 196612
  104.3 222.4 %copy-start.9 = (f32[128,128]{1,0:T(8,128)}, f32[128,128]{1,0:T(8,128)S(1)}, u32[]{:S(2)}) copy-start(f32[128,128]{1,0:T(8,128)S(1)} %fusion.181) | copy-start | bytes 196612
  104.5 223.4 %copy-start.11 = (f32[128,128]{1,0:T(8,128)}, f32[128,128]{1,0:T(8,128)S(1)}, u32[]{:S(2)}) copy-start(f32[128,128]{1,0:T(8,128)S(1)} %fusion.203) | copy-start | bytes 196612
  254.9 75.0 %copy-start = (f32[1,64,128]{2,1,0:T(8,128)S(1)}, f32[1,64,128]{2,1,0:T(8,128)}, u32[]{:S(2)}) copy-start(f32[1,64,128]{2,1,0:T(8,128)} %param.13) | copy-start | bytes 98308
  330.7 6.8 copy-start.18
  330.7 6.8 copy-start.19
  330.7 6.8 copy-start.20
  330.7 6.8 copy-start.21
  332.5 5.0 copy-start.2
  332.5 5.0 copy-start.4
  332.5 5.0 copy-start.6
  332.6 5.0 copy-start.8
  332.6 5.0 copy-start.10
  (3 other events, 12.5 us)
Sparse Core Ops, SparseCore 0:
  17.0 237.8 all-gather.5
  332.6 230.3 all-gather.7
where the time goes:
time: 735 us; the launch traced here: 727 us
  waiting for transfers between devices  363 us (49%)
  blocking collectives  153 us (21%)
  other arithmetic  103 us (14%)
  local copies, waits for them, and re-layouts  59 us (8%)
  matrix products  32.4 us (4%)
  between operations  15.4 us (2%)
    all_gather x2, waiting for transfers between devices, prefix(): pieces = jax.tree.map(lambda part: lax.all_gather(part, axis), value)  363 us
    select_n x62, other arithmetic, hop(): jnp.where(position < mine, new, old)  91.9 us
    unnamed x1, blocking collectives  79.9 us
    psum x1, blocking collectives, on_device(): lax.psum((rate_part, skip_part), ('seq', 'dp'))  73 us
    rev x2, local copies, waits for them, and re-layouts, prefix(): pieces = jax.tree.map(lambda part: part[::-1], pieces)  22.9 us
    mul x62, local copies, waits for them, and re-layouts, chain_link(): later[0][:, None, None] * earlier[1] + later[1]  21.9 us
  transfers between devices with their start and end apart: 2, of which 2 were waited for; matrix products, arithmetic and copies ran while one was open for 3% of the time, Pallas kernels for 0%

commit v1 on v0

v1 whole, which is shorter than its diff:
```python
import jax
import jax.numpy as jnp
from jax import lax
from jax.experimental import pallas as pl
from jax.experimental.pallas import tpu as pltpu
from jax.sharding import PartitionSpec as P

H = 64
P_SIZE = 32
N = 128
G = 4
K = 16
GP = K * P_SIZE

highest = lax.Precision.HIGHEST
f32 = jnp.float32
bf16 = jnp.bfloat16
VMEM_LIMIT = 48 * 1024 * 1024


def contract(left, right, dims):
    return lax.dot_general(left, right, ((dims[:1], dims[1:]), ((), ())), preferred_element_type=f32)


def per_feature(rows):
    heads, length = rows.shape
    return jnp.broadcast_to(rows[:, None, :], (heads, P_SIZE, length)).reshape(heads * P_SIZE, length)


def head_sum(features):
    return jnp.sum(features.reshape(-1, P_SIZE, features.shape[1]), axis=1)


def triangle(length, upper):
    row = lax.broadcasted_iota(jnp.int32, (length, length), 0)
    col = lax.broadcasted_iota(jnp.int32, (length, length), 1)
    return row <= col if upper else row >= col


def prepare_kernel(x_ref, dy_ref, step_ref, gate_ref, rate_ref, key_ref, query_ref,
                   send_ref, cum_ref, xt_ref, dyt_ref):
    length = x_ref.shape[0]
    step = step_ref[...]
    log_decay = gate_ref[...] - rate_ref[...] * step
    cum = jnp.dot(log_decay, triangle(length, True).astype(f32), precision=highest)
    cum_ref[...] = cum
    last = cum[:, length - 1:]
    x_t = x_ref[...].astype(f32).T
    dy_t = dy_ref[...].astype(f32).T
    xt_ref[...] = x_t.astype(bf16)
    dyt_ref[...] = dy_t.astype(bf16)
    weighted_inputs = (x_t * per_feature(step * jnp.exp(last - cum))).astype(bf16)
    weighted_grads = (dy_t * per_feature(jnp.exp(cum))).astype(bf16)
    local_state = contract(weighted_inputs, key_ref[...], (1, 0))
    seed = contract(weighted_grads, query_ref[...], (1, 0))
    owners, rows, _ = send_ref.shape
    per_owner = K // owners
    half = per_owner * P_SIZE
    send_ref[:, :half, :] = local_state.reshape(owners, half, N)
    send_ref[:, half:2 * half, :] = seed.reshape(owners, half, N)
    block_decay = jnp.broadcast_to(jnp.exp(last), (K, N))
    pad = rows - 2 * half
    for owner in range(owners):
        mine = block_decay[owner * per_owner:(owner + 1) * per_owner]
        if pad > per_owner:
            mine = jnp.concatenate([mine, jnp.zeros((pad - per_owner, N), f32)], axis=0)
        send_ref[owner, 2 * half:, :] = mine


def scan_kernel(blocks, half, recv_ref, out_ref):
    per_owner = half // P_SIZE

    def decay_of(block):
        return per_feature(recv_ref[block, 2 * half:2 * half + per_owner, :])

    state = jnp.zeros((half, N), f32)
    adjoint = jnp.zeros((half, N), f32)
    for forward in range(blocks):
        backward = blocks - 1 - forward
        out_ref[forward, :half, :] = state
        out_ref[backward, half:, :] = adjoint
        if forward < blocks - 1:
            state = decay_of(forward) * state + recv_ref[forward, :half, :]
            adjoint = decay_of(backward) * adjoint + recv_ref[backward, half:2 * half, :]


def intra_kernel(dy_ref, xt_ref, dyt_ref, step_ref, cum_ref, key_ref, query_ref,
                 intra_ref, dq_ref, dk_ref, flow_ref, own_ref, skip_ref):
    length = dy_ref.shape[0]
    keys, queries = key_ref[...], query_ref[...]
    scores = contract(queries, keys, (1, 1))
    causal = triangle(length, False)
    cum = cum_ref[...]
    cum_cols = cum.T
    step = step_ref[...]
    four = 128 // P_SIZE
    head_of_row = lax.broadcasted_iota(jnp.int32, (128, length), 0) // P_SIZE
    shared = jnp.zeros((length, length), f32)
    row_sums, col_sums = [], []
    for quad in range(K // four):
        lanes = slice(quad * 128, (quad + 1) * 128)
        x_quad = xt_ref[lanes, :].astype(f32)
        spread = jnp.concatenate(
            [jnp.where(head_of_row == i, x_quad, 0.0).astype(bf16) for i in range(four)], axis=1)
        dots = contract(dy_ref[:, lanes], spread, (1, 0))
        for i in range(four):
            head = quad * four + i
            gaps = cum_cols[:, head:head + 1] - cum[head:head + 1, :]
            decays = jnp.exp(jnp.where(causal, gaps, -1e30))
            mixing_low = (decays * scores).astype(bf16)
            pairs = decays * (dots[:, i * length:(i + 1) * length] * step[head:head + 1, :])
            shared = shared + pairs
            weighted = pairs * scores
            row_sums.append(jnp.sum(weighted, axis=1, keepdims=True))
            col_sums.append(jnp.sum(weighted, axis=0, keepdims=True))
            rows = slice(head * P_SIZE, (head + 1) * P_SIZE)
            intra_ref[rows, :] = contract(dyt_ref[rows, :], mixing_low, (1, 0))
    shared_low = shared.astype(bf16)
    dq_ref[...] = contract(shared_low, keys, (1, 0))
    dk_ref[...] = contract(shared_low, queries, (0, 0))
    flow_ref[...] = jnp.concatenate(row_sums, axis=1).T - jnp.concatenate(col_sums, axis=0)
    x_full = xt_ref[...].astype(f32)
    own_ref[...] = head_sum(x_full * intra_ref[...])
    skip_ref[...] = jnp.sum(head_sum(x_full * dyt_ref[...].astype(f32)), axis=1, keepdims=True)


def finish_kernel(states_ref, xt_ref, dyt_ref, step_ref, cum_ref, rate_ref, skip_ref, key_ref, query_ref,
                  intra_ref, dq_in_ref, dk_in_ref, flow_ref, own_ref,
                  dx_ref, dstep_ref, dk_ref, dq_ref, rate_part_ref):
    owners, rows, _ = states_ref.shape
    half = rows // 2
    length = step_ref.shape[1]
    state = states_ref[:, :half, :].reshape(GP, N)
    adjoint = states_ref[:, half:, :].reshape(GP, N)
    state_low, adjoint_low = state.astype(bf16), adjoint.astype(bf16)
    keys, queries = key_ref[...], query_ref[...]
    state_term = contract(adjoint_low, keys, (1, 1))
    carried = contract(state_low, queries, (1, 1))
    cum, step, rate = cum_ref[...], step_ref[...], rate_ref[...]
    last = cum[:, length - 1:]
    growth, tail = jnp.exp(cum), jnp.exp(last - cum)
    exit_weight = step * tail
    x_t, dy_t = xt_ref[...].astype(f32), dyt_ref[...].astype(f32)
    weighted_grads = (dy_t * per_feature(growth)).astype(bf16)
    weighted_inputs = (x_t * per_feature(exit_weight)).astype(bf16)
    dq_ref[...] = (dq_in_ref[...] + contract(weighted_grads, state_low, (0, 0))).astype(bf16)
    dk_ref[...] = (dk_in_ref[...] + contract(weighted_inputs, adjoint_low, (0, 0))).astype(bf16)
    entry_term = growth * head_sum(dy_t * carried)
    outside = head_sum(x_t * state_term)
    exit_term = exit_weight * outside
    closing = jnp.exp(last) * jnp.sum(head_sum(adjoint * state), axis=1, keepdims=True) + jnp.sum(
        exit_term, axis=1, keepdims=True)
    final_slot = lax.broadcasted_iota(jnp.int32, (K, length), 1) == length - 1
    d_cum = flow_ref[...] + entry_term - exit_term + jnp.where(final_slot, closing, 0.0)
    d_logs = jnp.dot(d_cum, triangle(length, False).astype(f32), precision=highest)
    dstep_ref[...] = own_ref[...] + tail * outside - rate * d_logs
    rate_part_ref[...] = -rate * jnp.sum(step * d_logs, axis=1, keepdims=True)
    d_scaled = intra_ref[...] + per_feature(tail) * state_term
    d_inputs = per_feature(step) * d_scaled + per_feature(jnp.broadcast_to(skip_ref[...], (K, length))) * dy_t
    dx_ref[...] = d_inputs.T.astype(bf16)


def total_over_devices(value):
    for axis in ("seq", "dp"):
        size, reach = lax.axis_size(axis), 1
        while reach < size:
            value = value + lax.ppermute(value, axis, [(i, i ^ reach) for i in range(size)])
            reach *= 2
    return value


def on_device(inputs, step_sizes, gate, decay_rate, skip, keys, queries, grads):
    length = inputs.shape[1]
    blocks = lax.axis_size("seq")
    tokens_all = length * blocks * lax.axis_size("dp")
    x, dy, step = inputs[0], grads[0], step_sizes[0]
    key_rows, query_rows = keys[0], queries[0]
    rate, skip_col = decay_rate.reshape(H, 1), skip.reshape(H, 1)
    per_owner = H // blocks
    half = per_owner * P_SIZE
    owners = blocks // G
    pad = -(-per_owner // 8) * 8

    tokens = pl.BlockSpec((length, GP), lambda g: (0, g))
    features = pl.BlockSpec((GP, length), lambda g: (g, 0))
    head_rows = pl.BlockSpec((K, length), lambda g: (g, 0))
    head_col = pl.BlockSpec((K, 1), lambda g: (g, 0))
    shared_row = pl.BlockSpec((1, length), lambda g: (0, 0))
    group_rows = pl.BlockSpec((length, N), lambda g: (0, g))
    params = pltpu.CompilerParams(vmem_limit_bytes=VMEM_LIMIT)

    def shape(dims, dtype=f32):
        return jax.ShapeDtypeStruct(dims, dtype)

    send, cum, x_t, dy_t = pl.pallas_call(
        prepare_kernel,
        grid=(G,),
        in_specs=[tokens, tokens, head_rows, shared_row, head_col, group_rows, group_rows],
        out_specs=[pl.BlockSpec((owners, 2 * half + pad, N), lambda g: (g, 0, 0)), head_rows, features, features],
        out_shape=[shape((blocks, 2 * half + pad, N)), shape((H, length)),
                   shape((H * P_SIZE, length), bf16), shape((H * P_SIZE, length), bf16)],
        compiler_params=params,
        cost_estimate=pl.CostEstimate(flops=70_000_000, bytes_accessed=5_000_000, transcendentals=20_000),
        name="prepare",
    )(x, dy, step, gate, rate, key_rows, query_rows)

    recv = lax.all_to_all(send, "seq", 0, 0)
    scanned = pl.pallas_call(
        lambda *refs: scan_kernel(blocks, half, *refs),
        out_shape=shape((blocks, 2 * half, N)),
        compiler_params=params,
        cost_estimate=pl.CostEstimate(flops=2_000_000, bytes_accessed=4_300_000, transcendentals=0),
        name="scan",
    )(recv)
    states = lax.all_to_all(scanned, "seq", 0, 0)

    intra, dq_intra, dk_intra, flow, own, skip_part = pl.pallas_call(
        intra_kernel,
        grid=(G,),
        in_specs=[tokens, features, features, head_rows, head_rows, group_rows, group_rows],
        out_specs=[features, group_rows, group_rows, head_rows, head_rows, head_col],
        out_shape=[shape((H * P_SIZE, length)), shape((length, G * N)), shape((length, G * N)),
                   shape((H, length)), shape((H, length)), shape((H, 1))],
        compiler_params=params,
        cost_estimate=pl.CostEstimate(flops=2_000_000_000, bytes_accessed=5_000_000, transcendentals=1_000_000),
        name="intra",
    )(dy, x_t, dy_t, step, cum, key_rows, query_rows)

    d_inputs, d_steps, d_keys, d_queries, rate_part = pl.pallas_call(
        finish_kernel,
        grid=(G,),
        in_specs=[pl.BlockSpec((owners, 2 * half, N), lambda g: (g, 0, 0)), features, features,
                  head_rows, head_rows, head_col, head_col, group_rows, group_rows,
                  features, group_rows, group_rows, head_rows, head_rows],
        out_specs=[tokens, head_rows, group_rows, group_rows, head_col],
        out_shape=[shape((length, H * P_SIZE), bf16), shape((H, length)),
                   shape((length, G * N), bf16), shape((length, G * N), bf16), shape((H, 1))],
        compiler_params=params,
        cost_estimate=pl.CostEstimate(flops=140_000_000, bytes_accessed=6_000_000, transcendentals=20_000),
        name="finish",
    )(states, x_t, dy_t, step, cum, rate, skip_col, key_rows, query_rows, intra, dq_intra, dk_intra, flow, own)

    totals = total_over_devices(jnp.concatenate([rate_part.reshape(1, H), skip_part.reshape(1, H)], axis=1))
    totals = totals[0] / tokens_all
    return (d_inputs[None], d_steps[None], d_keys[None], d_queries[None], totals[:H], totals[H:])


def solution(mesh):
    placed = (
        P("dp", "seq", None),
        P("dp", None, "seq"),
        P("dp", "seq"),
        P(),
        P(),
        P("dp", "seq", None),
        P("dp", "seq", None),
        P("dp", "seq", None),
    )
    return jax.shard_map(
        on_device,
        mesh=mesh,
        in_specs=placed,
        out_specs=(
            P("dp", "seq", None),
            P("dp", None, "seq"),
            P("dp", "seq", None),
            P("dp", "seq", None),
            P(),
            P(),
        ),
        check_vma=False,
    )
```

time: 735 us -> 179 us (0.24)
  waiting for transfers between devices: 363 us -> 57.8 us
  other arithmetic: 103 us -> 1.9 us
  blocking collectives: 153 us -> 66.5 us
  local copies, waits for them, and re-layouts: 59 us -> 22.1 us
  matrix products: 32.4 us -> 0 us
  between operations: 15.4 us -> 0.76 us
  starting transfers between devices: 0.08 us -> 14.6 us
  Pallas kernels: 0 us -> 14.3 us
    all_gather x2 -> x0, waiting for transfers between devices: 363 us -> none  [prefix(): pieces = jax.tree.map(lambda part: lax.all_gather(part, axis), value)]
    select_n x62 -> x0, other arithmetic: 91.9 us -> none  [hop(): jnp.where(position < mine, new, old)]
    unnamed x1 -> x0, blocking collectives: 79.9 us -> none
    psum x1 -> x0, blocking collectives: 73 us -> none  [on_device(): lax.psum((rate_part, skip_part), ('seq', 'dp'))]
    all_to_all x0 -> x1, blocking collectives: none -> 66.5 us  [on_device(): recv = lax.all_to_all(send, 'seq', 0, 0)]
    all_to_all x0 -> x1, waiting for transfers between devices: none -> 34.5 us  [on_device(): states = lax.all_to_all(scanned, 'seq', 0, 0)]
    dot_general x52 -> x0, matrix products: 32.4 us -> none  [the longest x4 7.13 us: block_grads(): jnp.einsum('tkp,skp->kts', grad_rows, input_rows, preferred_element_type=...]
    ppermute x0 -> x8, waiting for transfers between devices: none -> 23.3 us  [total_over_devices(): lax.ppermute(value, axis, [(i, i ^ reach) for i in range(size)])]
  transfers between devices with their start and end apart: 2 -> 9, of which waited for: 2 -> 9; matrix products, arithmetic and copies ran while one was open for 3% -> 1% of each run, Pallas kernels for 0% -> 4%
where the time goes in v1:
time: 179 us; the launch traced here: 178 us
  blocking collectives  66.5 us (37%)
  waiting for transfers between devices  57.8 us (32%)
  local copies, waits for them, and re-layouts  22.1 us (12%)
  starting transfers between devices  14.6 us (8%)
  Pallas kernels  14.3 us (8%)
  other arithmetic  1.9 us (1%)
    all_to_all x1, blocking collectives, on_device(): recv = lax.all_to_all(send, 'seq', 0, 0)  66.5 us
    all_to_all x1, waiting for transfers between devices, on_device(): states = lax.all_to_all(scanned, 'seq', 0, 0)  34.5 us
    ppermute x8, waiting for transfers between devices, total_over_devices(): lax.ppermute(value, axis, [(i, i ^ reach) for i in range(size)])  23.3 us
    unnamed x56, local copies, waits for them, and re-layouts  20.7 us
    ppermute x8, starting transfers between devices, total_over_devices(): lax.ppermute(value, axis, [(i, i ^ reach) for i in range(size)])  10.4 us
    pallas_call x1, Pallas kernels, on_device(): pl.pallas_call(intra_kernel, grid=(G,), in_specs=[tokens, features, featu...  7.78 us
    all_to_all x1, starting transfers between devices, on_device(): states = lax.all_to_all(scanned, 'seq', 0, 0)  4.15 us
    pallas_call x1, Pallas kernels, on_device(): pl.pallas_call(finish_kernel, grid=(G,), in_specs=[pl.BlockSpec((owners,...  3.8 us
  transfers between devices with their start and end apart: 9, of which 9 were waited for; matrix products, arithmetic and copies ran while one was open for 1% of the time, Pallas kernels for 4%

profile of v1, /device:TPU:16, one launch (start us, length us, event | category | flops | bytes accessed | tf_op | source)
XLA Modules:
  0.0 178.0 jit_solution(2882549270222501980)
XLA Ops:
  1.4 1.0 copy-done.1
  2.4 1.0 copy-done.2
  3.5 0.9 copy-done.10
  4.4 0.9 copy-done.12
  6.7 2.6 %prepare.1 = (f32[32,136,128]{2,1,0:T(8,128)S(1)}, f32[64,128]{1,0:T(8,128)S(1)}, bf16[2048,128]{1,0:T(8,128)(2,1)S(1)}, bf16[2048,128]{1,0:T(8,128)(2,1)S(1)}) custom-call(bf16[128,2048]{1,0:T(8,128)(2,1)S(1)} %bitcast.17, bf16[128,2048]{1,0:T(8,128)(2,1)S(1)} %bitcast.18, f32[64,128]{1,0:T(8,128)S(1)} %bitcast.26, f32[1,128]{1,0:T(1,128)S(1)} %copy-done.26, ...), custom_call_target="tpu_custom_call" | custom-call | flops 70000000 | bytes 5000000 | tf_op jit(solution)/shard_map/prepare/pallas_call | solution.py:195
  10.8 66.5 %all_to_all.10.refs_0_ = f32[32,136,128]{2,1,0:T(8,128)S(1)} all-to-all(f32[32,136,128]{2,1,0:T(8,128)S(1)} %get-tuple-element.21), channel_id=1, replica_groups=mesh['seq'=32,'dp'=8] {'seq'}, dimensions={0} | all-to-all | bytes 4456448 | tf_op jit(solution)/shard_map/all_to_all | solution.py:207
  77.6 1.3 copy-done
  78.9 4.2 %all-to-all-start.1 = ((f32[32,128,128]{2,1,0:T(8,128)}), f32[32,128,128]{2,1,0:T(8,128)S(1)}, u32[]{:S(2)}, u32[]{:S(2)}) async-start(f32[32,128,128]{2,1,0:T(8,128)} %copy-done), calls=%async_computation.1 | async-start | bytes 4194304 | tf_op jit(solution)/shard_map/all_to_all | solution.py:215
  83.2 1.0 copy-done.3
  84.3 1.0 copy-done.5
  85.3 1.0 copy-done.8
  86.3 7.8 %intra.1 = (f32[2048,128]{1,0:T(8,128)S(1)}, f32[128,512]{1,0:T(8,128)S(1)}, f32[128,512]{1,0:T(8,128)S(1)}, f32[64,128]{1,0:T(8,128)S(1)}, f32[64,128]{1,0:T(8,128)S(1)}, /*index=5*/f32[64,1]{1,0:T(8,128)S(1)}) custom-call(bf16[128,2048]{1,0:T(8,128)(2,1)S(1)} %bitcast.19, bf16[2048,128]{1,0:T(8,128)(2,1)S(1)} %copy-done.5, ...), custom_call_target="tpu_custom_call" | custom-call | flops 2000000000 | bytes 5000000 | tf_op jit(solution)/shard_map/intra/pallas_call | solution.py:217
  97.4 0.9 reduce.1
  98.2 34.5 %all-to-all-done.1.states_ref = f32[32,128,128]{2,1,0:T(8,128)S(1)} async-done(((f32[32,128,128]{2,1,0:T(8,128)}), f32[32,128,128]{2,1,0:T(8,128)S(1)}, u32[]{:S(2)}, u32[]{:S(2)}) %all-to-all-start.1) | async-done | bytes 2097184 | tf_op jit(solution)/shard_map/all_to_all | solution.py:215
  132.7 1.0 copy-done.6
  133.8 1.0 copy-done.9
  134.8 0.9 copy-done.15
  135.7 0.9 copy-done.17
  138.2 3.8 %finish.1 = (bf16[128,2048]{1,0:T(8,128)(2,1)}, f32[64,128]{1,0:T(8,128)}, bf16[128,512]{1,0:T(8,128)(2,1)}, bf16[128,512]{1,0:T(8,128)(2,1)}, f32[64,1]{1,0:T(8,128)S(1)}) custom-call(f32[32,128,128]{2,1,0:T(8,128)S(1)} %all-to-all-done.1.states_ref, bf16[2048,128]{1,0:T(8,128)(2,1)S(1)} %copy-done.6, bf16[2048,128]{1,0:T(8,128)(2,1)S(1)} %copy-done.9, ...), custom_call_target="tpu_custom_call" | custom-call | flops 140000000 | bytes 6000000 | tf_op jit(solution)/shard_map/finish/pallas_call | solution.py:229
  143.6 1.5 collective-permute-start
  145.1 2.0 %collective-permute-done = f32[1,128]{1,0:T(1,128)S(1)} collective-permute-done((f32[1,128]{1,0:T(1,128)S(1)}, f32[1,128]{1,0:T(1,128)S(1)}, u32[]{:S(2)}, u32[]{:S(2)}) %collective-permute-start) | collective-permute-done | bytes 544 | tf_op jit(solution)/shard_map/ppermute | solution.py:167
  147.2 2.5 %collective-permute-start.1 = (f32[1,128]{1,0:T(1,128)S(1)}, f32[1,128]{1,0:T(1,128)S(1)}, u32[]{:S(2)}, u32[]{:S(2)}) collective-permute-start(f32[1,128]{1,0:T(1,128)S(1)} %fusion), channel_id=1, source_target_pairs={{0,16},{8,24},{16,0},{24,8},{32,48},{40,56},{48,32},{56,40},{64,80... | collective-permute-start | bytes 1544 | tf_op jit(solution)/shard_map/ppermute | solution.py:167
  149.7 1.9 %collective-permute-done.1 = f32[1,128]{1,0:T(1,128)S(1)} collective-permute-done((f32[1,128]{1,0:T(1,128)S(1)}, f32[1,128]{1,0:T(1,128)S(1)}, u32[]{:S(2)}, u32[]{:S(2)}) %collective-permute-start.1) | collective-permute-done | bytes 544 | tf_op jit(solution)/shard_map/ppermute | solution.py:167
  151.7 2.2 %collective-permute-start.2 = (f32[1,128]{1,0:T(1,128)S(1)}, f32[1,128]{1,0:T(1,128)S(1)}, u32[]{:S(2)}, u32[]{:S(2)}) collective-permute-start(f32[1,128]{1,0:T(1,128)S(1)} %add.25), channel_id=1, source_target_pairs={{0,32},{8,40},{16,48},{24,56},{32,0},{40,8},{48,16},{56,24},{64,96... | collective-permute-start | bytes 1544 | tf_op jit(solution)/shard_map/ppermute | solution.py:167
  153.9 5.3 %collective-permute-done.2 = f32[1,128]{1,0:T(1,128)S(1)} collective-permute-done((f32[1,128]{1,0:T(1,128)S(1)}, f32[1,128]{1,0:T(1,128)S(1)}, u32[]{:S(2)}, u32[]{:S(2)}) %collective-permute-start.2) | collective-permute-done | bytes 544 | tf_op jit(solution)/shard_map/ppermute | solution.py:167
  159.8 2.9 %collective-permute-done.3 = f32[1,128]{1,0:T(1,128)S(1)} collective-permute-done((f32[1,128]{1,0:T(1,128)S(1)}, f32[1,128]{1,0:T(1,128)S(1)}, u32[]{:S(2)}, u32[]{:S(2)}) %collective-permute-start.3) | collective-permute-done | bytes 544 | tf_op jit(solution)/shard_map/ppermute | solution.py:167
  162.7 1.9 %collective-permute-start.4 = (f32[1,128]{1,0:T(1,128)S(1)}, f32[1,128]{1,0:T(1,128)S(1)}, u32[]{:S(2)}, u32[]{:S(2)}) collective-permute-start(f32[1,128]{1,0:T(1,128)S(1)} %add.27), channel_id=1, source_target_pairs={{0,128},{8,136},{16,144},{24,152},{32,160},{40,168},{48,176},{56,1... | collective-permute-start | bytes 1544 | tf_op jit(solution)/shard_map/ppermute | solution.py:167
  164.6 3.1 %collective-permute-done.4 = f32[1,128]{1,0:T(1,128)S(1)} collective-permute-done((f32[1,128]{1,0:T(1,128)S(1)}, f32[1,128]{1,0:T(1,128)S(1)}, u32[]{:S(2)}, u32[]{:S(2)}) %collective-permute-start.4) | collective-permute-done | bytes 544 | tf_op jit(solution)/shard_map/ppermute | solution.py:167
  167.7 1.1 collective-permute-done.5
  168.9 1.3 collective-permute-start.6
  170.1 2.3 %collective-permute-done.6 = f32[1,128]{1,0:T(1,128)S(1)} collective-permute-done((f32[1,128]{1,0:T(1,128)S(1)}, f32[1,128]{1,0:T(1,128)S(1)}, u32[]{:S(2)}, u32[]{:S(2)}) %collective-permute-start.6) | collective-permute-done | bytes 544 | tf_op jit(solution)/shard_map/ppermute | solution.py:167
  172.7 4.7 %collective-permute-done.7 = f32[1,128]{1,0:T(1,128)S(1)} collective-permute-done((f32[1,128]{1,0:T(1,128)S(1)}, f32[1,128]{1,0:T(1,128)S(1)}, u32[]{:S(2)}, u32[]{:S(2)}) %collective-permute-start.7) | collective-permute-done | bytes 544 | tf_op jit(solution)/shard_map/ppermute | solution.py:167
  (61 shorter events, 12.1 us)
Async XLA Ops:
  1.4 1.0 copy-start.1
  2.4 1.0 copy-start.2
  3.5 0.9 copy-start.10
  4.4 0.9 copy-start.12
  5.3 0.8 copy-start.18
  9.2 0.8 copy-start.4
  10.0 0.8 copy-start.7
  77.6 1.3 copy-start
  78.9 4.2 %copy-start.27 = (f32[64]{0:T(128)S(1)}, f32[64]{0:T(128)}, u32[]{:S(2)}) copy-start(f32[64]{0:T(128)} %param.12) | copy-start | bytes 772
  78.9 4.3 %copy-start.11 = (bf16[1,128,512]{2,1,0:T(8,128)(2,1)S(1)}, bf16[1,128,512]{2,1,0:T(8,128)(2,1)}, u32[]{:S(2)}) copy-start(bf16[1,128,512]{2,1,0:T(8,128)(2,1)} %param.13) | copy-start | bytes 393220
  78.9 4.3 %copy-start.13 = (bf16[1,128,512]{2,1,0:T(8,128)(2,1)S(1)}, bf16[1,128,512]{2,1,0:T(8,128)(2,1)}, u32[]{:S(2)}) copy-start(bf16[1,128,512]{2,1,0:T(8,128)(2,1)} %param.14) | copy-start | bytes 393220
  78.9 4.3 %copy-start.19 = (f32[1,64,128]{2,1,0:T(8,128)S(1)}, f32[1,64,128]{2,1,0:T(8,128)}, u32[]{:S(2)}) copy-start(f32[1,64,128]{2,1,0:T(8,128)} %param.9) | copy-start | bytes 98308
  78.9 53.8 %all-to-all-start.1 = ((f32[32,128,128]{2,1,0:T(8,128)}), f32[32,128,128]{2,1,0:T(8,128)S(1)}, u32[]{:S(2)}, u32[]{:S(2)}) async-start(f32[32,128,128]{2,1,0:T(8,128)} %copy-done), calls=%async_computation.1 | async-start | bytes 4194304 | tf_op jit(solution)/shard_map/all_to_all | solution.py:215
  83.2 1.0 copy-start.3
  84.3 1.0 copy-start.5
  85.3 1.0 copy-start.8
  94.1 0.7 copy-start.14
  94.8 0.7 copy-start.16
  132.7 1.0 copy-start.6
  133.8 1.0 copy-start.9
  134.8 0.9 copy-start.15
  135.7 0.9 copy-start.17
  136.7 0.8 copy-start.21
  137.5 0.8 copy-start.23
  143.6 3.6 %collective-permute-start = (f32[1,128]{1,0:T(1,128)S(1)}, f32[1,128]{1,0:T(1,128)S(1)}, u32[]{:S(2)}, u32[]{:S(2)}) collective-permute-start(f32[1,128]{1,0:T(1,128)S(1)} %pad_maximum_fusion), channel_id=1, source_target_pairs={{0,8},{8,0},{16,24},{24,16},{32,40},{40,32},{48,56},{56,48},{64,72... | collective-permute-start | bytes 1544 | tf_op jit(solution)/shard_map/ppermute | solution.py:167
  147.2 4.5 %collective-permute-start.1 = (f32[1,128]{1,0:T(1,128)S(1)}, f32[1,128]{1,0:T(1,128)S(1)}, u32[]{:S(2)}, u32[]{:S(2)}) collective-permute-start(f32[1,128]{1,0:T(1,128)S(1)} %fusion), channel_id=1, source_target_pairs={{0,16},{8,24},{16,0},{24,8},{32,48},{40,56},{48,32},{56,40},{64,80... | collective-permute-start | bytes 1544 | tf_op jit(solution)/shard_map/ppermute | solution.py:167
  151.7 7.4 %collective-permute-start.2 = (f32[1,128]{1,0:T(1,128)S(1)}, f32[1,128]{1,0:T(1,128)S(1)}, u32[]{:S(2)}, u32[]{:S(2)}) collective-permute-start(f32[1,128]{1,0:T(1,128)S(1)} %add.25), channel_id=1, source_target_pairs={{0,32},{8,40},{16,48},{24,56},{32,0},{40,8},{48,16},{56,24},{64,96... | collective-permute-start | bytes 1544 | tf_op jit(solution)/shard_map/ppermute | solution.py:167
  159.1 3.5 %collective-permute-start.3 = (f32[1,128]{1,0:T(1,128)S(1)}, f32[1,128]{1,0:T(1,128)S(1)}, u32[]{:S(2)}, u32[]{:S(2)}) collective-permute-start(f32[1,128]{1,0:T(1,128)S(1)} %add.26), channel_id=1, source_target_pairs={{0,64},{8,72},{16,80},{24,88},{32,96},{40,104},{48,112},{56,120},{... | collective-permute-start | bytes 1544 | tf_op jit(solution)/shard_map/ppermute | solution.py:167
  162.7 5.0 %collective-permute-start.4 = (f32[1,128]{1,0:T(1,128)S(1)}, f32[1,128]{1,0:T(1,128)S(1)}, u32[]{:S(2)}, u32[]{:S(2)}) collective-permute-start(f32[1,128]{1,0:T(1,128)S(1)} %add.27), channel_id=1, source_target_pairs={{0,128},{8,136},{16,144},{24,152},{32,160},{40,168},{48,176},{56,1... | collective-permute-start | bytes 1544 | tf_op jit(solution)/shard_map/ppermute | solution.py:167
  167.7 1.1 collective-permute-start.5
  168.9 3.5 %collective-permute-start.6 = (f32[1,128]{1,0:T(1,128)S(1)}, f32[1,128]{1,0:T(1,128)S(1)}, u32[]{:S(2)}, u32[]{:S(2)}) collective-permute-start(f32[1,128]{1,0:T(1,128)S(1)} %add.29), channel_id=1, source_target_pairs={{0,2},{1,3},{2,0},{3,1},{4,6},{5,7},{6,4},{7,5},{8,10},{9,11},{10,... | collective-permute-start | bytes 1544 | tf_op jit(solution)/shard_map/ppermute | solution.py:167
  172.4 5.0 %collective-permute-start.7 = (f32[1,128]{1,0:T(1,128)S(1)}, f32[1,128]{1,0:T(1,128)S(1)}, u32[]{:S(2)}, u32[]{:S(2)}) collective-permute-start(f32[1,128]{1,0:T(1,128)S(1)} %add.30), channel_id=1, source_target_pairs={{0,4},{1,5},{2,6},{3,7},{4,0},{5,1},{6,2},{7,3},{8,12},{9,13},{10,... | collective-permute-start | bytes 1544 | tf_op jit(solution)/shard_map/ppermute | solution.py:167
  (5 other events, 3.1 us)

commit v2 on v1

--- a/solution.py
+++ b/solution.py
@@ -15,7 +15,7 @@
 highest = lax.Precision.HIGHEST
 f32 = jnp.float32
 bf16 = jnp.bfloat16
-VMEM_LIMIT = 48 * 1024 * 1024
+VMEM_LIMIT = 60 * 1024 * 1024
 
 
 def contract(left, right, dims):
@@ -37,11 +37,33 @@
     return row <= col if upper else row >= col
 
 
+def column_of_group(row_ref):
+    first = pl.program_id(0) * K
+    row = lax.broadcasted_iota(jnp.int32, (K, H), 0)
+    lane = lax.broadcasted_iota(jnp.int32, (K, H), 1)
+    return jnp.sum(jnp.where(lane == first + row, row_ref[...], 0.0), axis=1, keepdims=True)
+
+
+def row_of_group(column, offset):
+    first = pl.program_id(0) * K + offset
+    row = lax.broadcasted_iota(jnp.int32, (K, 2 * H), 0)
+    lane = lax.broadcasted_iota(jnp.int32, (K, 2 * H), 1)
+    return jnp.sum(jnp.where(lane == first + row, column, 0.0), axis=0, keepdims=True)
+
+
+def accumulate(ref, start, value):
+    @pl.when(pl.program_id(0) == 0)
+    def _():
+        ref[...] = start
+
+    ref[...] += value
+
+
 def prepare_kernel(x_ref, dy_ref, step_ref, gate_ref, rate_ref, key_ref, query_ref,
                    send_ref, cum_ref, xt_ref, dyt_ref):
     length = x_ref.shape[0]
     step = step_ref[...]
-    log_decay = gate_ref[...] - rate_ref[...] * step
+    log_decay = gate_ref[...] - column_of_group(rate_ref) * step
     cum = jnp.dot(log_decay, triangle(length, True).astype(f32), precision=highest)
     cum_ref[...] = cum
     last = cum[:, length - 1:]
@@ -121,12 +143,13 @@
     flow_ref[...] = jnp.concatenate(row_sums, axis=1).T - jnp.concatenate(col_sums, axis=0)
     x_full = xt_ref[...].astype(f32)
     own_ref[...] = head_sum(x_full * intra_ref[...])
-    skip_ref[...] = jnp.sum(head_sum(x_full * dyt_ref[...].astype(f32)), axis=1, keepdims=True)
+    skip_part = jnp.sum(head_sum(x_full * dyt_ref[...].astype(f32)), axis=1, keepdims=True)
+    accumulate(skip_ref, jnp.zeros(skip_ref.shape, f32), row_of_group(skip_part, H))
 
 
 def finish_kernel(states_ref, xt_ref, dyt_ref, step_ref, cum_ref, rate_ref, skip_ref, key_ref, query_ref,
-                  intra_ref, dq_in_ref, dk_in_ref, flow_ref, own_ref,
-                  dx_ref, dstep_ref, dk_ref, dq_ref, rate_part_ref):
+                  intra_ref, dq_in_ref, dk_in_ref, flow_ref, own_ref, sums_in_ref,
+                  dx_ref, dstep_ref, dk_ref, dq_ref, sums_ref):
     owners, rows, _ = states_ref.shape
     half = rows // 2
     length = step_ref.shape[1]
@@ -136,7 +159,7 @@
     keys, queries = key_ref[...], query_ref[...]
     state_term = contract(adjoint_low, keys, (1, 1))
     carried = contract(state_low, queries, (1, 1))
-    cum, step, rate = cum_ref[...], step_ref[...], rate_ref[...]
+    cum, step, rate = cum_ref[...], step_ref[...], column_of_group(rate_ref)
     last = cum[:, length - 1:]
     growth, tail = jnp.exp(cum), jnp.exp(last - cum)
     exit_weight = step * tail
@@ -154,19 +177,22 @@
     d_cum = flow_ref[...] + entry_term - exit_term + jnp.where(final_slot, closing, 0.0)
     d_logs = jnp.dot(d_cum, triangle(length, False).astype(f32), precision=highest)
     dstep_ref[...] = own_ref[...] + tail * outside - rate * d_logs
-    rate_part_ref[...] = -rate * jnp.sum(step * d_logs, axis=1, keepdims=True)
+    rate_part = -rate * jnp.sum(step * d_logs, axis=1, keepdims=True)
+    accumulate(sums_ref, sums_in_ref[...], row_of_group(rate_part, 0))
     d_scaled = intra_ref[...] + per_feature(tail) * state_term
-    d_inputs = per_feature(step) * d_scaled + per_feature(jnp.broadcast_to(skip_ref[...], (K, length))) * dy_t
+    d_inputs = per_feature(step) * d_scaled + per_feature(jnp.broadcast_to(column_of_group(skip_ref), (K, length))) * dy_t
     dx_ref[...] = d_inputs.T.astype(bf16)
 
 
-def total_over_devices(value):
-    for axis in ("seq", "dp"):
-        size, reach = lax.axis_size(axis), 1
-        while reach < size:
-            value = value + lax.ppermute(value, axis, [(i, i ^ reach) for i in range(size)])
-            reach *= 2
-    return value
+def total_over_devices(row):
+    size = lax.axis_size("seq")
+    gathered = lax.all_to_all(jnp.broadcast_to(row[None], (size,) + row.shape), "seq", 0, 0)
+    row = jnp.sum(gathered, axis=0)
+    size, reach = lax.axis_size("dp"), 1
+    while reach < size:
+        row = row + lax.ppermute(row, "dp", [(i, i ^ reach) for i in range(size)])
+        reach *= 2
+    return row
 
 
 def on_device(inputs, step_sizes, gate, decay_rate, skip, keys, queries, grads):
@@ -175,7 +201,7 @@
     tokens_all = length * blocks * lax.axis_size("dp")
     x, dy, step = inputs[0], grads[0], step_sizes[0]
     key_rows, query_rows = keys[0], queries[0]
-    rate, skip_col = decay_rate.reshape(H, 1), skip.reshape(H, 1)
+    rate, skip_row = decay_rate.reshape(1, H), skip.reshape(1, H)
     per_owner = H // blocks
     half = per_owner * P_SIZE
     owners = blocks // G
@@ -184,7 +210,8 @@
     tokens = pl.BlockSpec((length, GP), lambda g: (0, g))
     features = pl.BlockSpec((GP, length), lambda g: (g, 0))
     head_rows = pl.BlockSpec((K, length), lambda g: (g, 0))
-    head_col = pl.BlockSpec((K, 1), lambda g: (g, 0))
+    per_head = pl.BlockSpec((1, H), lambda g: (0, 0))
+    sums_row = pl.BlockSpec((1, 2 * H), lambda g: (0, 0))
     shared_row = pl.BlockSpec((1, length), lambda g: (0, 0))
     group_rows = pl.BlockSpec((length, N), lambda g: (0, g))
     params = pltpu.CompilerParams(vmem_limit_bytes=VMEM_LIMIT)
@@ -195,7 +222,7 @@
     send, cum, x_t, dy_t = pl.pallas_call(
         prepare_kernel,
         grid=(G,),
-        in_specs=[tokens, tokens, head_rows, shared_row, head_col, group_rows, group_rows],
+        in_specs=[tokens, tokens, head_rows, shared_row, per_head, group_rows, group_rows],
         out_specs=[pl.BlockSpec((owners, 2 * half + pad, N), lambda g: (g, 0, 0)), head_rows, features, features],
         out_shape=[shape((blocks, 2 * half + pad, N)), shape((H, length)),
                    shape((H * P_SIZE, length), bf16), shape((H * P_SIZE, length), bf16)],
@@ -214,34 +241,33 @@
     )(recv)
     states = lax.all_to_all(scanned, "seq", 0, 0)
 
-    intra, dq_intra, dk_intra, flow, own, skip_part = pl.pallas_call(
+    intra, dq_intra, dk_intra, flow, own, sums = pl.pallas_call(
         intra_kernel,
         grid=(G,),
         in_specs=[tokens, features, features, head_rows, head_rows, group_rows, group_rows],
-        out_specs=[features, group_rows, group_rows, head_rows, head_rows, head_col],
+        out_specs=[features, group_rows, group_rows, head_rows, head_rows, sums_row],
         out_shape=[shape((H * P_SIZE, length)), shape((length, G * N)), shape((length, G * N)),
-                   shape((H, length)), shape((H, length)), shape((H, 1))],
+                   shape((H, length)), shape((H, length)), shape((1, 2 * H))],
         compiler_params=params,
         cost_estimate=pl.CostEstimate(flops=2_000_000_000, bytes_accessed=5_000_000, transcendentals=1_000_000),
         name="intra",
     )(dy, x_t, dy_t, step, cum, key_rows, query_rows)
 
-    d_inputs, d_steps, d_keys, d_queries, rate_part = pl.pallas_call(
+    d_inputs, d_steps, d_keys, d_queries, sums = pl.pallas_call(
         finish_kernel,
         grid=(G,),
         in_specs=[pl.BlockSpec((owners, 2 * half, N), lambda g: (g, 0, 0)), features, features,
-                  head_rows, head_rows, head_col, head_col, group_rows, group_rows,
-                  features, group_rows, group_rows, head_rows, head_rows],
-        out_specs=[tokens, head_rows, group_rows, group_rows, head_col],
+                  head_rows, head_rows, per_head, per_head, group_rows, group_rows,
+                  features, group_rows, group_rows, head_rows, head_rows, sums_row],
+        out_specs=[tokens, head_rows, group_rows, group_rows, sums_row],
         out_shape=[shape((length, H * P_SIZE), bf16), shape((H, length)),
-                   shape((length, G * N), bf16), shape((length, G * N), bf16), shape((H, 1))],
+                   shape((length, G * N), bf16), shape((length, G * N), bf16), shape((1, 2 * H))],
         compiler_params=params,
         cost_estimate=pl.CostEstimate(flops=140_000_000, bytes_accessed=6_000_000, transcendentals=20_000),
         name="finish",
-    )(states, x_t, dy_t, step, cum, rate, skip_col, key_rows, query_rows, intra, dq_intra, dk_intra, flow, own)
-
-    totals = total_over_devices(jnp.concatenate([rate_part.reshape(1, H), skip_part.reshape(1, H)], axis=1))
-    totals = totals[0] / tokens_all
+    )(states, x_t, dy_t, step, cum, rate, skip_row, key_rows, query_rows, intra, dq_intra, dk_intra, flow, own, sums)
+
+    totals = total_over_devices(sums)[0] / tokens_all
     return (d_inputs[None], d_steps[None], d_keys[None], d_queries[None], totals[:H], totals[H:])
 
 

time: 179 us -> 164 us (0.916)
  local copies, waits for them, and re-layouts: 22.1 us -> 2.6 us
  blocking collectives: 66.5 us -> 82.4 us
  waiting for transfers between devices: 57.8 us -> 48.1 us
  Pallas kernels: 14.3 us -> 23.8 us
  starting transfers between devices: 14.6 us -> 5.71 us
  other arithmetic: 1.9 us -> 0.03 us
    unnamed x56 -> x2, local copies, waits for them, and re-layouts: 20.7 us -> 1.35 us
    all_to_all x0 -> x1, blocking collectives: none -> 15.5 us  [total_over_devices(): lax.all_to_all(jnp.broadcast_to(row[None], (size,) + row.shape), 'seq', 0...]
    ppermute x8 -> x3, waiting for transfers between devices: 23.3 us -> 8.08 us  [total_over_devices(): row = row + lax.ppermute(row, 'dp', [(i, i ^ reach) for i in range(size)])]
    ppermute x8 -> x3, starting transfers between devices: 10.4 us -> 1.7 us  [total_over_devices(): row = row + lax.ppermute(row, 'dp', [(i, i ^ reach) for i in range(size)])]
    all_to_all x1, waiting for transfers between devices: 34.5 us -> 40 us  [on_device(): states = lax.all_to_all(scanned, 'seq', 0, 0)]
    pallas_call x1, Pallas kernels: 0.19 us -> 3.17 us  [on_device(): pl.pallas_call(lambda *refs: scan_kernel(blocks, half, *refs), out_shape=...]
    pallas_call x1, Pallas kernels: 2.55 us -> 4.96 us  [on_device(): pl.pallas_call(prepare_kernel, grid=(G,), in_specs=[tokens, tokens, head_...]
    pallas_call x1, Pallas kernels: 3.8 us -> 6.06 us  [on_device(): pl.pallas_call(finish_kernel, grid=(G,), in_specs=[pl.BlockSpec((owners,...]
  transfers between devices with their start and end apart: 9 -> 4, of which waited for: 9 -> 4; matrix products, arithmetic and copies ran while one was open for 1% -> 0% of each run, Pallas kernels for 4% -> 6%
where the time goes in v2:
time: 164 us; the launch traced here: 163 us
  blocking collectives  82.4 us (50%)
  waiting for transfers between devices  48.1 us (29%)
  Pallas kernels  23.8 us (15%)
  starting transfers between devices  5.71 us (3%)
  local copies, waits for them, and re-layouts  2.6 us (2%)
    all_to_all x1, blocking collectives, on_device(): recv = lax.all_to_all(send, 'seq', 0, 0)  66.9 us
    all_to_all x1, waiting for transfers between devices, on_device(): states = lax.all_to_all(scanned, 'seq', 0, 0)  40 us
    all_to_all x1, blocking collectives, total_over_devices(): lax.all_to_all(jnp.broadcast_to(row[None], (size,) + row.shape), 'seq', 0...  15.5 us
    pallas_call x1, Pallas kernels, on_device(): pl.pallas_call(intra_kernel, grid=(G,), in_specs=[tokens, features, featu...  9.64 us
    ppermute x3, waiting for transfers between devices, total_over_devices(): row = row + lax.ppermute(row, 'dp', [(i, i ^ reach) for i in range(size)])  8.08 us
    pallas_call x1, Pallas kernels, on_device(): pl.pallas_call(finish_kernel, grid=(G,), in_specs=[pl.BlockSpec((owners,...  6.06 us
    pallas_call x1, Pallas kernels, on_device(): pl.pallas_call(prepare_kernel, grid=(G,), in_specs=[tokens, tokens, head_...  4.96 us
    all_to_all x1, starting transfers between devices, on_device(): states = lax.all_to_all(scanned, 'seq', 0, 0)  4.01 us
  transfers between devices with their start and end apart: 4, of which 4 were waited for; matrix products, arithmetic and copies ran while one was open for 0% of the time, Pallas kernels for 6%

profile of v2, /device:TPU:16, one launch (start us, length us, event | category | flops | bytes accessed | tf_op | source)
XLA Modules:
  0.0 163.3 jit_solution(14397448872474210155)
XLA Ops:
  0.6 5.0 %prepare.1 = (f32[32,136,128]{2,1,0:T(8,128)}, f32[64,128]{1,0:T(8,128)}, bf16[2048,128]{1,0:T(8,128)(2,1)}, bf16[2048,128]{1,0:T(8,128)(2,1)}) custom-call(bf16[128,2048]{1,0:T(8,128)(2,1)} %bitcast.25, bf16[128,2048]{1,0:T(8,128)(2,1)} %bitcast.26, f32[64,128]{1,0:T(8,128)} %bitcast.28, f32[1,128]{1,0:T(1,128)} %gate_ref.1, f32[1,64]{1,0:T(1,128)} %bitcast.32, ...), custom_call_target="tpu_custom_call" | custom-call | flops 70000000 | bytes 5000000 | tf_op jit(solution)/shard_map/prepare/pallas_call | solution.py:222
  5.6 66.9 %all_to_all.15.refs_0_ = f32[32,136,128]{2,1,0:T(8,128)} all-to-all(f32[32,136,128]{2,1,0:T(8,128)} %get-tuple-element.21), channel_id=1, replica_groups=mesh['seq'=32,'dp'=8] {'seq'}, dimensions={0} | all-to-all | bytes 4456448 | tf_op jit(solution)/shard_map/all_to_all | solution.py:234
  72.5 3.2 %scan.1 = f32[32,128,128]{2,1,0:T(8,128)} custom-call(f32[32,136,128]{2,1,0:T(8,128)} %all_to_all.15.refs_0_), custom_call_target="tpu_custom_call" | custom-call | flops 2000000 | bytes 4300000 | tf_op jit(solution)/shard_map/scan/pallas_call | solution.py:235
  75.6 4.0 %all-to-all-start.1 = ((f32[32,128,128]{2,1,0:T(8,128)}), f32[32,128,128]{2,1,0:T(8,128)S(1)}, u32[]{:S(2)}, u32[]{:S(2)}) async-start(f32[32,128,128]{2,1,0:T(8,128)} %scan.1), calls=%async_computation.1 | async-start | bytes 4194304 | tf_op jit(solution)/shard_map/all_to_all | solution.py:242
  79.6 9.6 %intra.1 = (f32[2048,128]{1,0:T(8,128)}, f32[128,512]{1,0:T(8,128)}, f32[128,512]{1,0:T(8,128)}, f32[64,128]{1,0:T(8,128)}, f32[64,128]{1,0:T(8,128)}, /*index=5*/f32[1,128]{1,0:T(1,128)}) custom-call(bf16[128,2048]{1,0:T(8,128)(2,1)} %bitcast.27, bf16[2048,128]{1,0:T(8,128)(2,1)} %get-tuple-element.22.xt_ref, bf16[2048,128]{1,0:T(8,128)(2,1)} %get-tuple-element.23.dyt_ref, ...), custom_call_target="tpu_custom_call" | custom-call | flops 2000000000 | bytes 5000000 | tf_op jit(solution)/shard_map/intra/pallas_call | solution.py:244
  89.3 40.0 %all-to-all-done.1.states_ref = f32[32,128,128]{2,1,0:T(8,128)S(1)} async-done(((f32[32,128,128]{2,1,0:T(8,128)}), f32[32,128,128]{2,1,0:T(8,128)S(1)}, u32[]{:S(2)}, u32[]{:S(2)}) %all-to-all-start.1) | async-done | bytes 2097184 | tf_op jit(solution)/shard_map/all_to_all | solution.py:242
  129.3 0.0 copy-start
  129.3 1.3 copy-done
  130.6 6.1 %finish.1 = (bf16[128,2048]{1,0:T(8,128)(2,1)}, f32[64,128]{1,0:T(8,128)}, bf16[128,512]{1,0:T(8,128)(2,1)}, bf16[128,512]{1,0:T(8,128)(2,1)}, f32[1,128]{1,0:T(1,128)}) custom-call(f32[32,128,128]{2,1,0:T(8,128)} %copy-done, bf16[2048,128]{1,0:T(8,128)(2,1)} %get-tuple-element.22.xt_ref, bf16[2048,128]{1,0:T(8,128)(2,1)} %get-tuple-element.23.dyt_ref, ...), custom_call_target="tpu_custom_call" | custom-call | flops 140000000 | bytes 6000000 | tf_op jit(solution)/shard_map/finish/pallas_call | solution.py:256
  136.7 0.7 broadcast_in_dim.25
  137.3 15.5 %all_to_all.16 = f32[32,1,128]{2,1,0:T(1,128)S(1)} all-to-all(f32[32,1,128]{2,1,0:T(1,128)S(1)} %broadcast_in_dim.25), channel_id=1, replica_groups=mesh['seq'=32,'dp'=8] {'seq'}, dimensions={0} | all-to-all | bytes 32768 | tf_op jit(solution)/shard_map/all_to_all | solution.py:189
  152.9 0.1 collective-permute-start
  153.0 1.1 collective-permute-done
  154.1 1.3 collective-permute-start.1
  155.4 2.3 %collective-permute-done.1 = f32[1,128]{1,0:T(1,128)S(1)} collective-permute-done((f32[1,128]{1,0:T(1,128)S(1)}, f32[1,128]{1,0:T(1,128)S(1)}, u32[]{:S(2)}, u32[]{:S(2)}) %collective-permute-start.1) | collective-permute-done | bytes 544 | tf_op jit(solution)/shard_map/ppermute | solution.py:193
  157.6 0.3 collective-permute-start.2
  158.0 4.7 %collective-permute-done.2 = f32[1,128]{1,0:T(1,128)S(1)} collective-permute-done((f32[1,128]{1,0:T(1,128)S(1)}, f32[1,128]{1,0:T(1,128)S(1)}, u32[]{:S(2)}, u32[]{:S(2)}) %collective-permute-start.2) | collective-permute-done | bytes 544 | tf_op jit(solution)/shard_map/ppermute | solution.py:193
  162.7 0.6 slice_bitcast_fusion
  (4 shorter events, 0.0 us)
Async XLA Ops:
  75.6 53.6 %all-to-all-start.1 = ((f32[32,128,128]{2,1,0:T(8,128)}), f32[32,128,128]{2,1,0:T(8,128)S(1)}, u32[]{:S(2)}, u32[]{:S(2)}) async-start(f32[32,128,128]{2,1,0:T(8,128)} %scan.1), calls=%async_computation.1 | async-start | bytes 4194304 | tf_op jit(solution)/shard_map/all_to_all | solution.py:242
  129.3 1.3 copy-start
  152.9 1.2 collective-permute-start
  154.1 3.5 %collective-permute-start.1 = (f32[1,128]{1,0:T(1,128)S(1)}, f32[1,128]{1,0:T(1,128)S(1)}, u32[]{:S(2)}, u32[]{:S(2)}) collective-permute-start(f32[1,128]{1,0:T(1,128)S(1)} %bitcast_add_fusion), channel_id=1, source_target_pairs={{0,2},{1,3},{2,0},{3,1},{4,6},{5,7},{6,4},{7,5},{8,10},{9,11},{10,... | collective-permute-start | bytes 1544 | tf_op jit(solution)/shard_map/ppermute | solution.py:193
  157.6 5.0 %collective-permute-start.2 = (f32[1,128]{1,0:T(1,128)S(1)}, f32[1,128]{1,0:T(1,128)S(1)}, u32[]{:S(2)}, u32[]{:S(2)}) collective-permute-start(f32[1,128]{1,0:T(1,128)S(1)} %add.10), channel_id=1, source_target_pairs={{0,4},{1,5},{2,6},{3,7},{4,0},{5,1},{6,2},{7,3},{8,12},{9,13},{10,... | collective-permute-start | bytes 1544 | tf_op jit(solution)/shard_map/ppermute | solution.py:193

commit v3 on v2

--- a/solution.py
+++ b/solution.py
@@ -11,11 +11,15 @@
 G = 4
 K = 16
 GP = K * P_SIZE
+PAIR = 2
+PG = G // PAIR
+MSG = GP + K
 
 highest = lax.Precision.HIGHEST
 f32 = jnp.float32
 bf16 = jnp.bfloat16
 VMEM_LIMIT = 60 * 1024 * 1024
+SMALL_LIMIT = 16 * 1024 * 1024
 
 
 def contract(left, right, dims):
@@ -37,15 +41,23 @@
     return row <= col if upper else row >= col
 
 
-def column_of_group(row_ref):
-    first = pl.program_id(0) * K
+def mode_of(position, place):
+    return lax.rem(position + PAIR - place, PAIR)
+
+
+def group_of(step, position):
+    return mode_of(position, step // PG) * PG + lax.rem(step, PG)
+
+
+def column_of_group(row_ref, group):
+    first = group * K
     row = lax.broadcasted_iota(jnp.int32, (K, H), 0)
     lane = lax.broadcasted_iota(jnp.int32, (K, H), 1)
     return jnp.sum(jnp.where(lane == first + row, row_ref[...], 0.0), axis=1, keepdims=True)
 
 
-def row_of_group(column, offset):
-    first = pl.program_id(0) * K + offset
+def row_of_group(column, group, offset):
+    first = group * K + offset
     row = lax.broadcasted_iota(jnp.int32, (K, 2 * H), 0)
     lane = lax.broadcasted_iota(jnp.int32, (K, 2 * H), 1)
     return jnp.sum(jnp.where(lane == first + row, column, 0.0), axis=0, keepdims=True)
@@ -59,11 +71,13 @@
     ref[...] += value
 
 
-def prepare_kernel(x_ref, dy_ref, step_ref, gate_ref, rate_ref, key_ref, query_ref,
-                   send_ref, cum_ref, xt_ref, dyt_ref):
+def prepare_kernel(position_ref, x_ref, dy_ref, step_ref, gate_ref, rate_ref, key_ref, query_ref,
+                   state_refs, seed_refs, cum_ref, xt_ref, dyt_ref):
     length = x_ref.shape[0]
+    grid_step = pl.program_id(0)
+    group = group_of(grid_step, position_ref[0])
     step = step_ref[...]
-    log_decay = gate_ref[...] - column_of_group(rate_ref) * step
+    log_decay = gate_ref[...] - column_of_group(rate_ref, group) * step
     cum = jnp.dot(log_decay, triangle(length, True).astype(f32), precision=highest)
     cum_ref[...] = cum
     last = cum[:, length - 1:]
@@ -75,35 +89,44 @@
     weighted_grads = (dy_t * per_feature(jnp.exp(cum))).astype(bf16)
     local_state = contract(weighted_inputs, key_ref[...], (1, 0))
     seed = contract(weighted_grads, query_ref[...], (1, 0))
-    owners, rows, _ = send_ref.shape
-    per_owner = K // owners
-    half = per_owner * P_SIZE
-    send_ref[:, :half, :] = local_state.reshape(owners, half, N)
-    send_ref[:, half:2 * half, :] = seed.reshape(owners, half, N)
     block_decay = jnp.broadcast_to(jnp.exp(last), (K, N))
-    pad = rows - 2 * half
-    for owner in range(owners):
-        mine = block_decay[owner * per_owner:(owner + 1) * per_owner]
-        if pad > per_owner:
-            mine = jnp.concatenate([mine, jnp.zeros((pad - per_owner, N), f32)], axis=0)
-        send_ref[owner, 2 * half:, :] = mine
-
-
-def scan_kernel(blocks, half, recv_ref, out_ref):
-    per_owner = half // P_SIZE
-
-    def decay_of(block):
-        return per_feature(recv_ref[block, 2 * half:2 * half + per_owner, :])
-
-    state = jnp.zeros((half, N), f32)
-    adjoint = jnp.zeros((half, N), f32)
-    for forward in range(blocks):
-        backward = blocks - 1 - forward
-        out_ref[forward, :half, :] = state
-        out_ref[backward, half:, :] = adjoint
-        if forward < blocks - 1:
-            state = decay_of(forward) * state + recv_ref[forward, :half, :]
-            adjoint = decay_of(backward) * adjoint + recv_ref[backward, half:2 * half, :]
+    for place in range(PAIR):
+        @pl.when(grid_step // PG == place)
+        def _():
+            for ref, value in ((state_refs[place], local_state), (seed_refs[place], seed)):
+                ref[0, :GP, :] = value
+                ref[0, GP:, :] = block_decay
+
+
+def combine_kernel(recv_state_ref, state_ref, recv_seed_ref, seed_ref, send_ref):
+    pad = jnp.zeros((send_ref.shape[1] - 2 * P_SIZE - 2, N), f32)
+    for head in range(K):
+        rows = slice(head * P_SIZE, (head + 1) * P_SIZE)
+        decay_row = slice(GP + head, GP + head + 1)
+        state_decay, seed_decay = state_ref[0, decay_row, :], seed_ref[0, decay_row, :]
+        send_ref[head, :P_SIZE, :] = state_decay * recv_state_ref[0, rows, :] + state_ref[0, rows, :]
+        send_ref[head, P_SIZE:2 * P_SIZE, :] = seed_decay * recv_seed_ref[0, rows, :] + seed_ref[0, rows, :]
+        send_ref[head, 2 * P_SIZE:, :] = jnp.concatenate(
+            [state_decay * recv_state_ref[0, decay_row, :], seed_decay * recv_seed_ref[0, decay_row, :], pad], axis=0)
+
+
+def scan_kernel(recv_ref, out_ref):
+    blocks = recv_ref.shape[0]
+    states, seeds = slice(0, P_SIZE), slice(P_SIZE, 2 * P_SIZE)
+    for first in range(PAIR):
+        carry = jnp.zeros((P_SIZE, N), f32)
+        for block in range(first, blocks, PAIR):
+            out_ref[block, states, :] = carry
+            carry = recv_ref[block, 2 * P_SIZE:2 * P_SIZE + 1, :] * carry + recv_ref[block, states, :]
+        if first < PAIR - 1:
+            out_ref[first, states, :] = carry
+        final = blocks - PAIR + first
+        carry = jnp.zeros((P_SIZE, N), f32)
+        for block in range(final, -1, -PAIR):
+            out_ref[block, seeds, :] = carry
+            carry = recv_ref[block, 2 * P_SIZE + 1:2 * P_SIZE + 2, :] * carry + recv_ref[block, seeds, :]
+        if first > 0:
+            out_ref[final, seeds, :] = carry
 
 
 def intra_kernel(dy_ref, xt_ref, dyt_ref, step_ref, cum_ref, key_ref, query_ref,
@@ -144,22 +167,36 @@
     x_full = xt_ref[...].astype(f32)
     own_ref[...] = head_sum(x_full * intra_ref[...])
     skip_part = jnp.sum(head_sum(x_full * dyt_ref[...].astype(f32)), axis=1, keepdims=True)
-    accumulate(skip_ref, jnp.zeros(skip_ref.shape, f32), row_of_group(skip_part, H))
-
-
-def finish_kernel(states_ref, xt_ref, dyt_ref, step_ref, cum_ref, rate_ref, skip_ref, key_ref, query_ref,
+    accumulate(skip_ref, jnp.zeros(skip_ref.shape, f32), row_of_group(skip_part, pl.program_id(0), H))
+
+
+def finish_kernel(position_ref, carry_ref, state_in_ref, adjoint_in_ref, recv_state_ref, recv_seed_ref,
+                  xt_ref, dyt_ref, step_ref, cum_ref, rate_ref, skip_ref, key_ref, query_ref,
                   intra_ref, dq_in_ref, dk_in_ref, flow_ref, own_ref, sums_in_ref,
-                  dx_ref, dstep_ref, dk_ref, dq_ref, sums_ref):
-    owners, rows, _ = states_ref.shape
-    half = rows // 2
+                  dx_ref, dstep_ref, dk_ref, dq_ref, sums_ref, state_scratch, adjoint_scratch):
+    grid_step = pl.program_id(0)
+    group = group_of(grid_step, position_ref[0])
     length = step_ref.shape[1]
-    state = states_ref[:, :half, :].reshape(GP, N)
-    adjoint = states_ref[:, half:, :].reshape(GP, N)
+
+    def advanced(recv_ref, carry):
+        return per_feature(recv_ref[0, GP:, :]) * carry.reshape(GP, N) + recv_ref[0, :GP, :]
+
+    @pl.when(grid_step < PG)
+    def _():
+        state_scratch[...] = state_in_ref[...].reshape(GP, N)
+        adjoint_scratch[...] = advanced(recv_seed_ref, carry_ref[:, P_SIZE:, :])
+
+    @pl.when(grid_step >= PG)
+    def _():
+        state_scratch[...] = advanced(recv_state_ref, carry_ref[:, :P_SIZE, :])
+        adjoint_scratch[...] = adjoint_in_ref[...].reshape(GP, N)
+
+    state, adjoint = state_scratch[...], adjoint_scratch[...]
     state_low, adjoint_low = state.astype(bf16), adjoint.astype(bf16)
     keys, queries = key_ref[...], query_ref[...]
     state_term = contract(adjoint_low, keys, (1, 1))
     carried = contract(state_low, queries, (1, 1))
-    cum, step, rate = cum_ref[...], step_ref[...], column_of_group(rate_ref)
+    cum, step, rate = cum_ref[...], step_ref[...], column_of_group(rate_ref, group)
     last = cum[:, length - 1:]
     growth, tail = jnp.exp(cum), jnp.exp(last - cum)
     exit_weight = step * tail
@@ -178,9 +215,9 @@
     d_logs = jnp.dot(d_cum, triangle(length, False).astype(f32), precision=highest)
     dstep_ref[...] = own_ref[...] + tail * outside - rate * d_logs
     rate_part = -rate * jnp.sum(step * d_logs, axis=1, keepdims=True)
-    accumulate(sums_ref, sums_in_ref[...], row_of_group(rate_part, 0))
+    accumulate(sums_ref, sums_in_ref[...], row_of_group(rate_part, group, 0))
     d_scaled = intra_ref[...] + per_feature(tail) * state_term
-    d_inputs = per_feature(step) * d_scaled + per_feature(jnp.broadcast_to(column_of_group(skip_ref), (K, length))) * dy_t
+    d_inputs = per_feature(step) * d_scaled + per_feature(jnp.broadcast_to(column_of_group(skip_ref, group), (K, length))) * dy_t
     dx_ref[...] = d_inputs.T.astype(bf16)
 
 
@@ -202,50 +239,85 @@
     x, dy, step = inputs[0], grads[0], step_sizes[0]
     key_rows, query_rows = keys[0], queries[0]
     rate, skip_row = decay_rate.reshape(1, H), skip.reshape(1, H)
-    per_owner = H // blocks
-    half = per_owner * P_SIZE
-    owners = blocks // G
-    pad = -(-per_owner // 8) * 8
-
-    tokens = pl.BlockSpec((length, GP), lambda g: (0, g))
-    features = pl.BlockSpec((GP, length), lambda g: (g, 0))
-    head_rows = pl.BlockSpec((K, length), lambda g: (g, 0))
-    per_head = pl.BlockSpec((1, H), lambda g: (0, 0))
-    sums_row = pl.BlockSpec((1, 2 * H), lambda g: (0, 0))
-    shared_row = pl.BlockSpec((1, length), lambda g: (0, 0))
-    group_rows = pl.BlockSpec((length, N), lambda g: (0, g))
-    params = pltpu.CompilerParams(vmem_limit_bytes=VMEM_LIMIT)
+    position = lax.axis_index("seq").astype(jnp.int32).reshape(1)
+    owned = H // (PAIR * blocks)
+    assert owned == 1
+
+    def ordered(dims, index):
+        return pl.BlockSpec(dims, lambda s, position_ref: index(group_of(s, position_ref[0])))
+
+    def stepped(dims, place):
+        return pl.BlockSpec(dims, lambda s, position_ref: (jnp.clip(s - place * PG, 0, PG - 1), 0, 0))
 
     def shape(dims, dtype=f32):
         return jax.ShapeDtypeStruct(dims, dtype)
 
-    send, cum, x_t, dy_t = pl.pallas_call(
+    params = pltpu.CompilerParams(vmem_limit_bytes=VMEM_LIMIT)
+    small = pltpu.CompilerParams(vmem_limit_bytes=SMALL_LIMIT)
+    tokens = ordered((length, GP), lambda g: (0, g))
+    features = ordered((GP, length), lambda g: (g, 0))
+    head_rows = ordered((K, length), lambda g: (g, 0))
+    group_rows = ordered((length, N), lambda g: (0, g))
+    shared_row = ordered((1, length), lambda g: (0, 0))
+    per_head = ordered((1, H), lambda g: (0, 0))
+    sums_row = ordered((1, 2 * H), lambda g: (0, 0))
+    message = shape((PG, MSG, N))
+
+    states, seeds, cum, x_t, dy_t = pl.pallas_call(
         prepare_kernel,
-        grid=(G,),
-        in_specs=[tokens, tokens, head_rows, shared_row, per_head, group_rows, group_rows],
-        out_specs=[pl.BlockSpec((owners, 2 * half + pad, N), lambda g: (g, 0, 0)), head_rows, features, features],
-        out_shape=[shape((blocks, 2 * half + pad, N)), shape((H, length)),
+        grid_spec=pltpu.PrefetchScalarGridSpec(
+            num_scalar_prefetch=1,
+            grid=(G,),
+            in_specs=[tokens, tokens, head_rows, shared_row, per_head, group_rows, group_rows],
+            out_specs=[[stepped((1, MSG, N), place) for place in range(PAIR)],
+                       [stepped((1, MSG, N), place) for place in range(PAIR)], head_rows, features, features],
+        ),
+        out_shape=[[message] * PAIR, [message] * PAIR, shape((H, length)),
                    shape((H * P_SIZE, length), bf16), shape((H * P_SIZE, length), bf16)],
         compiler_params=params,
         cost_estimate=pl.CostEstimate(flops=70_000_000, bytes_accessed=5_000_000, transcendentals=20_000),
         name="prepare",
-    )(x, dy, step, gate, rate, key_rows, query_rows)
-
+    )(position, x, dy, step, gate, rate, key_rows, query_rows)
+
+    ahead = [(i, i + 1) for i in range(blocks - 1)]
+    recv_state = lax.ppermute(states[0], "seq", ahead)
+    recv_seed = lax.ppermute(seeds[1], "seq", [(j, i) for i, j in ahead])
+
+    one_message = pl.BlockSpec((1, MSG, N), lambda s: (s, 0, 0))
+    slot = 2 * P_SIZE + 8
+    send = pl.pallas_call(
+        combine_kernel,
+        grid=(PG,),
+        in_specs=[one_message] * 4,
+        out_specs=pl.BlockSpec((K, slot, N), lambda s: (s, 0, 0)),
+        out_shape=shape((blocks, slot, N)),
+        compiler_params=small,
+        cost_estimate=pl.CostEstimate(flops=1_000_000, bytes_accessed=3_300_000, transcendentals=0),
+        name="combine",
+    )(recv_state, states[1], recv_seed, seeds[0])
     recv = lax.all_to_all(send, "seq", 0, 0)
     scanned = pl.pallas_call(
-        lambda *refs: scan_kernel(blocks, half, *refs),
-        out_shape=shape((blocks, 2 * half, N)),
-        compiler_params=params,
-        cost_estimate=pl.CostEstimate(flops=2_000_000, bytes_accessed=4_300_000, transcendentals=0),
+        scan_kernel,
+        out_shape=shape((blocks, 2 * P_SIZE, N)),
+        compiler_params=small,
+        cost_estimate=pl.CostEstimate(flops=1_000_000, bytes_accessed=2_200_000, transcendentals=0),
         name="scan",
     )(recv)
-    states = lax.all_to_all(scanned, "seq", 0, 0)
-
+    carries = lax.all_to_all(scanned, "seq", 0, 0)
+    around = [(i, (i + 1) % blocks) for i in range(blocks)]
+    state_in = lax.ppermute(carries[:, :P_SIZE], "seq", [(j, i) for i, j in around])
+    adjoint_in = lax.ppermute(carries[:, P_SIZE:], "seq", around)
+
+    plain_tokens = pl.BlockSpec((length, GP), lambda g: (0, g))
+    plain_features = pl.BlockSpec((GP, length), lambda g: (g, 0))
+    plain_heads = pl.BlockSpec((K, length), lambda g: (g, 0))
+    plain_rows = pl.BlockSpec((length, N), lambda g: (0, g))
     intra, dq_intra, dk_intra, flow, own, sums = pl.pallas_call(
         intra_kernel,
         grid=(G,),
-        in_specs=[tokens, features, features, head_rows, head_rows, group_rows, group_rows],
-        out_specs=[features, group_rows, group_rows, head_rows, head_rows, sums_row],
+        in_specs=[plain_tokens, plain_features, plain_features, plain_heads, plain_heads, plain_rows, plain_rows],
+        out_specs=[plain_features, plain_rows, plain_rows, plain_heads, plain_heads,
+                   pl.BlockSpec((1, 2 * H), lambda g: (0, 0))],
         out_shape=[shape((H * P_SIZE, length)), shape((length, G * N)), shape((length, G * N)),
                    shape((H, length)), shape((H, length)), shape((1, 2 * H))],
         compiler_params=params,
@@ -255,17 +327,25 @@
 
     d_inputs, d_steps, d_keys, d_queries, sums = pl.pallas_call(
         finish_kernel,
-        grid=(G,),
-        in_specs=[pl.BlockSpec((owners, 2 * half, N), lambda g: (g, 0, 0)), features, features,
-                  head_rows, head_rows, per_head, per_head, group_rows, group_rows,
-                  features, group_rows, group_rows, head_rows, head_rows, sums_row],
-        out_specs=[tokens, head_rows, group_rows, group_rows, sums_row],
+        grid_spec=pltpu.PrefetchScalarGridSpec(
+            num_scalar_prefetch=1,
+            grid=(G,),
+            in_specs=[
+                pl.BlockSpec((K, 2 * P_SIZE, N), lambda s, position_ref: (lax.rem(s, PG), 0, 0)),
+                stepped((K, P_SIZE, N), 0), stepped((K, P_SIZE, N), 1),
+                stepped((1, MSG, N), 1), stepped((1, MSG, N), 0),
+                features, features, head_rows, head_rows, per_head, per_head, group_rows, group_rows,
+                features, group_rows, group_rows, head_rows, head_rows, sums_row],
+            out_specs=[tokens, head_rows, group_rows, group_rows, sums_row],
+            scratch_shapes=[pltpu.VMEM((GP, N), f32), pltpu.VMEM((GP, N), f32)],
+        ),
         out_shape=[shape((length, H * P_SIZE), bf16), shape((H, length)),
                    shape((length, G * N), bf16), shape((length, G * N), bf16), shape((1, 2 * H))],
         compiler_params=params,
         cost_estimate=pl.CostEstimate(flops=140_000_000, bytes_accessed=6_000_000, transcendentals=20_000),
         name="finish",
-    )(states, x_t, dy_t, step, cum, rate, skip_row, key_rows, query_rows, intra, dq_intra, dk_intra, flow, own, sums)
+    )(position, carries, state_in, adjoint_in, recv_state, recv_seed, x_t, dy_t, step, cum, rate, skip_row,
+      key_rows, query_rows, intra, dq_intra, dk_intra, flow, own, sums)
 
     totals = total_over_devices(sums)[0] / tokens_all
     return (d_inputs[None], d_steps[None], d_keys[None], d_queries[None], totals[:H], totals[H:])

time: 164 us -> 151 us (0.921)
  waiting for transfers between devices: 48.1 us -> 22.8 us
  starting transfers between devices: 5.71 us -> 12.3 us
  blocking collectives: 82.4 us -> 87.9 us
  local copies, waits for them, and re-layouts: 2.6 us -> 4.53 us
    all_to_all x1 -> x0, waiting for transfers between devices: 40 us -> none  [on_device(): states = lax.all_to_all(scanned, 'seq', 0, 0)]
    all_to_all x0 -> x1, blocking collectives: none -> 31.6 us  [on_device(): carries = lax.all_to_all(scanned, 'seq', 0, 0)]
    all_to_all x1, blocking collectives: 66.9 us -> 42.4 us  [on_device(): recv = lax.all_to_all(send, 'seq', 0, 0)]
    ppermute x0 -> x4, waiting for transfers between devices: none -> 14.7 us  [the longest x1 10.5 us: on_device(): recv_state = lax.ppermute(states[0], 'seq', ahead)]
    ppermute x0 -> x4, starting transfers between devices: none -> 10.6 us  [the longest x1 3.85 us: on_device(): recv_state = lax.ppermute(states[0], 'seq', ahead)]
    all_to_all x1 -> x0, starting transfers between devices: 4.01 us -> none  [on_device(): states = lax.all_to_all(scanned, 'seq', 0, 0)]
    unnamed x2 -> x14, local copies, waits for them, and re-layouts: 1.35 us -> 3.25 us
    pallas_call x4 -> x5, Pallas kernels: 23.8 us -> 22.7 us  [the longest x1 9.65 us: on_device(): pl.pallas_call(intra_kernel, grid=(G,), in_specs=[plain_tokens, plain_fea...]
  transfers between devices with their start and end apart: 4 -> 7, of which waited for: 4 -> 5; matrix products, arithmetic and copies ran while one was open for 0% -> 0% of each run, Pallas kernels for 6% -> 6%
where the time goes in v3:
time: 151 us
  blocking collectives  87.9 us (58%)
  waiting for transfers between devices  22.8 us (15%)
  Pallas kernels  22.7 us (15%)
  starting transfers between devices  12.3 us (8%)
  local copies, waits for them, and re-layouts  4.53 us (3%)
    all_to_all x1, blocking collectives, on_device(): recv = lax.all_to_all(send, 'seq', 0, 0)  42.4 us
    all_to_all x1, blocking collectives, on_device(): carries = lax.all_to_all(scanned, 'seq', 0, 0)  31.6 us
    all_to_all x1, blocking collectives, total_over_devices(): lax.all_to_all(jnp.broadcast_to(row[None], (size,) + row.shape), 'seq', 0...  13.9 us
    ppermute x1, waiting for transfers between devices, on_device(): recv_state = lax.ppermute(states[0], 'seq', ahead)  10.5 us
    pallas_call x1, Pallas kernels, on_device(): pl.pallas_call(intra_kernel, grid=(G,), in_specs=[plain_tokens, plain_fea...  9.65 us
    ppermute x3, waiting for transfers between devices, total_over_devices(): row = row + lax.ppermute(row, 'dp', [(i, i ^ reach) for i in range(size)])  8.07 us
    pallas_call x1, Pallas kernels, on_device(): pl.pallas_call(finish_kernel, grid_spec=pltpu.PrefetchScalarGridSpec(num_...  7.06 us
    pallas_call x1, Pallas kernels, on_device(): pl.pallas_call(prepare_kernel, grid_spec=pltpu.PrefetchScalarGridSpec(num...  5.71 us
  transfers between devices with their start and end apart: 7, of which 5 were waited for; matrix products, arithmetic and copies ran while one was open for 0% of the time, Pallas kernels for 6%

profile of v3, /device:TPU:16, one launch (start us, length us, event | category | flops | bytes accessed | tf_op | source)
XLA Modules:
  0.0 150.9 jit_solution(11391902690731379054)
XLA Ops:
  0.6 5.7 %prepare.1 = (f32[2,528,128]{2,1,0:T(8,128)}, f32[2,528,128]{2,1,0:T(8,128)}, f32[2,528,128]{2,1,0:T(8,128)}, f32[2,528,128]{2,1,0:T(8,128)}, f32[64,128]{1,0:T(...) custom-call(s32[1]{0:T(128)} %bitcast.position_ref, bf16[128,2048]{1,0:T(8,128)(2,1)} %bitcast.20, ...), custom_call_target="tpu_custom_call" | custom-call | flops 70000000 | bytes 5000000 | tf_op jit(solution)/shard_map/prepare/pallas_call | solution.py:266
  6.3 3.9 %collective-permute-start = (f32[2,528,128]{2,1,0:T(8,128)}, f32[2,528,128]{2,1,0:T(8,128)S(1)}, u32[]{:S(2)}, u32[]{:S(2)}) collective-permute-start(f32[2,528,128]{2,1,0:T(8,128)} %get-tuple-element.24), channel_id=1, source_target_pairs={{0,8},{8,16},{16,24},{24,32},{32,40},{40,48},{48,56},{56,64},{64,7... | collective-permute-start | bytes 1622024 | tf_op jit(solution)/shard_map/ppermute | solution.py:283
  10.2 1.3 collective-permute-start.1
  11.5 10.5 %collective-permute-done.recv_state_ref = f32[2,528,128]{2,1,0:T(8,128)S(1)} collective-permute-done((f32[2,528,128]{2,1,0:T(8,128)}, f32[2,528,128]{2,1,0:T(8,128)S(1)}, u32[]{:S(2)}, u32[]{:S(2)}) %collective-permute-start) | collective-permute-done | bytes 540704 | tf_op jit(solution)/shard_map/ppermute | solution.py:283
  22.0 4.2 %collective-permute-done.1.recv_seed_ref = f32[2,528,128]{2,1,0:T(8,128)S(1)} collective-permute-done((f32[2,528,128]{2,1,0:T(8,128)}, f32[2,528,128]{2,1,0:T(8,128)S(1)}, u32[]{:S(2)}, u32[]{:S(2)}) %collective-permute-start.1) | collective-permute-done | bytes 540704 | tf_op jit(solution)/shard_map/ppermute | solution.py:284
  26.2 1.2 copy-done.2
  27.4 1.0 copy-done.3
  28.5 0.2 combine.1
  28.7 0.0 copy-done
  28.7 0.0 copy-done.1
  28.7 42.4 %all_to_all.15.recv_ref = f32[32,72,128]{2,1,0:T(8,128)S(1)} all-to-all(f32[32,72,128]{2,1,0:T(8,128)S(1)} %combine.1), channel_id=1, replica_groups=mesh['seq'=32,'dp'=8] {'seq'}, dimensions={0} | all-to-all | bytes 2359296 | tf_op jit(solution)/shard_map/all_to_all | solution.py:298
  71.1 0.1 scan.1
  71.2 31.6 %all_to_all.16.carry_ref = f32[32,64,128]{2,1,0:T(8,128)S(1)} all-to-all(f32[32,64,128]{2,1,0:T(8,128)S(1)} %scan.1), channel_id=1, replica_groups=mesh['seq'=32,'dp'=8] {'seq'}, dimensions={0} | all-to-all | bytes 2097152 | tf_op jit(solution)/shard_map/all_to_all | solution.py:306
  102.8 0.1 fusion
  102.9 1.6 %collective-permute-start.3 = (f32[32,32,128]{2,1,0:T(8,128)S(1)}, f32[32,32,128]{2,1,0:T(8,128)S(1)}, u32[]{:S(2)}, u32[]{:S(2)}) collective-permute-start(f32[32,32,128]{2,1,0:T(8,128)S(1)} %get-tuple-element.42), channel_id=1, source_target_pairs={{0,8},{8,16},{16,24},{24,32},{32,40},{40,48},{48,56},{56,64},{64,7... | collective-permute-start | bytes 1572872 | tf_op jit(solution)/shard_map/ppermute | solution.py:309
  104.4 3.9 %collective-permute-start.2 = (f32[32,32,128]{2,1,0:T(8,128)S(1)}, f32[32,32,128]{2,1,0:T(8,128)S(1)}, u32[]{:S(2)}, u32[]{:S(2)}) collective-permute-start(f32[32,32,128]{2,1,0:T(8,128)S(1)} %get-tuple-element.43), channel_id=1, source_target_pairs={{8,0},{16,8},{24,16},{32,24},{40,32},{48,40},{56,48},{64,56},{72,6... | collective-permute-start | bytes 1572872 | tf_op jit(solution)/shard_map/ppermute | solution.py:308
  108.3 9.6 %intra.1 = (f32[2048,128]{1,0:T(8,128)}, f32[128,512]{1,0:T(8,128)}, f32[128,512]{1,0:T(8,128)}, f32[64,128]{1,0:T(8,128)}, f32[64,128]{1,0:T(8,128)}, /*index=5*/f32[1,128]{1,0:T(1,128)}) custom-call(bf16[128,2048]{1,0:T(8,128)(2,1)} %bitcast.22, bf16[2048,128]{1,0:T(8,128)(2,1)} %get-tuple-element.28.xt_ref, bf16[2048,128]{1,0:T(8,128)(2,1)} %get-tuple-element.29.dyt_ref, ...), custom_call_target="tpu_custom_call" | custom-call | flops 2000000000 | bytes 5000000 | tf_op jit(solution)/shard_map/intra/pallas_call | solution.py:315
  118.0 0.0 collective-permute-done.3.adjoint_in_ref
  118.0 0.0 collective-permute-done.2.state_in_ref
  118.0 0.0 copy-start.6
  118.0 0.8 copy-done.5
  118.8 0.2 copy-done.6
  118.9 7.1 %finish.1 = (bf16[128,2048]{1,0:T(8,128)(2,1)}, f32[64,128]{1,0:T(8,128)}, bf16[128,512]{1,0:T(8,128)(2,1)}, bf16[128,512]{1,0:T(8,128)(2,1)}, f32[1,128]{1,0:T(1,128)}) custom-call(s32[1]{0:T(128)} %bitcast.position_ref, f32[32,64,128]{2,1,0:T(8,128)} %copy-done.4, f32[32,32,128]{2,1,0:T(8,128)} %copy-done.6, f32[32,32,128]{2,1,0:T(8,128)} %copy-done.5, ...), custom_call_target="tpu_custom_call" | custom-call | flops 140000000 | bytes 6000000 | tf_op jit(solution)/shard_map/finish/pallas_call | solution.py:328
  126.0 0.6 broadcast_in_dim.25
  126.6 13.9 %all_to_all.17 = f32[32,1,128]{2,1,0:T(1,128)S(1)} all-to-all(f32[32,1,128]{2,1,0:T(1,128)S(1)} %broadcast_in_dim.25), channel_id=1, replica_groups=mesh['seq'=32,'dp'=8] {'seq'}, dimensions={0} | all-to-all | bytes 32768 | tf_op jit(solution)/shard_map/all_to_all | solution.py:226
  140.6 0.1 collective-permute-start.4
  140.6 1.1 collective-permute-done.4
  141.8 1.3 collective-permute-start.5
  143.0 2.3 %collective-permute-done.5 = f32[1,128]{1,0:T(1,128)S(1)} collective-permute-done((f32[1,128]{1,0:T(1,128)S(1)}, f32[1,128]{1,0:T(1,128)S(1)}, u32[]{:S(2)}, u32[]{:S(2)}) %collective-permute-start.5) | collective-permute-done | bytes 544 | tf_op jit(solution)/shard_map/ppermute | solution.py:230
  145.3 0.3 collective-permute-start.6
  145.6 4.7 %collective-permute-done.6 = f32[1,128]{1,0:T(1,128)S(1)} collective-permute-done((f32[1,128]{1,0:T(1,128)S(1)}, f32[1,128]{1,0:T(1,128)S(1)}, u32[]{:S(2)}, u32[]{:S(2)}) %collective-permute-start.6) | collective-permute-done | bytes 544 | tf_op jit(solution)/shard_map/ppermute | solution.py:230
  150.4 0.6 slice_bitcast_fusion
  (11 shorter events, 0.0 us)
Async XLA Ops:
  6.3 15.7 %collective-permute-start = (f32[2,528,128]{2,1,0:T(8,128)}, f32[2,528,128]{2,1,0:T(8,128)S(1)}, u32[]{:S(2)}, u32[]{:S(2)}) collective-permute-start(f32[2,528,128]{2,1,0:T(8,128)} %get-tuple-element.24), channel_id=1, source_target_pairs={{0,8},{8,16},{16,24},{24,32},{32,40},{40,48},{48,56},{56,64},{64,7... | collective-permute-start | bytes 1622024 | tf_op jit(solution)/shard_map/ppermute | solution.py:283
  10.2 16.0 %collective-permute-start.1 = (f32[2,528,128]{2,1,0:T(8,128)}, f32[2,528,128]{2,1,0:T(8,128)S(1)}, u32[]{:S(2)}, u32[]{:S(2)}) collective-permute-start(f32[2,528,128]{2,1,0:T(8,128)} %get-tuple-element.26), channel_id=1, source_target_pairs={{8,0},{16,8},{24,16},{32,24},{40,32},{48,40},{56,48},{64,56},{72,6... | collective-permute-start | bytes 1622024 | tf_op jit(solution)/shard_map/ppermute | solution.py:284
  22.0 6.7 %copy-start = (f32[2,528,128]{2,1,0:T(8,128)}, f32[2,528,128]{2,1,0:T(8,128)S(1)}, u32[]{:S(2)}) copy-start(f32[2,528,128]{2,1,0:T(8,128)S(1)} %collective-permute-done.recv_state_ref) | copy-start | bytes 1622020
  26.2 2.5 %copy-start.1 = (f32[2,528,128]{2,1,0:T(8,128)}, f32[2,528,128]{2,1,0:T(8,128)S(1)}, u32[]{:S(2)}) copy-start(f32[2,528,128]{2,1,0:T(8,128)S(1)} %collective-permute-done.1.recv_seed_ref) | copy-start | bytes 1622020
  26.2 1.2 copy-start.2
  27.4 1.0 copy-start.3
  102.8 15.2 %copy-start.4 = (f32[32,64,128]{2,1,0:T(8,128)}, f32[32,64,128]{2,1,0:T(8,128)S(1)}, u32[]{:S(2)}) copy-start(f32[32,64,128]{2,1,0:T(8,128)S(1)} %all_to_all.16.carry_ref) | copy-start | bytes 3145732
  102.9 15.1 %collective-permute-start.3 = (f32[32,32,128]{2,1,0:T(8,128)S(1)}, f32[32,32,128]{2,1,0:T(8,128)S(1)}, u32[]{:S(2)}, u32[]{:S(2)}) collective-permute-start(f32[32,32,128]{2,1,0:T(8,128)S(1)} %get-tuple-element.42), channel_id=1, source_target_pairs={{0,8},{8,16},{16,24},{24,32},{32,40},{40,48},{48,56},{56,64},{64,7... | collective-permute-start | bytes 1572872 | tf_op jit(solution)/shard_map/ppermute | solution.py:309
  104.4 13.5 %collective-permute-start.2 = (f32[32,32,128]{2,1,0:T(8,128)S(1)}, f32[32,32,128]{2,1,0:T(8,128)S(1)}, u32[]{:S(2)}, u32[]{:S(2)}) collective-permute-start(f32[32,32,128]{2,1,0:T(8,128)S(1)} %get-tuple-element.43), channel_id=1, source_target_pairs={{8,0},{16,8},{24,16},{32,24},{40,32},{48,40},{56,48},{64,56},{72,6... | collective-permute-start | bytes 1572872 | tf_op jit(solution)/shard_map/ppermute | solution.py:308
  118.0 0.8 copy-start.5
  118.0 1.0 copy-start.6
  140.6 1.2 collective-permute-start.4
  141.8 3.5 %collective-permute-start.5 = (f32[1,128]{1,0:T(1,128)S(1)}, f32[1,128]{1,0:T(1,128)S(1)}, u32[]{:S(2)}, u32[]{:S(2)}) collective-permute-start(f32[1,128]{1,0:T(1,128)S(1)} %bitcast_add_fusion), channel_id=1, source_target_pairs={{0,2},{1,3},{2,0},{3,1},{4,6},{5,7},{6,4},{7,5},{8,10},{9,11},{10,... | collective-permute-start | bytes 1544 | tf_op jit(solution)/shard_map/ppermute | solution.py:230
  145.3 5.0 %collective-permute-start.6 = (f32[1,128]{1,0:T(1,128)S(1)}, f32[1,128]{1,0:T(1,128)S(1)}, u32[]{:S(2)}, u32[]{:S(2)}) collective-permute-start(f32[1,128]{1,0:T(1,128)S(1)} %add.10), channel_id=1, source_target_pairs={{0,4},{1,5},{2,6},{3,7},{4,0},{5,1},{6,2},{7,3},{8,12},{9,13},{10,... | collective-permute-start | bytes 1544 | tf_op jit(solution)/shard_map/ppermute | solution.py:230

commit v4 on v3

v4 whole, which is shorter than its diff:
```python
import jax
import jax.numpy as jnp
from jax import lax
from jax.experimental import pallas as pl
from jax.experimental.pallas import tpu as pltpu
from jax.sharding import PartitionSpec as P

H = 64
P_SIZE = 32
N = 128
G = 4
K = 16
GP = K * P_SIZE
PAIR = 2
PG = G // PAIR
MSG = GP + K

highest = lax.Precision.HIGHEST
f32 = jnp.float32
bf16 = jnp.bfloat16
VMEM_LIMIT = 60 * 1024 * 1024
SMALL_LIMIT = 16 * 1024 * 1024


def contract(left, right, dims):
    return lax.dot_general(left, right, ((dims[:1], dims[1:]), ((), ())), preferred_element_type=f32)


def per_feature(rows):
    heads, length = rows.shape
    return jnp.broadcast_to(rows[:, None, :], (heads, P_SIZE, length)).reshape(heads * P_SIZE, length)


def head_sum(features):
    return jnp.sum(features.reshape(-1, P_SIZE, features.shape[1]), axis=1)


def triangle(length, upper):
    row = lax.broadcasted_iota(jnp.int32, (length, length), 0)
    col = lax.broadcasted_iota(jnp.int32, (length, length), 1)
    return row <= col if upper else row >= col


def mode_of(position, place):
    return lax.rem(position + PAIR - place, PAIR)


def group_of(step, position):
    return mode_of(position, step // PG) * PG + lax.rem(step, PG)


def column_of_group(row_ref, group):
    first = group * K
    row = lax.broadcasted_iota(jnp.int32, (K, H), 0)
    lane = lax.broadcasted_iota(jnp.int32, (K, H), 1)
    return jnp.sum(jnp.where(lane == first + row, row_ref[...], 0.0), axis=1, keepdims=True)


def row_of_group(column, group, offset):
    first = group * K + offset
    row = lax.broadcasted_iota(jnp.int32, (K, 2 * H), 0)
    lane = lax.broadcasted_iota(jnp.int32, (K, 2 * H), 1)
    return jnp.sum(jnp.where(lane == first + row, column, 0.0), axis=0, keepdims=True)


def accumulate(ref, start, value):
    @pl.when(pl.program_id(0) == 0)
    def _():
        ref[...] = start

    ref[...] += value


def prepare_kernel(first, position_ref, x_ref, x_step_ref, x_rate_ref, key_ref,
                   dy_ref, dy_step_ref, gate_ref, query_ref, state_ref, seed_ref, *cum_refs):
    length = x_ref.shape[0]
    upper = triangle(length, True).astype(f32)
    sides = ((first, x_ref, x_step_ref, key_ref, state_ref), (1 - first, dy_ref, dy_step_ref, query_ref, seed_ref))
    for place, features_ref, step_ref, rows_ref, out_ref in sides:
        mode = mode_of(position_ref[0], place)
        step = step_ref[...]
        rate = column_of_group(x_rate_ref, mode * PG + pl.program_id(0))
        cum = jnp.dot(gate_ref[...] - rate * step, upper, precision=highest)
        if cum_refs:
            cum_refs[0][mode, 0] = cum
        last = cum[:, length - 1:]
        weight = step * jnp.exp(last - cum) if place == first else jnp.exp(cum)
        weighted = (features_ref[...].astype(f32).T * per_feature(weight)).astype(bf16)
        out_ref[0, :GP, :] = contract(weighted, rows_ref[...], (1, 0))
        out_ref[0, GP:, :] = jnp.broadcast_to(jnp.exp(last), (K, N))


def combine_kernel(position_ref, recv_state_ref, state_ref, recv_seed_ref, seed_ref, send_ref, *, blocks):
    pad = jnp.zeros((send_ref.shape[1] - 2 * P_SIZE - 2, N), f32)
    before, after = position_ref[0] > 0, position_ref[0] < blocks - 1
    for head in range(K):
        rows = slice(head * P_SIZE, (head + 1) * P_SIZE)
        decay_row = slice(GP + head, GP + head + 1)
        state_decay = jnp.where(before, state_ref[0, decay_row, :], 0.0)
        seed_decay = jnp.where(after, seed_ref[0, decay_row, :], 0.0)
        send_ref[head, :P_SIZE, :] = state_decay * recv_state_ref[0, rows, :] + state_ref[0, rows, :]
        send_ref[head, P_SIZE:2 * P_SIZE, :] = seed_decay * recv_seed_ref[0, rows, :] + seed_ref[0, rows, :]
        send_ref[head, 2 * P_SIZE:, :] = jnp.concatenate(
            [state_decay * recv_state_ref[0, decay_row, :], seed_decay * recv_seed_ref[0, decay_row, :], pad], axis=0)


def scan_kernel(recv_ref, out_ref):
    blocks = recv_ref.shape[0]
    states, seeds = slice(0, P_SIZE), slice(P_SIZE, 2 * P_SIZE)
    for first in range(PAIR):
        carry = jnp.zeros((P_SIZE, N), f32)
        for block in range(first, blocks, PAIR):
            out_ref[block, states, :] = carry
            carry = recv_ref[block, 2 * P_SIZE:2 * P_SIZE + 1, :] * carry + recv_ref[block, states, :]
        if first < PAIR - 1:
            out_ref[first, states, :] = carry
        final = blocks - PAIR + first
        carry = jnp.zeros((P_SIZE, N), f32)
        for block in range(final, -1, -PAIR):
            out_ref[block, seeds, :] = carry
            carry = recv_ref[block, 2 * P_SIZE + 1:2 * P_SIZE + 2, :] * carry + recv_ref[block, seeds, :]
        if first > 0:
            out_ref[final, seeds, :] = carry


def intra_kernel(x_ref, dy_ref, step_ref, cum_ref, key_ref, query_ref,
                 xt_ref, dyt_ref, intra_ref, dq_ref, dk_ref, flow_ref, own_ref, skip_ref):
    length = dy_ref.shape[0]
    x_full = x_ref[...].astype(f32).T
    dy_full = dy_ref[...].astype(f32).T
    xt_ref[...] = x_full.astype(bf16)
    dyt_ref[...] = dy_full.astype(bf16)
    keys, queries = key_ref[...], query_ref[...]
    scores = contract(queries, keys, (1, 1))
    causal = triangle(length, False)
    cum = cum_ref[0, 0]
    cum_cols = cum.T
    step = step_ref[...]
    four = 128 // P_SIZE
    head_of_row = lax.broadcasted_iota(jnp.int32, (128, length), 0) // P_SIZE
    shared = jnp.zeros((length, length), f32)
    row_sums, col_sums = [], []
    for quad in range(K // four):
        lanes = slice(quad * 128, (quad + 1) * 128)
        x_quad = x_full[lanes, :]
        spread = jnp.concatenate(
            [jnp.where(head_of_row == i, x_quad, 0.0).astype(bf16) for i in range(four)], axis=1)
        dots = contract(dy_ref[:, lanes], spread, (1, 0))
        for i in range(four):
            head = quad * four + i
            gaps = cum_cols[:, head:head + 1] - cum[head:head + 1, :]
            decays = jnp.exp(jnp.where(causal, gaps, -1e30))
            mixing_low = (decays * scores).astype(bf16)
            pairs = decays * (dots[:, i * length:(i + 1) * length] * step[head:head + 1, :])
            shared = shared + pairs
            weighted = pairs * scores
            row_sums.append(jnp.sum(weighted, axis=1, keepdims=True))
            col_sums.append(jnp.sum(weighted, axis=0, keepdims=True))
            rows = slice(head * P_SIZE, (head + 1) * P_SIZE)
            intra_ref[rows, :] = contract(dyt_ref[rows, :], mixing_low, (1, 0))
    shared_low = shared.astype(bf16)
    dq_ref[...] = contract(shared_low, keys, (1, 0))
    dk_ref[...] = contract(shared_low, queries, (0, 0))
    flow_ref[...] = jnp.concatenate(row_sums, axis=1).T - jnp.concatenate(col_sums, axis=0)
    own_ref[...] = head_sum(x_full * intra_ref[...])
    skip_part = jnp.sum(head_sum(x_full * dy_full), axis=1, keepdims=True)
    accumulate(skip_ref, jnp.zeros(skip_ref.shape, f32), row_of_group(skip_part, pl.program_id(0), H))


def rates_kernel(position_ref, carry_ref, state_in_ref, adjoint_in_ref, recv_state_ref, recv_seed_ref,
                 xt_ref, dyt_ref, step_ref, cum_ref, rate_ref, key_ref, query_ref,
                 flow_ref, own_ref, sums_in_ref,
                 dstep_ref, sums_ref, state_low_ref, adjoint_low_ref,
                 state_scratch, adjoint_scratch, sums_scratch, *, blocks):
    grid_step = pl.program_id(0)
    position = position_ref[0]
    group = group_of(grid_step, position)
    length = step_ref.shape[1]

    def advanced(recv_ref, carry, inside):
        moved = per_feature(recv_ref[0, GP:, :]) * carry.reshape(GP, N) + recv_ref[0, :GP, :]
        return jnp.where(inside, moved, 0.0)

    @pl.when(grid_step < PG)
    def _():
        state_scratch[...] = state_in_ref[...].reshape(GP, N)
        adjoint_scratch[...] = advanced(recv_seed_ref, carry_ref[:, P_SIZE:, :], position < blocks - 1)

    @pl.when(grid_step >= PG)
    def _():
        state_scratch[...] = advanced(recv_state_ref, carry_ref[:, :P_SIZE, :], position > 0)
        adjoint_scratch[...] = adjoint_in_ref[...].reshape(GP, N)

    state, adjoint = state_scratch[...], adjoint_scratch[...]
    state_low, adjoint_low = state.astype(bf16), adjoint.astype(bf16)
    state_low_ref[...] = state_low
    adjoint_low_ref[...] = adjoint_low
    state_term = contract(adjoint_low, key_ref[...], (1, 1))
    carried = contract(state_low, query_ref[...], (1, 1))
    cum, step, rate = cum_ref[0, 0], step_ref[...], column_of_group(rate_ref, group)
    last = cum[:, length - 1:]
    tail = jnp.exp(last - cum)
    entry_term = jnp.exp(cum) * head_sum(dyt_ref[...].astype(f32) * carried)
    outside = tail * head_sum(xt_ref[...].astype(f32) * state_term)
    exit_term = step * outside
    closing = jnp.exp(last) * jnp.sum(head_sum(adjoint * state), axis=1, keepdims=True) + jnp.sum(
        exit_term, axis=1, keepdims=True)
    final_slot = lax.broadcasted_iota(jnp.int32, (K, length), 1) == length - 1
    d_cum = flow_ref[...] + entry_term - exit_term + jnp.where(final_slot, closing, 0.0)
    d_logs = jnp.dot(d_cum, triangle(length, False).astype(f32), precision=highest)
    dstep_ref[...] = own_ref[...] + outside - rate * d_logs
    rate_part = -rate * jnp.sum(step * d_logs, axis=1, keepdims=True)
    accumulate(sums_scratch, sums_in_ref[...], row_of_group(rate_part, group, 0))

    @pl.when(grid_step == G - 1)
    def _():
        sums_ref[...] = jnp.broadcast_to(sums_scratch[...][None], sums_ref.shape)


def finish_kernel(state_low_ref, adjoint_low_ref, xt_ref, dyt_ref, step_ref, cum_ref, skip_ref, key_ref,
                  intra_ref, dq_in_ref, dk_in_ref, dx_ref, dk_ref, dq_ref):
    group = pl.program_id(0)
    length = step_ref.shape[1]
    cum, step = cum_ref[0, 0], step_ref[...]
    growth, tail = jnp.exp(cum), jnp.exp(cum[:, length - 1:] - cum)
    x_t, dy_t = xt_ref[...].astype(f32), dyt_ref[...].astype(f32)
    state_low, adjoint_low = state_low_ref[...], adjoint_low_ref[...]
    weighted_grads = (dy_t * per_feature(growth)).astype(bf16)
    weighted_inputs = (x_t * per_feature(step * tail)).astype(bf16)
    dq_ref[...] = (dq_in_ref[...] + contract(weighted_grads, state_low, (0, 0))).astype(bf16)
    dk_ref[...] = (dk_in_ref[...] + contract(weighted_inputs, adjoint_low, (0, 0))).astype(bf16)
    state_term = contract(adjoint_low, key_ref[...], (1, 1))
    d_scaled = intra_ref[...] + per_feature(tail) * state_term
    skips = jnp.broadcast_to(column_of_group(skip_ref, group), (K, length))
    dx_ref[...] = (per_feature(step) * d_scaled + per_feature(skips) * dy_t).T.astype(bf16)


def total_over_devices(copies, beside):
    row, _ = lax.optimization_barrier((lax.all_to_all(copies, "seq", 0, 0), beside))
    row = jnp.sum(row, axis=0)
    size, reach = lax.axis_size("dp"), 1
    while reach < size:
        row = row + lax.ppermute(row, "dp", [(i, i ^ reach) for i in range(size)])
        reach *= 2
    return row


def on_device(inputs, step_sizes, gate, decay_rate, skip, keys, queries, grads):
    length = inputs.shape[1]
    blocks = lax.axis_size("seq")
    tokens_all = length * blocks * lax.axis_size("dp")
    x, dy, step = inputs[0], grads[0], step_sizes[0]
    key_rows, query_rows = keys[0], queries[0]
    rate, skip_row = decay_rate.reshape(1, H), skip.reshape(1, H)
    position = lax.axis_index("seq").astype(jnp.int32).reshape(1)
    owned = H // (PAIR * blocks)
    assert owned == 1

    def block(dims, index):
        return pl.BlockSpec(dims, lambda s, *_: index(s))

    def ordered(dims, index):
        return pl.BlockSpec(dims, lambda s, position_ref: index(group_of(s, position_ref[0])))

    def placed_at(place, dims, index):
        return pl.BlockSpec(dims, lambda s, position_ref: index(group_of(s + place * PG, position_ref[0])))

    def stepped(dims, place):
        return pl.BlockSpec(dims, lambda s, position_ref: (jnp.clip(s - place * PG, 0, PG - 1), 0, 0))

    def shape(dims, dtype=f32):
        return jax.ShapeDtypeStruct(dims, dtype)

    params = pltpu.CompilerParams(vmem_limit_bytes=VMEM_LIMIT)
    small = pltpu.CompilerParams(vmem_limit_bytes=SMALL_LIMIT)
    tokens = ((length, GP), lambda g: (0, g))
    features = ((GP, length), lambda g: (g, 0))
    head_rows = ((K, length), lambda g: (g, 0))
    cum_rows = ((1, 1, K, length), lambda g: (g // PG, g % PG, 0, 0))
    group_rows = ((length, N), lambda g: (0, g))
    gate_row = block((1, length), lambda s: (0, 0))
    per_head = block((1, H), lambda s: (0, 0))
    sums_row = block((1, 2 * H), lambda s: (0, 0))
    one_message = block((1, MSG, N), lambda s: (s, 0, 0))
    message = shape((PG, MSG, N))
    cums = shape((PAIR, PG, K, length))
    low_states = shape((H * P_SIZE, N), bf16)

    def prepare(first):
        other = 1 - first
        kept = pltpu.VMEM(message.shape, f32)
        out_specs, out_shape = [one_message] * 2, [message if first == 0 else kept] * 2
        if first == 0:
            out_specs.append(block((PAIR, 1, K, length), lambda s: (0, s, 0, 0)))
            out_shape.append(cums)
        return pl.pallas_call(
            lambda *refs: prepare_kernel(first, *refs),
            grid_spec=pltpu.PrefetchScalarGridSpec(
                num_scalar_prefetch=1,
                grid=(PG,),
                in_specs=[placed_at(first, *tokens), placed_at(first, *head_rows), per_head,
                          placed_at(first, *group_rows), placed_at(other, *tokens), placed_at(other, *head_rows),
                          gate_row, placed_at(other, *group_rows)],
                out_specs=out_specs,
            ),
            out_shape=out_shape,
            compiler_params=params if first == 0 else small,
            cost_estimate=pl.CostEstimate(flops=500_000_000, bytes_accessed=2_500_000, transcendentals=10_000),
            name="prepare",
        )(position, x, step, rate, key_rows, dy, step, gate, query_rows)

    around = [(i, (i + 1) % blocks) for i in range(blocks)]
    back = [(j, i) for i, j in around]
    first_states, second_seeds, cum = prepare(0)
    recv_state = lax.ppermute(first_states, "seq", around)
    recv_seed = lax.ppermute(second_seeds, "seq", back)
    second_states, first_seeds = prepare(1)

    slot = 2 * P_SIZE + 8
    send = pl.pallas_call(
        lambda *refs: combine_kernel(*refs, blocks=blocks),
        grid_spec=pltpu.PrefetchScalarGridSpec(
            num_scalar_prefetch=1,
            grid=(PG,),
            in_specs=[one_message] * 4,
            out_specs=block((K, slot, N), lambda s: (s, 0, 0)),
        ),
        out_shape=shape((blocks, slot, N)),
        compiler_params=small,
        cost_estimate=pl.CostEstimate(flops=1_000_000, bytes_accessed=3_300_000, transcendentals=0),
        name="combine",
    )(position, recv_state, second_states, recv_seed, first_seeds)
    recv = lax.all_to_all(send, "seq", 0, 0)
    scanned = pl.pallas_call(
        scan_kernel,
        out_shape=shape((blocks, 2 * P_SIZE, N)),
        compiler_params=small,
        cost_estimate=pl.CostEstimate(flops=1_000_000, bytes_accessed=2_200_000, transcendentals=0),
        name="scan",
    )(recv)
    carries = lax.all_to_all(scanned, "seq", 0, 0)
    state_in = lax.ppermute(carries[:, :P_SIZE], "seq", back)
    adjoint_in = lax.ppermute(carries[:, P_SIZE:], "seq", around)

    x_t, dy_t, intra, dq_intra, dk_intra, flow, own, sums = pl.pallas_call(
        intra_kernel,
        grid=(G,),
        in_specs=[block(*tokens), block(*tokens), block(*head_rows), block(*cum_rows), block(*group_rows),
                  block(*group_rows)],
        out_specs=[block(*features), block(*features), block(*features), block(*group_rows), block(*group_rows),
                   block(*head_rows), block(*head_rows), sums_row],
        out_shape=[shape((H * P_SIZE, length), bf16), shape((H * P_SIZE, length), bf16),
                   shape((H * P_SIZE, length)), shape((length, G * N)), shape((length, G * N)),
                   shape((H, length)), shape((H, length)), shape((1, 2 * H))],
        compiler_params=params,
        cost_estimate=pl.CostEstimate(flops=2_000_000_000, bytes_accessed=5_000_000, transcendentals=1_000_000),
        name="intra",
    )(x, dy, step, cum, key_rows, query_rows)

    d_steps, sum_copies, state_low, adjoint_low = pl.pallas_call(
        lambda *refs: rates_kernel(*refs, blocks=blocks),
        grid_spec=pltpu.PrefetchScalarGridSpec(
            num_scalar_prefetch=1,
            grid=(G,),
            in_specs=[
                block((K, 2 * P_SIZE, N), lambda s: (lax.rem(s, PG), 0, 0)),
                stepped((K, P_SIZE, N), 0), stepped((K, P_SIZE, N), 1),
                stepped((1, MSG, N), 1), stepped((1, MSG, N), 0),
                ordered(*features), ordered(*features), ordered(*head_rows),
                ordered((1, 1, K, length), lambda g: (lax.div(g, PG), lax.rem(g, PG), 0, 0)),
                per_head, ordered(*group_rows), ordered(*group_rows),
                ordered(*head_rows), ordered(*head_rows), sums_row],
            out_specs=[ordered(*head_rows), block((blocks, 1, 2 * H), lambda s: (0, 0, 0)),
                       ordered((GP, N), lambda g: (g, 0)), ordered((GP, N), lambda g: (g, 0))],
            scratch_shapes=[pltpu.VMEM((GP, N), f32), pltpu.VMEM((GP, N), f32), pltpu.VMEM((1, 2 * H), f32)],
        ),
        out_shape=[shape((H, length)), shape((blocks, 1, 2 * H)), low_states, low_states],
        compiler_params=params,
        cost_estimate=pl.CostEstimate(flops=140_000_000, bytes_accessed=6_000_000, transcendentals=20_000),
        name="rates",
    )(position, carries, state_in, adjoint_in, recv_state, recv_seed, x_t, dy_t, step, cum, rate,
      key_rows, query_rows, flow, own, sums)

    d_inputs, d_keys, d_queries = pl.pallas_call(
        finish_kernel,
        grid=(G,),
        in_specs=[block((GP, N), lambda g: (g, 0)), block((GP, N), lambda g: (g, 0)), block(*features),
                  block(*features), block(*head_rows), block(*cum_rows), per_head, block(*group_rows),
                  block(*features), block(*group_rows), block(*group_rows)],
        out_specs=[block(*tokens), block(*group_rows), block(*group_rows)],
        out_shape=[shape((length, H * P_SIZE), bf16), shape((length, G * N), bf16), shape((length, G * N), bf16)],
        compiler_params=params,
        cost_estimate=pl.CostEstimate(flops=1_000_000_000, bytes_accessed=5_000_000, transcendentals=20_000),
        name="finish",
    )(state_low, adjoint_low, x_t, dy_t, step, cum, skip_row, key_rows, intra, dq_intra, dk_intra)

    totals = total_over_devices(sum_copies, d_keys)[0] / tokens_all
    return (d_inputs[None], d_steps[None], d_keys[None], d_queries[None], totals[:H], totals[H:])


def solution(mesh):
    placed = (
        P("dp", "seq", None),
        P("dp", None, "seq"),
        P("dp", "seq"),
        P(),
        P(),
        P("dp", "seq", None),
        P("dp", "seq", None),
        P("dp", "seq", None),
    )
    return jax.shard_map(
        on_device,
        mesh=mesh,
        in_specs=placed,
        out_specs=(
            P("dp", "seq", None),
            P("dp", None, "seq"),
            P("dp", "seq", None),
            P("dp", "seq", None),
            P(),
            P(),
        ),
        check_vma=False,
    )
```

time: 151 us -> 144 us (0.954)
  blocking collectives: 87.9 us -> 70.2 us
  starting transfers between devices: 12.3 us -> 19.3 us
  Pallas kernels: 22.7 us -> 27.1 us
  local copies, waits for them, and re-layouts: 4.53 us -> 2.45 us
    all_to_all x1 -> x0, blocking collectives: 13.9 us -> none  [total_over_devices(): lax.all_to_all(jnp.broadcast_to(row[None], (size,) + row.shape), 'seq', 0...]
    all_to_all x0 -> x1, waiting for transfers between devices: none -> 5.03 us  [total_over_devices(): lax.all_to_all(copies, 'seq', 0, 0)]
    ppermute x3, waiting for transfers between devices: 14.7 us -> 10.3 us  [the longest x1 10.3 us: on_device(): recv_state = lax.ppermute(first_states, 'seq', around)]
    pallas_call x4 -> x6, Pallas kernels: 22.6 us -> 27 us  [the longest x1 10 us: on_device(): pl.pallas_call(intra_kernel, grid=(G,), in_specs=[block(*tokens), block(*...]
    all_to_all x1, blocking collectives: 42.4 us -> 38.4 us  [on_device(): recv = lax.all_to_all(send, 'seq', 0, 0)]
    all_to_all x0 -> x1, starting transfers between devices: none -> 3.95 us  [total_over_devices(): lax.all_to_all(copies, 'seq', 0, 0)]
    ppermute x3, starting transfers between devices: 9 us -> 12 us  [the longest x1 6.22 us: on_device(): recv_seed = lax.ppermute(second_seeds, 'seq', back)]
    unnamed x14 -> x24, local copies, waits for them, and re-layouts: 3.25 us -> 1.79 us
  transfers between devices with their start and end apart: 7 -> 8, of which waited for: 5 -> 5; matrix products, arithmetic and copies ran while one was open for 0% -> 0% of each run, Pallas kernels for 6% -> 12%
where the time goes in v4:
time: 144 us; the launch traced here: 143 us
  blocking collectives  70.2 us (49%)
  Pallas kernels  27.1 us (19%)
  waiting for transfers between devices  23.4 us (16%)
  starting transfers between devices  19.3 us (13%)
  local copies, waits for them, and re-layouts  2.45 us (2%)
    all_to_all x1, blocking collectives, on_device(): recv = lax.all_to_all(send, 'seq', 0, 0)  38.4 us
    all_to_all x1, blocking collectives, on_device(): carries = lax.all_to_all(scanned, 'seq', 0, 0)  31.8 us
    ppermute x1, waiting for transfers between devices, on_device(): recv_state = lax.ppermute(first_states, 'seq', around)  10.3 us
    pallas_call x1, Pallas kernels, on_device(): pl.pallas_call(intra_kernel, grid=(G,), in_specs=[block(*tokens), block(*...  10 us
    ppermute x3, waiting for transfers between devices, total_over_devices(): row = row + lax.ppermute(row, 'dp', [(i, i ^ reach) for i in range(size)])  8.08 us
    pallas_call x1, Pallas kernels, on_device(): pl.pallas_call(lambda *refs: rates_kernel(*refs, blocks=blocks), grid_spe...  6.24 us
    ppermute x1, starting transfers between devices, on_device(): recv_seed = lax.ppermute(second_seeds, 'seq', back)  6.22 us
    pallas_call x2, Pallas kernels, prepare(): pl.pallas_call(lambda *refs: prepare_kernel(first, *refs), grid_spec=pltp...  5.79 us
  transfers between devices with their start and end apart: 8, of which 5 were waited for; matrix products, arithmetic and copies ran while one was open for 0% of the time, Pallas kernels for 12%

profile of v4, /device:TPU:16, one launch (start us, length us, event | category | flops | bytes accessed | tf_op | source)
XLA Modules:
  0.0 143.3 jit_solution(8679035142996206688)
XLA Ops:
  0.7 0.0 copy-start.4
  0.7 0.0 copy-start.2
  0.7 0.0 copy-start.6
  0.7 3.7 %prepare.2 = (f32[2,528,128]{2,1,0:T(8,128)}, f32[2,528,128]{2,1,0:T(8,128)}, f32[2,2,16,128]{3,2,1,0:T(8,128)}) custom-call(s32[1]{0:T(128)} %bitcast.refs_0_, bf16[128,2048]{1,0:T(8,128)(2,1)} %bitcast.37, f32[64,128]{1,0:T(8,128)} %bitcast.23, f32[1,64]{1,0:T(1,128)} %bitcast.34, bf16[128,512]{1,0:T(8,128)(2,1)} %bitcast.18, bf16[128,2048]{1,0:T(8,128)(2,1)} %bitcast.40, ...), custom_call_target="tpu_custom_call" | custom-call | flops 500000000 | bytes 2500000 | tf_op jit(solution)/shard_map/prepare/pallas_call | solution.py:296
  4.4 2.0 %collective-permute-start = (f32[2,528,128]{2,1,0:T(8,128)}, f32[2,528,128]{2,1,0:T(8,128)S(1)}, u32[]{:S(2)}, u32[]{:S(2)}) collective-permute-start(f32[2,528,128]{2,1,0:T(8,128)} %get-tuple-element.27), channel_id=1, source_target_pairs={{0,8},{8,16},{16,24},{24,32},{32,40},{40,48},{48,56},{56,64},{64,7... | collective-permute-start | bytes 1622024 | tf_op jit(solution)/shard_map/ppermute | solution.py:315
  6.4 6.2 %collective-permute-start.1 = (f32[2,528,128]{2,1,0:T(8,128)}, f32[2,528,128]{2,1,0:T(8,128)S(1)}, u32[]{:S(2)}, u32[]{:S(2)}) collective-permute-start(f32[2,528,128]{2,1,0:T(8,128)} %get-tuple-element.29), channel_id=1, source_target_pairs={{8,0},{16,8},{24,16},{32,24},{40,32},{48,40},{56,48},{64,56},{72,6... | collective-permute-start | bytes 1622024 | tf_op jit(solution)/shard_map/ppermute | solution.py:316
  12.7 2.1 %prepare.3 = (f32[2,528,128]{2,1,0:T(8,128)S(1)}, f32[2,528,128]{2,1,0:T(8,128)S(1)}) custom-call(s32[1]{0:T(128)} %bitcast.refs_0_, bf16[128,2048]{1,0:T(8,128)(2,1)S(1)} %bitcast.39, f32[64,128]{1,0:T(8,128)S(1)} %bitcast.28, f32[1,64]{1,0:T(1,128)S(1)} %bitcast.36, bf16[128,512]{1,0:T(8,128)(2,1)S(1)} %bitcast.22, bf16[128,2048]{1,0:T(8,128)(2,1)S(1)} %bitcast.42, ...), custom_call_target="tpu_custom_call" | custom-call | flops 500000000 | bytes 2500000 | tf_op jit(solution)/shard_map/prepare/pallas_call | solution.py:296
  14.8 10.3 %collective-permute-done.refs_1_.refs_4_ = f32[2,528,128]{2,1,0:T(8,128)S(1)} collective-permute-done((f32[2,528,128]{2,1,0:T(8,128)}, f32[2,528,128]{2,1,0:T(8,128)S(1)}, u32[]{:S(2)}, u32[]{:S(2)}) %collective-permute-start) | collective-permute-done | bytes 540704 | tf_op jit(solution)/shard_map/ppermute | solution.py:315
  25.0 0.2 combine.1
  25.2 0.6 copy-done
  25.9 0.2 copy-done.1
  26.1 38.4 %all_to_all.15.recv_ref = f32[32,72,128]{2,1,0:T(8,128)S(1)} all-to-all(f32[32,72,128]{2,1,0:T(8,128)S(1)} %combine.1), channel_id=1, replica_groups=mesh['seq'=32,'dp'=8] {'seq'}, dimensions={0} | all-to-all | bytes 2359296 | tf_op jit(solution)/shard_map/all_to_all | solution.py:333
  64.5 0.1 scan.1
  64.6 31.8 %all_to_all.16.refs_1_ = f32[32,64,128]{2,1,0:T(8,128)S(1)} all-to-all(f32[32,64,128]{2,1,0:T(8,128)S(1)} %scan.1), channel_id=1, replica_groups=mesh['seq'=32,'dp'=8] {'seq'}, dimensions={0} | all-to-all | bytes 2097152 | tf_op jit(solution)/shard_map/all_to_all | solution.py:341
  96.3 0.1 fusion
  96.4 1.6 %collective-permute-start.3 = (f32[32,32,128]{2,1,0:T(8,128)S(1)}, f32[32,32,128]{2,1,0:T(8,128)S(1)}, u32[]{:S(2)}, u32[]{:S(2)}) collective-permute-start(f32[32,32,128]{2,1,0:T(8,128)S(1)} %get-tuple-element.48), channel_id=1, source_target_pairs={{0,8},{8,16},{16,24},{24,32},{32,40},{40,48},{48,56},{56,64},{64,7... | collective-permute-start | bytes 1572872 | tf_op jit(solution)/shard_map/ppermute | solution.py:343
  98.0 3.8 %collective-permute-start.2 = (f32[32,32,128]{2,1,0:T(8,128)S(1)}, f32[32,32,128]{2,1,0:T(8,128)S(1)}, u32[]{:S(2)}, u32[]{:S(2)}) collective-permute-start(f32[32,32,128]{2,1,0:T(8,128)S(1)} %get-tuple-element.49), channel_id=1, source_target_pairs={{8,0},{16,8},{24,16},{32,24},{40,32},{48,40},{56,48},{64,56},{72,6... | collective-permute-start | bytes 1572872 | tf_op jit(solution)/shard_map/ppermute | solution.py:342
  101.9 10.0 %intra.1 = (bf16[2048,128]{1,0:T(8,128)(2,1)}, bf16[2048,128]{1,0:T(8,128)(2,1)}, f32[2048,128]{1,0:T(8,128)}, f32[128,512]{1,0:T(8,128)}, f32[128,512]{1,0:T(8,...) custom-call(bf16[128,2048]{1,0:T(8,128)(2,1)} %bitcast.38, bf16[128,2048]{1,0:T(8,128)(2,1)} %bitcast.41, ...), custom_call_target="tpu_custom_call" | custom-call | flops 2000000000 | bytes 5000000 | tf_op jit(solution)/shard_map/intra/pallas_call | solution.py:345
  111.9 0.8 copy-done.10
  112.7 0.2 copy-done.11
  112.9 6.2 %rates.1 = (f32[64,128]{1,0:T(8,128)}, f32[32,1,128]{2,1,0:T(1,128)}, bf16[2048,128]{1,0:T(8,128)(2,1)}, bf16[2048,128]{1,0:T(8,128)(2,1)}) custom-call(s32[1]{0:T(128)} %bitcast.refs_0_, f32[32,64,128]{2,1,0:T(8,128)} %copy-done.9, f32[32,32,128]{2,1,0:T(8,128)} %copy-done.11, f32[32,32,128]{2,1,0:T(8,128)} %copy-done.10, f32[2,528,128]{2,1,0:T(8,128)} %copy-done, ...), custom_call_target="tpu_custom_call" | custom-call | flops 140000000 | bytes 6000000 | tf_op jit(solution)/shard_map/rates/pallas_call | solution.py:360
  119.1 4.0 %all-to-all-start.2 = ((f32[32,1,128]{2,1,0:T(1,128)}), f32[32,1,128]{2,1,0:T(1,128)S(1)}, u32[]{:S(2)}, u32[]{:S(2)}) async-start(f32[32,1,128]{2,1,0:T(1,128)} %get-tuple-element.46), calls=%async_computation.2 | async-start | bytes 32768 | tf_op jit(solution)/shard_map/all_to_all | solution.py:239
  123.1 4.7 %finish.1 = (bf16[128,2048]{1,0:T(8,128)(2,1)}, bf16[128,512]{1,0:T(8,128)(2,1)}, bf16[128,512]{1,0:T(8,128)(2,1)}) custom-call(bf16[2048,128]{1,0:T(8,128)(2,1)} %get-tuple-element.37.state_low_ref, bf16[2048,128]{1,0:T(8,128)(2,1)} %get-tuple-element.38.adjoint_low_ref, bf16[2048,128]{1,0:T(8,128)(2,1)} %get-tuple-element.32.refs_6_.xt_ref, ...), custom_call_target="tpu_custom_call" | custom-call | flops 1000000000 | bytes 5000000 | tf_op jit(solution)/shard_map/finish/pallas_call | solution.py:384
  127.8 5.0 %all-to-all-done.2 = f32[32,1,128]{2,1,0:T(1,128)S(1)} async-done(((f32[32,1,128]{2,1,0:T(1,128)}), f32[32,1,128]{2,1,0:T(1,128)S(1)}, u32[]{:S(2)}, u32[]{:S(2)}) %all-to-all-start.2) | async-done | bytes 16416 | tf_op jit(solution)/shard_map/all_to_all | solution.py:239
  132.8 0.1 reduce_sum.11
  132.9 0.1 collective-permute-start.4
  133.0 1.1 collective-permute-done.4
  134.1 1.3 collective-permute-start.5
  135.4 2.3 %collective-permute-done.5 = f32[1,128]{1,0:T(1,128)S(1)} collective-permute-done((f32[1,128]{1,0:T(1,128)S(1)}, f32[1,128]{1,0:T(1,128)S(1)}, u32[]{:S(2)}, u32[]{:S(2)}) %collective-permute-start.5) | collective-permute-done | bytes 544 | tf_op jit(solution)/shard_map/ppermute | solution.py:243
  137.6 0.3 collective-permute-start.6
  138.0 4.7 %collective-permute-done.6 = f32[1,128]{1,0:T(1,128)S(1)} collective-permute-done((f32[1,128]{1,0:T(1,128)S(1)}, f32[1,128]{1,0:T(1,128)S(1)}, u32[]{:S(2)}, u32[]{:S(2)}) %collective-permute-start.6) | collective-permute-done | bytes 544 | tf_op jit(solution)/shard_map/ppermute | solution.py:243
  142.7 0.6 slice_bitcast_fusion
  (23 shorter events, 0.1 us)
Async XLA Ops:
  0.6 12.0 %copy-start.8 = (f32[1,128]{1,0:T(1,128)S(1)}, f32[1,128]{1,0:T(1,128)}, u32[]{:S(2)}) copy-start(f32[1,128]{1,0:T(1,128)} %refs_7_.3) | copy-start | bytes 1540
  0.6 12.0 %copy-start.7 = (bf16[1,128,2048]{2,1,0:T(8,128)(2,1)S(1)}, bf16[1,128,2048]{2,1,0:T(8,128)(2,1)}, u32[]{:S(2)}) copy-start(bf16[1,128,2048]{2,1,0:T(8,128)(2,1)} %param.15) | copy-start | bytes 1572868
  0.7 12.0 %copy-start.4 = (bf16[1,128,512]{2,1,0:T(8,128)(2,1)S(1)}, bf16[1,128,512]{2,1,0:T(8,128)(2,1)}, u32[]{:S(2)}) copy-start(bf16[1,128,512]{2,1,0:T(8,128)(2,1)} %param.14) | copy-start | bytes 393220
  0.7 12.0 %copy-start.2 = (bf16[1,128,512]{2,1,0:T(8,128)(2,1)S(1)}, bf16[1,128,512]{2,1,0:T(8,128)(2,1)}, u32[]{:S(2)}) copy-start(bf16[1,128,512]{2,1,0:T(8,128)(2,1)} %param.13) | copy-start | bytes 393220
  0.7 12.0 %copy-start.5 = (f32[64]{0:T(128)S(1)}, f32[64]{0:T(128)}, u32[]{:S(2)}) copy-start(f32[64]{0:T(128)} %param.11) | copy-start | bytes 772
  0.7 12.0 %copy-start.3 = (f32[1,64,128]{2,1,0:T(8,128)S(1)}, f32[1,64,128]{2,1,0:T(8,128)}, u32[]{:S(2)}) copy-start(f32[1,64,128]{2,1,0:T(8,128)} %param.9) | copy-start | bytes 98308
  0.7 12.0 %copy-start.6 = (bf16[1,128,2048]{2,1,0:T(8,128)(2,1)S(1)}, bf16[1,128,2048]{2,1,0:T(8,128)(2,1)}, u32[]{:S(2)}) copy-start(bf16[1,128,2048]{2,1,0:T(8,128)(2,1)} %param.8) | copy-start | bytes 1572868
  4.4 20.6 %collective-permute-start = (f32[2,528,128]{2,1,0:T(8,128)}, f32[2,528,128]{2,1,0:T(8,128)S(1)}, u32[]{:S(2)}, u32[]{:S(2)}) collective-permute-start(f32[2,528,128]{2,1,0:T(8,128)} %get-tuple-element.27), channel_id=1, source_target_pairs={{0,8},{8,16},{16,24},{24,32},{32,40},{40,48},{48,56},{56,64},{64,7... | collective-permute-start | bytes 1622024 | tf_op jit(solution)/shard_map/ppermute | solution.py:315
  6.4 18.6 %collective-permute-start.1 = (f32[2,528,128]{2,1,0:T(8,128)}, f32[2,528,128]{2,1,0:T(8,128)S(1)}, u32[]{:S(2)}, u32[]{:S(2)}) collective-permute-start(f32[2,528,128]{2,1,0:T(8,128)} %get-tuple-element.29), channel_id=1, source_target_pairs={{8,0},{16,8},{24,16},{32,24},{40,32},{48,40},{56,48},{64,56},{72,6... | collective-permute-start | bytes 1622024 | tf_op jit(solution)/shard_map/ppermute | solution.py:316
  25.0 0.8 copy-start
  25.0 1.0 copy-start.1
  96.3 15.5 %copy-start.9 = (f32[32,64,128]{2,1,0:T(8,128)}, f32[32,64,128]{2,1,0:T(8,128)S(1)}, u32[]{:S(2)}) copy-start(f32[32,64,128]{2,1,0:T(8,128)S(1)} %all_to_all.16.refs_1_) | copy-start | bytes 3145732
  96.4 15.5 %collective-permute-start.3 = (f32[32,32,128]{2,1,0:T(8,128)S(1)}, f32[32,32,128]{2,1,0:T(8,128)S(1)}, u32[]{:S(2)}, u32[]{:S(2)}) collective-permute-start(f32[32,32,128]{2,1,0:T(8,128)S(1)} %get-tuple-element.48), channel_id=1, source_target_pairs={{0,8},{8,16},{16,24},{24,32},{32,40},{40,48},{48,56},{56,64},{64,7... | collective-permute-start | bytes 1572872 | tf_op jit(solution)/shard_map/ppermute | solution.py:343
  98.0 13.9 %collective-permute-start.2 = (f32[32,32,128]{2,1,0:T(8,128)S(1)}, f32[32,32,128]{2,1,0:T(8,128)S(1)}, u32[]{:S(2)}, u32[]{:S(2)}) collective-permute-start(f32[32,32,128]{2,1,0:T(8,128)S(1)} %get-tuple-element.49), channel_id=1, source_target_pairs={{8,0},{16,8},{24,16},{32,24},{40,32},{48,40},{56,48},{64,56},{72,6... | collective-permute-start | bytes 1572872 | tf_op jit(solution)/shard_map/ppermute | solution.py:342
  111.9 0.8 copy-start.10
  111.9 0.9 copy-start.11
  119.1 13.7 %all-to-all-start.2 = ((f32[32,1,128]{2,1,0:T(1,128)}), f32[32,1,128]{2,1,0:T(1,128)S(1)}, u32[]{:S(2)}, u32[]{:S(2)}) async-start(f32[32,1,128]{2,1,0:T(1,128)} %get-tuple-element.46), calls=%async_computation.2 | async-start | bytes 32768 | tf_op jit(solution)/shard_map/all_to_all | solution.py:239
  132.9 1.2 collective-permute-start.4
  134.1 3.5 %collective-permute-start.5 = (f32[1,128]{1,0:T(1,128)S(1)}, f32[1,128]{1,0:T(1,128)S(1)}, u32[]{:S(2)}, u32[]{:S(2)}) collective-permute-start(f32[1,128]{1,0:T(1,128)S(1)} %bitcast_add_fusion), channel_id=1, source_target_pairs={{0,2},{1,3},{2,0},{3,1},{4,6},{5,7},{6,4},{7,5},{8,10},{9,11},{10,... | collective-permute-start | bytes 1544 | tf_op jit(solution)/shard_map/ppermute | solution.py:243
  137.6 5.0 %collective-permute-start.6 = (f32[1,128]{1,0:T(1,128)S(1)}, f32[1,128]{1,0:T(1,128)S(1)}, u32[]{:S(2)}, u32[]{:S(2)}) collective-permute-start(f32[1,128]{1,0:T(1,128)S(1)} %add.10), channel_id=1, source_target_pairs={{0,4},{1,5},{2,6},{3,7},{4,0},{5,1},{6,2},{7,3},{8,12},{9,13},{10,... | collective-permute-start | bytes 1544 | tf_op jit(solution)/shard_map/ppermute | solution.py:243

commit v5 on v4

--- a/solution.py
+++ b/solution.py
@@ -91,36 +91,42 @@
 
 
 def combine_kernel(position_ref, recv_state_ref, state_ref, recv_seed_ref, seed_ref, send_ref, *, blocks):
-    pad = jnp.zeros((send_ref.shape[1] - 2 * P_SIZE - 2, N), f32)
+    owners, rows, _ = send_ref.shape
+    per_owner = K // owners
+    half = per_owner * P_SIZE
+    pad = jnp.zeros((rows - 2 * half - 2 * per_owner, N), f32)
     before, after = position_ref[0] > 0, position_ref[0] < blocks - 1
-    for head in range(K):
-        rows = slice(head * P_SIZE, (head + 1) * P_SIZE)
-        decay_row = slice(GP + head, GP + head + 1)
-        state_decay = jnp.where(before, state_ref[0, decay_row, :], 0.0)
-        seed_decay = jnp.where(after, seed_ref[0, decay_row, :], 0.0)
-        send_ref[head, :P_SIZE, :] = state_decay * recv_state_ref[0, rows, :] + state_ref[0, rows, :]
-        send_ref[head, P_SIZE:2 * P_SIZE, :] = seed_decay * recv_seed_ref[0, rows, :] + seed_ref[0, rows, :]
-        send_ref[head, 2 * P_SIZE:, :] = jnp.concatenate(
-            [state_decay * recv_state_ref[0, decay_row, :], seed_decay * recv_seed_ref[0, decay_row, :], pad], axis=0)
-
-
-def scan_kernel(recv_ref, out_ref):
-    blocks = recv_ref.shape[0]
-    states, seeds = slice(0, P_SIZE), slice(P_SIZE, 2 * P_SIZE)
-    for first in range(PAIR):
-        carry = jnp.zeros((P_SIZE, N), f32)
-        for block in range(first, blocks, PAIR):
-            out_ref[block, states, :] = carry
-            carry = recv_ref[block, 2 * P_SIZE:2 * P_SIZE + 1, :] * carry + recv_ref[block, states, :]
-        if first < PAIR - 1:
-            out_ref[first, states, :] = carry
-        final = blocks - PAIR + first
-        carry = jnp.zeros((P_SIZE, N), f32)
-        for block in range(final, -1, -PAIR):
-            out_ref[block, seeds, :] = carry
-            carry = recv_ref[block, 2 * P_SIZE + 1:2 * P_SIZE + 2, :] * carry + recv_ref[block, seeds, :]
-        if first > 0:
-            out_ref[final, seeds, :] = carry
+    for owner in range(owners):
+        decays = []
+        for start, keep, recv_ref, own_ref in ((0, before, recv_state_ref, state_ref), (half, after, recv_seed_ref, seed_ref)):
+            for place in range(per_owner):
+                head = owner * per_owner + place
+                mine = slice(head * P_SIZE, (head + 1) * P_SIZE)
+                decay_row = slice(GP + head, GP + head + 1)
+                decay = jnp.where(keep, own_ref[0, decay_row, :], 0.0)
+                target = slice(start + place * P_SIZE, start + (place + 1) * P_SIZE)
+                send_ref[owner, target, :] = decay * recv_ref[0, mine, :] + own_ref[0, mine, :]
+                decays.append(decay * recv_ref[0, decay_row, :])
+        send_ref[owner, 2 * half:, :] = jnp.concatenate(decays + [pad], axis=0)
+
+
+def scan_kernel(position_ref, recv_ref, out_ref):
+    pairs, rows, _ = out_ref.shape
+    half = rows // 2
+    per_owner = half // P_SIZE
+    parity = lax.rem(position_ref[0], PAIR)
+    state = jnp.zeros((half, N), f32)
+    adjoint = jnp.zeros((half, N), f32)
+    for forward in range(pairs):
+        backward = pairs - 1 - forward
+        out_ref[forward, :half, :] = state
+        out_ref[backward, half:, :] = adjoint
+        decay = per_feature(recv_ref[forward, 2 * half:2 * half + per_owner, :])
+        state = decay * state + recv_ref[forward, :half, :]
+        decay = per_feature(recv_ref[backward, 2 * half + per_owner:2 * half + 2 * per_owner, :])
+        adjoint = decay * adjoint + recv_ref[backward, half:2 * half, :]
+    out_ref[0, :half, :] = jnp.where(parity == 0, state, 0.0)
+    out_ref[pairs - 1, half:, :] = jnp.where(parity == 1, adjoint, 0.0)
 
 
 def intra_kernel(x_ref, dy_ref, step_ref, cum_ref, key_ref, query_ref,
@@ -184,11 +190,11 @@
     @pl.when(grid_step < PG)
     def _():
         state_scratch[...] = state_in_ref[...].reshape(GP, N)
-        adjoint_scratch[...] = advanced(recv_seed_ref, carry_ref[:, P_SIZE:, :], position < blocks - 1)
+        adjoint_scratch[...] = advanced(recv_seed_ref, carry_ref[:, carry_ref.shape[1] // 2:, :], position < blocks - 1)
 
     @pl.when(grid_step >= PG)
     def _():
-        state_scratch[...] = advanced(recv_state_ref, carry_ref[:, :P_SIZE, :], position > 0)
+        state_scratch[...] = advanced(recv_state_ref, carry_ref[:, :carry_ref.shape[1] // 2, :], position > 0)
         adjoint_scratch[...] = adjoint_in_ref[...].reshape(GP, N)
 
     state, adjoint = state_scratch[...], adjoint_scratch[...]
@@ -253,8 +259,11 @@
     key_rows, query_rows = keys[0], queries[0]
     rate, skip_row = decay_rate.reshape(1, H), skip.reshape(1, H)
     position = lax.axis_index("seq").astype(jnp.int32).reshape(1)
-    owned = H // (PAIR * blocks)
-    assert owned == 1
+    pairs = blocks // PAIR
+    owned = H // blocks
+    owners = pairs // PG
+    half = owned * P_SIZE
+    parities = [list(range(parity, blocks, PAIR)) for parity in range(PAIR)]
 
     def block(dims, index):
         return pl.BlockSpec(dims, lambda s, *_: index(s))
@@ -316,31 +325,37 @@
     recv_seed = lax.ppermute(second_seeds, "seq", back)
     second_states, first_seeds = prepare(1)
 
-    slot = 2 * P_SIZE + 8
+    slot = 2 * half + 8
     send = pl.pallas_call(
         lambda *refs: combine_kernel(*refs, blocks=blocks),
         grid_spec=pltpu.PrefetchScalarGridSpec(
             num_scalar_prefetch=1,
             grid=(PG,),
             in_specs=[one_message] * 4,
-            out_specs=block((K, slot, N), lambda s: (s, 0, 0)),
+            out_specs=block((owners, slot, N), lambda s: (s, 0, 0)),
         ),
-        out_shape=shape((blocks, slot, N)),
+        out_shape=shape((pairs, slot, N)),
         compiler_params=small,
         cost_estimate=pl.CostEstimate(flops=1_000_000, bytes_accessed=3_300_000, transcendentals=0),
         name="combine",
     )(position, recv_state, second_states, recv_seed, first_seeds)
-    recv = lax.all_to_all(send, "seq", 0, 0)
+    recv = lax.all_to_all(send, "seq", 0, 0, axis_index_groups=parities)
     scanned = pl.pallas_call(
         scan_kernel,
-        out_shape=shape((blocks, 2 * P_SIZE, N)),
+        grid_spec=pltpu.PrefetchScalarGridSpec(
+            num_scalar_prefetch=1,
+            grid=(1,),
+            in_specs=[block((pairs, slot, N), lambda s: (0, 0, 0))],
+            out_specs=block((pairs, 2 * half, N), lambda s: (0, 0, 0)),
+        ),
+        out_shape=shape((pairs, 2 * half, N)),
         compiler_params=small,
         cost_estimate=pl.CostEstimate(flops=1_000_000, bytes_accessed=2_200_000, transcendentals=0),
         name="scan",
-    )(recv)
-    carries = lax.all_to_all(scanned, "seq", 0, 0)
-    state_in = lax.ppermute(carries[:, :P_SIZE], "seq", back)
-    adjoint_in = lax.ppermute(carries[:, P_SIZE:], "seq", around)
+    )(position, recv)
+    carries = lax.all_to_all(scanned, "seq", 0, 0, axis_index_groups=parities)
+    state_in = lax.ppermute(carries[:, :half], "seq", back)
+    adjoint_in = lax.ppermute(carries[:, half:], "seq", around)
 
     x_t, dy_t, intra, dq_intra, dk_intra, flow, own, sums = pl.pallas_call(
         intra_kernel,
@@ -363,8 +378,8 @@
             num_scalar_prefetch=1,
             grid=(G,),
             in_specs=[
-                block((K, 2 * P_SIZE, N), lambda s: (lax.rem(s, PG), 0, 0)),
-                stepped((K, P_SIZE, N), 0), stepped((K, P_SIZE, N), 1),
+                block((owners, 2 * half, N), lambda s: (lax.rem(s, PG), 0, 0)),
+                stepped((owners, half, N), 0), stepped((owners, half, N), 1),
                 stepped((1, MSG, N), 1), stepped((1, MSG, N), 0),
                 ordered(*features), ordered(*features), ordered(*head_rows),
                 ordered((1, 1, K, length), lambda g: (lax.div(g, PG), lax.rem(g, PG), 0, 0)),

time: 144 us -> 139 us (0.965)
  blocking collectives: 70.2 us -> 64 us
    all_to_all x2, blocking collectives: 70.2 us -> 64 us  [the longest x1 33.4 us: on_device(): recv = lax.all_to_all(send, 'seq', 0, 0, axis_index_groups=parities)]
  transfers between devices with their start and end apart: 8 -> 8, of which waited for: 5 -> 6; matrix products, arithmetic and copies ran while one was open for 0% -> 0% of each run, Pallas kernels for 12% -> 12%
where the time goes in v5:
time: 139 us
  blocking collectives  64 us (46%)
  Pallas kernels  27.1 us (19%)
  waiting for transfers between devices  23.7 us (17%)
  starting transfers between devices  20.6 us (15%)
  local copies, waits for them, and re-layouts  2.33 us (2%)
    all_to_all x1, blocking collectives, on_device(): recv = lax.all_to_all(send, 'seq', 0, 0, axis_index_groups=parities)  33.4 us
    all_to_all x1, blocking collectives, on_device(): carries = lax.all_to_all(scanned, 'seq', 0, 0, axis_index_groups=parities)  30.6 us
    ppermute x1, waiting for transfers between devices, on_device(): recv_state = lax.ppermute(first_states, 'seq', around)  10.3 us
    pallas_call x1, Pallas kernels, on_device(): pl.pallas_call(intra_kernel, grid=(G,), in_specs=[block(*tokens), block(*...  10 us
    ppermute x3, waiting for transfers between devices, total_over_devices(): row = row + lax.ppermute(row, 'dp', [(i, i ^ reach) for i in range(size)])  8.06 us
    pallas_call x1, Pallas kernels, on_device(): pl.pallas_call(lambda *refs: rates_kernel(*refs, blocks=blocks), grid_spe...  6.24 us
    ppermute x1, starting transfers between devices, on_device(): recv_seed = lax.ppermute(second_seeds, 'seq', back)  6.22 us
    pallas_call x2, Pallas kernels, prepare(): pl.pallas_call(lambda *refs: prepare_kernel(first, *refs), grid_spec=pltp...  5.79 us
  transfers between devices with their start and end apart: 8, of which 6 were waited for; matrix products, arithmetic and copies ran while one was open for 0% of the time, Pallas kernels for 12%

profile of v5, /device:TPU:16, one launch (start us, length us, event | category | flops | bytes accessed | tf_op | source)
XLA Modules:
  0.0 138.5 jit_solution(631684484969490617)
XLA Ops:
  0.7 0.0 copy-start.4
  0.7 0.0 copy-start.2
  0.7 3.7 %prepare.2 = (f32[2,528,128]{2,1,0:T(8,128)}, f32[2,528,128]{2,1,0:T(8,128)}, f32[2,2,16,128]{3,2,1,0:T(8,128)}) custom-call(s32[1]{0:T(128)} %bitcast.refs_0_.position_ref, bf16[128,2048]{1,0:T(8,128)(2,1)} %bitcast.37, f32[64,128]{1,0:T(8,128)} %bitcast.23, f32[1,64]{1,0:T(1,128)} %bitcast.34, bf16[128,512]{1,0:T(8,128)(2,1)} %bitcast.18, ...), custom_call_target="tpu_custom_call" | custom-call | flops 500000000 | bytes 2500000 | tf_op jit(solution)/shard_map/prepare/pallas_call | solution.py:305
  4.4 2.0 %collective-permute-start = (f32[2,528,128]{2,1,0:T(8,128)}, f32[2,528,128]{2,1,0:T(8,128)S(1)}, u32[]{:S(2)}, u32[]{:S(2)}) collective-permute-start(f32[2,528,128]{2,1,0:T(8,128)} %get-tuple-element.27), channel_id=1, source_target_pairs={{0,8},{8,16},{16,24},{24,32},{32,40},{40,48},{48,56},{56,64},{64,7... | collective-permute-start | bytes 1622024 | tf_op jit(solution)/shard_map/ppermute | solution.py:324
  6.4 6.2 %collective-permute-start.1 = (f32[2,528,128]{2,1,0:T(8,128)}, f32[2,528,128]{2,1,0:T(8,128)S(1)}, u32[]{:S(2)}, u32[]{:S(2)}) collective-permute-start(f32[2,528,128]{2,1,0:T(8,128)} %get-tuple-element.29), channel_id=1, source_target_pairs={{8,0},{16,8},{24,16},{32,24},{40,32},{48,40},{56,48},{64,56},{72,6... | collective-permute-start | bytes 1622024 | tf_op jit(solution)/shard_map/ppermute | solution.py:325
  12.7 2.1 %prepare.3 = (f32[2,528,128]{2,1,0:T(8,128)S(1)}, f32[2,528,128]{2,1,0:T(8,128)S(1)}) custom-call(s32[1]{0:T(128)} %bitcast.refs_0_.position_ref, bf16[128,2048]{1,0:T(8,128)(2,1)S(1)} %bitcast.39, f32[64,128]{1,0:T(8,128)S(1)} %bitcast.28, f32[1,64]{1,0:T(1,128)S(1)} %bitcast.36, bf16[128,512]{1,0:T(8,128)(2,1)S(1)} %bitcast.22, ...), custom_call_target="tpu_custom_call" | custom-call | flops 500000000 | bytes 2500000 | tf_op jit(solution)/shard_map/prepare/pallas_call | solution.py:305
  14.8 10.3 %collective-permute-done.refs_1_.refs_4_ = f32[2,528,128]{2,1,0:T(8,128)S(1)} collective-permute-done((f32[2,528,128]{2,1,0:T(8,128)}, f32[2,528,128]{2,1,0:T(8,128)S(1)}, u32[]{:S(2)}, u32[]{:S(2)}) %collective-permute-start) | collective-permute-done | bytes 540704 | tf_op jit(solution)/shard_map/ppermute | solution.py:324
  25.0 0.2 combine.1
  25.3 0.6 copy-done
  25.9 0.2 copy-done.1
  26.1 33.4 %all_to_all.15.recv_ref = f32[16,136,128]{2,1,0:T(8,128)S(1)} all-to-all(f32[16,136,128]{2,1,0:T(8,128)S(1)} %combine.1), channel_id=1, replica_groups={{0,16,32,48,64,80,96,112,128,144,160,176,192,208,224,240},{8,24,40,56,7..., dimensions={0} | all-to-all | bytes 2228224 | tf_op jit(solution)/shard_map/all_to_all | solution.py:342
  59.4 0.1 scan.1
  59.5 30.6 %all_to_all.16.refs_1_ = f32[16,128,128]{2,1,0:T(8,128)S(1)} all-to-all(f32[16,128,128]{2,1,0:T(8,128)S(1)} %scan.1), channel_id=1, replica_groups={{0,16,32,48,64,80,96,112,128,144,160,176,192,208,224,240},{8,24,40,56,7..., dimensions={0} | all-to-all | bytes 2097152 | tf_op jit(solution)/shard_map/all_to_all | solution.py:356
  90.2 0.1 fusion
  90.3 3.9 %collective-permute-start.3 = (f32[16,64,128]{2,1,0:T(8,128)S(1)}, f32[16,64,128]{2,1,0:T(8,128)S(1)}, u32[]{:S(2)}, u32[]{:S(2)}) collective-permute-start(f32[16,64,128]{2,1,0:T(8,128)S(1)} %get-tuple-element.48), channel_id=1, source_target_pairs={{0,8},{8,16},{16,24},{24,32},{32,40},{40,48},{48,56},{56,64},{64,7... | collective-permute-start | bytes 1572872 | tf_op jit(solution)/shard_map/ppermute | solution.py:358
  94.2 1.5 %collective-permute-start.2 = (f32[16,64,128]{2,1,0:T(8,128)S(1)}, f32[16,64,128]{2,1,0:T(8,128)S(1)}, u32[]{:S(2)}, u32[]{:S(2)}) collective-permute-start(f32[16,64,128]{2,1,0:T(8,128)S(1)} %get-tuple-element.49), channel_id=1, source_target_pairs={{8,0},{16,8},{24,16},{32,24},{40,32},{48,40},{56,48},{64,56},{72,6... | collective-permute-start | bytes 1572872 | tf_op jit(solution)/shard_map/ppermute | solution.py:357
  95.7 10.0 %intra.1 = (bf16[2048,128]{1,0:T(8,128)(2,1)}, bf16[2048,128]{1,0:T(8,128)(2,1)}, f32[2048,128]{1,0:T(8,128)}, f32[128,512]{1,0:T(8,128)}, f32[128,512]{1,0:T(8,...) custom-call(bf16[128,2048]{1,0:T(8,128)(2,1)} %bitcast.38, bf16[128,2048]{1,0:T(8,128)(2,1)} %bitcast.41, ...), custom_call_target="tpu_custom_call" | custom-call | flops 2000000000 | bytes 5000000 | tf_op jit(solution)/shard_map/intra/pallas_call | solution.py:360
  105.7 0.3 collective-permute-done.2.refs_2_
  106.0 0.5 copy-done.10
  106.5 0.3 copy-done.11
  106.8 6.2 %rates.1 = (f32[64,128]{1,0:T(8,128)}, f32[32,1,128]{2,1,0:T(1,128)}, bf16[2048,128]{1,0:T(8,128)(2,1)}, bf16[2048,128]{1,0:T(8,128)(2,1)}) custom-call(s32[1]{0:T(128)} %bitcast.refs_0_.position_ref, f32[16,128,128]{2,1,0:T(8,128)} %copy-done.9, f32[16,64,128]{2,1,0:T(8,128)} %copy-done.11, f32[16,64,128]{2,1,0:T(8,128)} %copy-done.10, ...), custom_call_target="tpu_custom_call" | custom-call | flops 140000000 | bytes 6000000 | tf_op jit(solution)/shard_map/rates/pallas_call | solution.py:375
  113.0 5.3 %all-to-all-start.2 = ((f32[32,1,128]{2,1,0:T(1,128)}), f32[32,1,128]{2,1,0:T(1,128)S(1)}, u32[]{:S(2)}, u32[]{:S(2)}) async-start(f32[32,1,128]{2,1,0:T(1,128)} %get-tuple-element.46), calls=%async_computation.2 | async-start | bytes 32768 | tf_op jit(solution)/shard_map/all_to_all | solution.py:245
  118.3 4.7 %finish.1 = (bf16[128,2048]{1,0:T(8,128)(2,1)}, bf16[128,512]{1,0:T(8,128)(2,1)}, bf16[128,512]{1,0:T(8,128)(2,1)}) custom-call(bf16[2048,128]{1,0:T(8,128)(2,1)} %get-tuple-element.37.state_low_ref, bf16[2048,128]{1,0:T(8,128)(2,1)} %get-tuple-element.38.adjoint_low_ref, bf16[2048,128]{1,0:T(8,128)(2,1)} %get-tuple-element.32.refs_6_.xt_ref, ...), custom_call_target="tpu_custom_call" | custom-call | flops 1000000000 | bytes 5000000 | tf_op jit(solution)/shard_map/finish/pallas_call | solution.py:399
  123.0 5.0 %all-to-all-done.2 = f32[32,1,128]{2,1,0:T(1,128)S(1)} async-done(((f32[32,1,128]{2,1,0:T(1,128)}), f32[32,1,128]{2,1,0:T(1,128)S(1)}, u32[]{:S(2)}, u32[]{:S(2)}) %all-to-all-start.2) | async-done | bytes 16416 | tf_op jit(solution)/shard_map/all_to_all | solution.py:245
  128.1 0.1 reduce_sum.11
  128.1 0.1 collective-permute-start.4
  128.2 1.1 collective-permute-done.4
  129.3 1.3 collective-permute-start.5
  130.6 2.3 %collective-permute-done.5 = f32[1,128]{1,0:T(1,128)S(1)} collective-permute-done((f32[1,128]{1,0:T(1,128)S(1)}, f32[1,128]{1,0:T(1,128)S(1)}, u32[]{:S(2)}, u32[]{:S(2)}) %collective-permute-start.5) | collective-permute-done | bytes 544 | tf_op jit(solution)/shard_map/ppermute | solution.py:249
  132.9 0.3 collective-permute-start.6
  133.2 4.7 %collective-permute-done.6 = f32[1,128]{1,0:T(1,128)S(1)} collective-permute-done((f32[1,128]{1,0:T(1,128)S(1)}, f32[1,128]{1,0:T(1,128)S(1)}, u32[]{:S(2)}, u32[]{:S(2)}) %collective-permute-start.6) | collective-permute-done | bytes 544 | tf_op jit(solution)/shard_map/ppermute | solution.py:249
  137.9 0.6 slice_bitcast_fusion
  (23 shorter events, 0.1 us)
Async XLA Ops:
  0.6 12.0 %copy-start.8 = (f32[1,128]{1,0:T(1,128)S(1)}, f32[1,128]{1,0:T(1,128)}, u32[]{:S(2)}) copy-start(f32[1,128]{1,0:T(1,128)} %refs_7_.3) | copy-start | bytes 1540
  0.6 12.0 %copy-start.7 = (bf16[1,128,2048]{2,1,0:T(8,128)(2,1)S(1)}, bf16[1,128,2048]{2,1,0:T(8,128)(2,1)}, u32[]{:S(2)}) copy-start(bf16[1,128,2048]{2,1,0:T(8,128)(2,1)} %param.15) | copy-start | bytes 1572868
  0.7 12.0 %copy-start.4 = (bf16[1,128,512]{2,1,0:T(8,128)(2,1)S(1)}, bf16[1,128,512]{2,1,0:T(8,128)(2,1)}, u32[]{:S(2)}) copy-start(bf16[1,128,512]{2,1,0:T(8,128)(2,1)} %param.14) | copy-start | bytes 393220
  0.7 12.0 %copy-start.2 = (bf16[1,128,512]{2,1,0:T(8,128)(2,1)S(1)}, bf16[1,128,512]{2,1,0:T(8,128)(2,1)}, u32[]{:S(2)}) copy-start(bf16[1,128,512]{2,1,0:T(8,128)(2,1)} %param.13) | copy-start | bytes 393220
  0.7 12.0 %copy-start.5 = (f32[64]{0:T(128)S(1)}, f32[64]{0:T(128)}, u32[]{:S(2)}) copy-start(f32[64]{0:T(128)} %param.11) | copy-start | bytes 772
  0.7 12.0 %copy-start.3 = (f32[1,64,128]{2,1,0:T(8,128)S(1)}, f32[1,64,128]{2,1,0:T(8,128)}, u32[]{:S(2)}) copy-start(f32[1,64,128]{2,1,0:T(8,128)} %param.9) | copy-start | bytes 98308
  0.7 12.0 %copy-start.6 = (bf16[1,128,2048]{2,1,0:T(8,128)(2,1)S(1)}, bf16[1,128,2048]{2,1,0:T(8,128)(2,1)}, u32[]{:S(2)}) copy-start(bf16[1,128,2048]{2,1,0:T(8,128)(2,1)} %param.8) | copy-start | bytes 1572868
  4.4 20.6 %collective-permute-start = (f32[2,528,128]{2,1,0:T(8,128)}, f32[2,528,128]{2,1,0:T(8,128)S(1)}, u32[]{:S(2)}, u32[]{:S(2)}) collective-permute-start(f32[2,528,128]{2,1,0:T(8,128)} %get-tuple-element.27), channel_id=1, source_target_pairs={{0,8},{8,16},{16,24},{24,32},{32,40},{40,48},{48,56},{56,64},{64,7... | collective-permute-start | bytes 1622024 | tf_op jit(solution)/shard_map/ppermute | solution.py:324
  6.4 18.6 %collective-permute-start.1 = (f32[2,528,128]{2,1,0:T(8,128)}, f32[2,528,128]{2,1,0:T(8,128)S(1)}, u32[]{:S(2)}, u32[]{:S(2)}) collective-permute-start(f32[2,528,128]{2,1,0:T(8,128)} %get-tuple-element.29), channel_id=1, source_target_pairs={{8,0},{16,8},{24,16},{32,24},{40,32},{48,40},{56,48},{64,56},{72,6... | collective-permute-start | bytes 1622024 | tf_op jit(solution)/shard_map/ppermute | solution.py:325
  25.0 0.8 copy-start
  25.0 1.0 copy-start.1
  90.2 15.6 %copy-start.9 = (f32[16,128,128]{2,1,0:T(8,128)}, f32[16,128,128]{2,1,0:T(8,128)S(1)}, u32[]{:S(2)}) copy-start(f32[16,128,128]{2,1,0:T(8,128)S(1)} %all_to_all.16.refs_1_) | copy-start | bytes 3145732
  90.3 15.5 %collective-permute-start.3 = (f32[16,64,128]{2,1,0:T(8,128)S(1)}, f32[16,64,128]{2,1,0:T(8,128)S(1)}, u32[]{:S(2)}, u32[]{:S(2)}) collective-permute-start(f32[16,64,128]{2,1,0:T(8,128)S(1)} %get-tuple-element.48), channel_id=1, source_target_pairs={{0,8},{8,16},{16,24},{24,32},{32,40},{40,48},{48,56},{56,64},{64,7... | collective-permute-start | bytes 1572872 | tf_op jit(solution)/shard_map/ppermute | solution.py:358
  94.2 11.8 %collective-permute-start.2 = (f32[16,64,128]{2,1,0:T(8,128)S(1)}, f32[16,64,128]{2,1,0:T(8,128)S(1)}, u32[]{:S(2)}, u32[]{:S(2)}) collective-permute-start(f32[16,64,128]{2,1,0:T(8,128)S(1)} %get-tuple-element.49), channel_id=1, source_target_pairs={{8,0},{16,8},{24,16},{32,24},{40,32},{48,40},{56,48},{64,56},{72,6... | collective-permute-start | bytes 1572872 | tf_op jit(solution)/shard_map/ppermute | solution.py:357
  105.7 0.8 copy-start.10
  106.0 0.8 copy-start.11
  113.0 15.0 %all-to-all-start.2 = ((f32[32,1,128]{2,1,0:T(1,128)}), f32[32,1,128]{2,1,0:T(1,128)S(1)}, u32[]{:S(2)}, u32[]{:S(2)}) async-start(f32[32,1,128]{2,1,0:T(1,128)} %get-tuple-element.46), calls=%async_computation.2 | async-start | bytes 32768 | tf_op jit(solution)/shard_map/all_to_all | solution.py:245
  128.1 1.2 collective-permute-start.4
  129.3 3.5 %collective-permute-start.5 = (f32[1,128]{1,0:T(1,128)S(1)}, f32[1,128]{1,0:T(1,128)S(1)}, u32[]{:S(2)}, u32[]{:S(2)}) collective-permute-start(f32[1,128]{1,0:T(1,128)S(1)} %bitcast_add_fusion), channel_id=1, source_target_pairs={{0,2},{1,3},{2,0},{3,1},{4,6},{5,7},{6,4},{7,5},{8,10},{9,11},{10,... | collective-permute-start | bytes 1544 | tf_op jit(solution)/shard_map/ppermute | solution.py:249
  132.9 5.0 %collective-permute-start.6 = (f32[1,128]{1,0:T(1,128)S(1)}, f32[1,128]{1,0:T(1,128)S(1)}, u32[]{:S(2)}, u32[]{:S(2)}) collective-permute-start(f32[1,128]{1,0:T(1,128)S(1)} %add.10), channel_id=1, source_target_pairs={{0,4},{1,5},{2,6},{3,7},{4,0},{5,1},{6,2},{7,3},{8,12},{9,13},{10,... | collective-permute-start | bytes 1544 | tf_op jit(solution)/shard_map/ppermute | solution.py:249

commit v6 on v5

v6 whole, which is shorter than its diff:
```python
import jax
import jax.numpy as jnp
from jax import lax
from jax.experimental import pallas as pl
from jax.experimental.pallas import tpu as pltpu
from jax.sharding import PartitionSpec as P

H = 64
P_SIZE = 32
N = 128
G = 4
K = 16
GP = K * P_SIZE
SPAN = 4
MSG = GP + K

highest = lax.Precision.HIGHEST
f32 = jnp.float32
bf16 = jnp.bfloat16
VMEM_LIMIT = 60 * 1024 * 1024
SMALL_LIMIT = 16 * 1024 * 1024


def contract(left, right, dims):
    return lax.dot_general(left, right, ((dims[:1], dims[1:]), ((), ())), preferred_element_type=f32)


def per_feature(rows):
    heads, length = rows.shape
    return jnp.broadcast_to(rows[:, None, :], (heads, P_SIZE, length)).reshape(heads * P_SIZE, length)


def head_sum(features):
    return jnp.sum(features.reshape(-1, P_SIZE, features.shape[1]), axis=1)


def triangle(length, upper):
    row = lax.broadcasted_iota(jnp.int32, (length, length), 0)
    col = lax.broadcasted_iota(jnp.int32, (length, length), 1)
    return row <= col if upper else row >= col


def group_at(position, place):
    return lax.rem(position + SPAN - place, SPAN)


def column_of_group(row_ref, group):
    first = group * K
    row = lax.broadcasted_iota(jnp.int32, (K, H), 0)
    lane = lax.broadcasted_iota(jnp.int32, (K, H), 1)
    return jnp.sum(jnp.where(lane == first + row, row_ref[...], 0.0), axis=1, keepdims=True)


def row_of_group(column, group, offset):
    first = group * K + offset
    row = lax.broadcasted_iota(jnp.int32, (K, 2 * H), 0)
    lane = lax.broadcasted_iota(jnp.int32, (K, 2 * H), 1)
    return jnp.sum(jnp.where(lane == first + row, column, 0.0), axis=0, keepdims=True)


def accumulate(ref, start, value):
    @pl.when(pl.program_id(0) == 0)
    def _():
        ref[...] = start

    ref[...] += value


def prepare_kernel(first, position_ref, x_ref, x_step_ref, rate_ref, key_ref,
                   dy_ref, dy_step_ref, gate_ref, query_ref, state_ref, seed_ref, *cum_refs):
    length = x_ref.shape[0]
    hop = first + pl.program_id(0)
    upper = triangle(length, True).astype(f32)
    sides = ((True, hop, x_ref, x_step_ref, key_ref, state_ref),
             (False, SPAN - 1 - hop, dy_ref, dy_step_ref, query_ref, seed_ref))
    for forward, place, features_ref, step_ref, rows_ref, out_ref in sides:
        group = group_at(position_ref[0], place)
        step = step_ref[...]
        log_decay = gate_ref[...] - column_of_group(rate_ref, group) * step
        cum = jnp.dot(log_decay, upper, precision=highest)
        if cum_refs:
            cum_refs[0][group] = cum
        last = cum[:, length - 1:]
        weight = step * jnp.exp(last - cum) if forward else jnp.exp(cum)
        weighted = (features_ref[...].astype(f32).T * per_feature(weight)).astype(bf16)
        out_ref[0, :GP, :] = contract(weighted, rows_ref[...], (1, 0))
        out_ref[0, GP:, :] = jnp.broadcast_to(jnp.exp(last), (K, N))


def link_kernel(position_ref, recv_state_ref, state_ref, recv_seed_ref, seed_ref, state_out_ref, seed_out_ref, *, blocks):
    before, after = position_ref[0] > 0, position_ref[0] < blocks - 1
    for keep, recv_ref, own_ref, out_ref in ((before, recv_state_ref, state_ref, state_out_ref),
                                             (after, recv_seed_ref, seed_ref, seed_out_ref)):
        decay = jnp.where(keep, own_ref[0, GP:, :], 0.0)
        out_ref[0, :GP, :] = per_feature(decay) * recv_ref[0, :GP, :] + own_ref[0, :GP, :]
        out_ref[0, GP:, :] = decay * recv_ref[0, GP:, :]


def combine_kernel(position_ref, recv_state_ref, state_ref, recv_seed_ref, seed_ref, send_ref, *, blocks):
    owners, rows, _ = send_ref.shape
    per_owner = K // owners
    half = per_owner * P_SIZE
    pad = jnp.zeros((rows - 2 * half - 2 * per_owner, N), f32)
    before, after = position_ref[0] > 0, position_ref[0] < blocks - 1
    for owner in range(owners):
        decays = []
        for start, keep, recv_ref, own_ref in ((0, before, recv_state_ref, state_ref), (half, after, recv_seed_ref, seed_ref)):
            for place in range(per_owner):
                head = owner * per_owner + place
                mine = slice(head * P_SIZE, (head + 1) * P_SIZE)
                decay_row = slice(GP + head, GP + head + 1)
                decay = jnp.where(keep, own_ref[0, decay_row, :], 0.0)
                target = slice(start + place * P_SIZE, start + (place + 1) * P_SIZE)
                send_ref[owner, target, :] = decay * recv_ref[0, mine, :] + own_ref[0, mine, :]
                decays.append(decay * recv_ref[0, decay_row, :])
        send_ref[owner, 2 * half:, :] = jnp.concatenate(decays + [pad], axis=0)


def scan_kernel(position_ref, recv_ref, out_ref):
    spans, rows, _ = out_ref.shape
    half = rows // 2
    per_owner = half // P_SIZE
    place = lax.rem(position_ref[0], SPAN)
    state = jnp.zeros((half, N), f32)
    adjoint = jnp.zeros((half, N), f32)
    for forward in range(spans):
        backward = spans - 1 - forward
        out_ref[forward, :half, :] = state
        out_ref[backward, half:, :] = adjoint
        decay = per_feature(recv_ref[forward, 2 * half:2 * half + per_owner, :])
        state = decay * state + recv_ref[forward, :half, :]
        decay = per_feature(recv_ref[backward, 2 * half + per_owner:2 * half + 2 * per_owner, :])
        adjoint = decay * adjoint + recv_ref[backward, half:2 * half, :]
    out_ref[0, :half, :] = jnp.where(place < SPAN - 1, state, 0.0)
    out_ref[spans - 1, half:, :] = jnp.where(place > 0, adjoint, 0.0)


def intra_kernel(first, x_ref, dy_ref, step_ref, cum_ref, key_ref, query_ref, sums_in_ref, *refs):
    xt_ref, dyt_ref, intra_ref, dq_ref, dk_ref, flow_ref, own_ref, skip_ref = refs[-8:]
    length = dy_ref.shape[0]
    x_full = x_ref[...].astype(f32).T
    dy_full = dy_ref[...].astype(f32).T
    xt_ref[...] = x_full.astype(bf16)
    dyt_ref[...] = dy_full.astype(bf16)
    keys, queries = key_ref[...], query_ref[...]
    scores = contract(queries, keys, (1, 1))
    causal = triangle(length, False)
    cum = cum_ref[0]
    cum_cols = cum.T
    step = step_ref[...]
    four = 128 // P_SIZE
    head_of_row = lax.broadcasted_iota(jnp.int32, (128, length), 0) // P_SIZE
    shared = jnp.zeros((length, length), f32)
    row_sums, col_sums = [], []
    for quad in range(K // four):
        lanes = slice(quad * 128, (quad + 1) * 128)
        x_quad = x_full[lanes, :]
        spread = jnp.concatenate(
            [jnp.where(head_of_row == i, x_quad, 0.0).astype(bf16) for i in range(four)], axis=1)
        dots = contract(dy_ref[:, lanes], spread, (1, 0))
        for i in range(four):
            head = quad * four + i
            gaps = cum_cols[:, head:head + 1] - cum[head:head + 1, :]
            decays = jnp.exp(jnp.where(causal, gaps, -1e30))
            mixing_low = (decays * scores).astype(bf16)
            pairs = decays * (dots[:, i * length:(i + 1) * length] * step[head:head + 1, :])
            shared = shared + pairs
            weighted = pairs * scores
            row_sums.append(jnp.sum(weighted, axis=1, keepdims=True))
            col_sums.append(jnp.sum(weighted, axis=0, keepdims=True))
            rows = slice(head * P_SIZE, (head + 1) * P_SIZE)
            intra_ref[rows, :] = contract(dyt_ref[rows, :], mixing_low, (1, 0))
    shared_low = shared.astype(bf16)
    dq_ref[...] = contract(shared_low, keys, (1, 0))
    dk_ref[...] = contract(shared_low, queries, (0, 0))
    flow_ref[...] = jnp.concatenate(row_sums, axis=1).T - jnp.concatenate(col_sums, axis=0)
    own_ref[...] = head_sum(x_full * intra_ref[...])
    skip_part = jnp.sum(head_sum(x_full * dy_full), axis=1, keepdims=True)
    accumulate(skip_ref, sums_in_ref[...], row_of_group(skip_part, first + pl.program_id(0), H))


def rates_kernel(places, blocks, position_ref, *refs):
    refs = list(refs)
    parts = [refs.pop(0) for _ in range(8)]
    (xt_ref, dyt_ref, step_ref, cum_ref, rate_ref, key_ref, query_ref, flow_ref, own_ref, sums_in_ref) = refs[:10]
    (dstep_ref, state_low_ref, adjoint_low_ref, sums_ref, state_scratch, adjoint_scratch, sums_scratch) = refs[-7:]
    grid_step = pl.program_id(0)
    position = position_ref[0]
    group = group_at(position, places[0] + grid_step * (places[1] - places[0]))
    length = step_ref.shape[1]

    def advanced(carry_ref, recv_ref, edge, inside):
        carry = carry_ref[...].reshape(GP, N)
        if edge:
            return carry
        moved = per_feature(recv_ref[0, GP:, :]) * carry + recv_ref[0, :GP, :]
        return jnp.where(inside, moved, 0.0)

    for index, place in enumerate(places):
        @pl.when(grid_step == index)
        def _():
            carry_state, recv_state, carry_adjoint, recv_seed = parts[4 * index:4 * index + 4]
            state_scratch[...] = advanced(carry_state, recv_state, place == 0, position > 0)
            adjoint_scratch[...] = advanced(carry_adjoint, recv_seed, place == SPAN - 1, position < blocks - 1)

    state, adjoint = state_scratch[...], adjoint_scratch[...]
    state_low, adjoint_low = state.astype(bf16), adjoint.astype(bf16)
    state_low_ref[...] = state_low
    adjoint_low_ref[...] = adjoint_low
    state_term = contract(adjoint_low, key_ref[...], (1, 1))
    carried = contract(state_low, query_ref[...], (1, 1))
    cum, step, rate = cum_ref[0], step_ref[...], column_of_group(rate_ref, group)
    last = cum[:, length - 1:]
    tail = jnp.exp(last - cum)
    entry_term = jnp.exp(cum) * head_sum(dyt_ref[...].astype(f32) * carried)
    outside = tail * head_sum(xt_ref[...].astype(f32) * state_term)
    exit_term = step * outside
    closing = jnp.exp(last) * jnp.sum(head_sum(adjoint * state), axis=1, keepdims=True) + jnp.sum(
        exit_term, axis=1, keepdims=True)
    final_slot = lax.broadcasted_iota(jnp.int32, (K, length), 1) == length - 1
    d_cum = flow_ref[...] + entry_term - exit_term + jnp.where(final_slot, closing, 0.0)
    d_logs = jnp.dot(d_cum, triangle(length, False).astype(f32), precision=highest)
    dstep_ref[...] = own_ref[...] + outside - rate * d_logs
    rate_part = -rate * jnp.sum(step * d_logs, axis=1, keepdims=True)
    accumulate(sums_scratch, sums_in_ref[...], row_of_group(rate_part, group, 0))

    @pl.when(grid_step == len(places) - 1)
    def _():
        sums_ref[...] = jnp.broadcast_to(sums_scratch[...].reshape((1,) * (len(sums_ref.shape) - 2) + (1, 2 * H)), sums_ref.shape)


def finish_kernel(state_low_ref, adjoint_low_ref, xt_ref, dyt_ref, step_ref, cum_ref, skip_ref, key_ref,
                  intra_ref, dq_in_ref, dk_in_ref, dx_ref, dk_ref, dq_ref):
    group = pl.program_id(0)
    length = step_ref.shape[1]
    cum, step = cum_ref[0], step_ref[...]
    growth, tail = jnp.exp(cum), jnp.exp(cum[:, length - 1:] - cum)
    x_t, dy_t = xt_ref[...].astype(f32), dyt_ref[...].astype(f32)
    state_low, adjoint_low = state_low_ref[...], adjoint_low_ref[...]
    weighted_grads = (dy_t * per_feature(growth)).astype(bf16)
    weighted_inputs = (x_t * per_feature(step * tail)).astype(bf16)
    dq_ref[...] = (dq_in_ref[...] + contract(weighted_grads, state_low, (0, 0))).astype(bf16)
    dk_ref[...] = (dk_in_ref[...] + contract(weighted_inputs, adjoint_low, (0, 0))).astype(bf16)
    state_term = contract(adjoint_low, key_ref[...], (1, 1))
    d_scaled = intra_ref[...] + per_feature(tail) * state_term
    skips = jnp.broadcast_to(column_of_group(skip_ref, group), (K, length))
    dx_ref[...] = (per_feature(step) * d_scaled + per_feature(skips) * dy_t).T.astype(bf16)


def total_over_devices(copies, beside):
    row, _ = lax.optimization_barrier((lax.all_to_all(copies, "seq", 0, 0), beside))
    row = jnp.sum(row, axis=0)
    size, reach = lax.axis_size("dp"), 1
    while reach < size:
        row = row + lax.ppermute(row, "dp", [(i, i ^ reach) for i in range(size)])
        reach *= 2
    return row


def on_device(inputs, step_sizes, gate, decay_rate, skip, keys, queries, grads):
    length = inputs.shape[1]
    blocks = lax.axis_size("seq")
    tokens_all = length * blocks * lax.axis_size("dp")
    x, dy, step = inputs[0], grads[0], step_sizes[0]
    key_rows, query_rows = keys[0], queries[0]
    rate, skip_row = decay_rate.reshape(1, H), skip.reshape(1, H)
    position = lax.axis_index("seq").astype(jnp.int32).reshape(1)
    spans = blocks // SPAN
    owned = K // spans
    half = owned * P_SIZE
    remainders = [list(range(place, blocks, SPAN)) for place in range(SPAN)]

    def block(dims, index):
        return pl.BlockSpec(dims, lambda s, *_: index(s))

    def placed_at(place_of_step, dims, index):
        return pl.BlockSpec(dims, lambda s, position_ref: index(group_at(position_ref[0], place_of_step(s))))

    def shape(dims, dtype=f32):
        return jax.ShapeDtypeStruct(dims, dtype)

    params = pltpu.CompilerParams(vmem_limit_bytes=VMEM_LIMIT)
    small = pltpu.CompilerParams(vmem_limit_bytes=SMALL_LIMIT)
    tokens = ((length, GP), lambda g: (0, g))
    features = ((GP, length), lambda g: (g, 0))
    head_rows = ((K, length), lambda g: (g, 0))
    cum_rows = ((1, K, length), lambda g: (g, 0, 0))
    group_rows = ((length, N), lambda g: (0, g))
    gate_row = block((1, length), lambda s: (0, 0))
    per_head = block((1, H), lambda s: (0, 0))
    sums_row = block((1, 2 * H), lambda s: (0, 0))
    one_message = block((1, MSG, N), lambda s: (s, 0, 0))
    whole_message = block((1, MSG, N), lambda s: (0, 0, 0))
    anywhere = pl.BlockSpec(memory_space=pl.ANY)
    low_states = shape((H * P_SIZE, N), bf16)

    def prepare(first, hops):
        forward, backward = lambda s: first + s, lambda s: SPAN - 1 - first - s
        made = pltpu.VMEM if first > 0 else shape
        out_specs, out_shape = [one_message] * 2, [made((hops, MSG, N), f32)] * 2
        if first > 0:
            out_specs.append(block((G, K, length), lambda s: (0, 0, 0)))
            out_shape.append(shape((G, K, length)))
        return pl.pallas_call(
            lambda *refs: prepare_kernel(first, *refs),
            grid_spec=pltpu.PrefetchScalarGridSpec(
                num_scalar_prefetch=1,
                grid=(hops,),
                in_specs=[placed_at(forward, *tokens), placed_at(forward, *head_rows), per_head,
                          placed_at(forward, *group_rows), placed_at(backward, *tokens),
                          placed_at(backward, *head_rows), gate_row, placed_at(backward, *group_rows)],
                out_specs=out_specs,
            ),
            out_shape=out_shape,
            compiler_params=small if first > 0 else params,
            cost_estimate=pl.CostEstimate(flops=400_000_000 * hops, bytes_accessed=1_300_000 * hops, transcendentals=0),
            name="prepare",
        )(position, x, step, rate, key_rows, dy, step, gate, query_rows)

    around = [(i, (i + 1) % blocks) for i in range(blocks)]
    back = [(j, i) for i, j in around]
    state, seed = prepare(0, 1)
    next_states, next_seeds, cum = prepare(1, SPAN - 1)
    def intra_half(first, sums, earlier):
        steps = G // 2

        def at(dims, index):
            return block(dims, lambda s: index(first + s))

        return pl.pallas_call(
            lambda *refs: intra_kernel(first, *refs),
            grid=(steps,),
            in_specs=[at(*tokens), at(*tokens), at(*head_rows), at(*cum_rows), at(*group_rows), at(*group_rows),
                      sums_row] + [anywhere] * len(earlier),
            out_specs=[at(*features), at(*features), at(*features), at(*group_rows), at(*group_rows),
                       at(*head_rows), at(*head_rows), sums_row],
            out_shape=[shape((H * P_SIZE, length), bf16), shape((H * P_SIZE, length), bf16),
                       shape((H * P_SIZE, length)), shape((length, G * N)), shape((length, G * N)),
                       shape((H, length)), shape((H, length)), shape((1, 2 * H))],
            input_output_aliases={7 + i: i for i in range(len(earlier))},
            compiler_params=params,
            cost_estimate=pl.CostEstimate(flops=2_000_000_000, bytes_accessed=2_500_000, transcendentals=500_000),
            name="intra",
        )(x, dy, step, cum, key_rows, query_rows, sums, *earlier)

    recv_states, recv_seeds = [None], [None]
    slot = 2 * half + 8
    for hop in range(1, SPAN):
        recv_states.append(lax.ppermute(state, "seq", around))
        recv_seeds.append(lax.ppermute(seed, "seq", back))
        if hop == 2:
            outcome = intra_half(0, jnp.zeros((1, 2 * H), f32), ())
        if hop == 3:
            outcome = intra_half(G // 2, sums, tuple(outcome[:-1]))
        if hop > 1:
            recv_seeds[-1], sums = lax.optimization_barrier((recv_seeds[-1], outcome[-1]))
        own = block((1, MSG, N), lambda s, hop=hop: (hop - 1, 0, 0))
        final = hop == SPAN - 1
        linked = pl.pallas_call(
            lambda *refs, final=final: (combine_kernel if final else link_kernel)(*refs, blocks=blocks),
            grid_spec=pltpu.PrefetchScalarGridSpec(
                num_scalar_prefetch=1,
                grid=(1,),
                in_specs=[whole_message, own, whole_message, own],
                out_specs=block((spans, slot, N), lambda s: (0, 0, 0)) if final else [whole_message] * 2,
            ),
            out_shape=shape((spans, slot, N)) if final else [shape((1, MSG, N))] * 2,
            compiler_params=small,
            cost_estimate=pl.CostEstimate(flops=300_000, bytes_accessed=1_600_000, transcendentals=0),
            name="combine" if final else "link",
        )(position, recv_states[-1], next_states, recv_seeds[-1], next_seeds)
        if final:
            send = linked
        else:
            state, seed = linked

    recv = lax.all_to_all(send, "seq", 0, 0, axis_index_groups=remainders)
    scanned = pl.pallas_call(
        scan_kernel,
        grid_spec=pltpu.PrefetchScalarGridSpec(
            num_scalar_prefetch=1,
            grid=(1,),
            in_specs=[block((spans, slot, N), lambda s: (0, 0, 0))],
            out_specs=block((spans, 2 * half, N), lambda s: (0, 0, 0)),
        ),
        out_shape=shape((spans, 2 * half, N)),
        compiler_params=small,
        cost_estimate=pl.CostEstimate(flops=500_000, bytes_accessed=1_100_000, transcendentals=0),
        name="scan",
    )(position, recv)
    carries = lax.all_to_all(scanned, "seq", 0, 0, axis_index_groups=remainders)
    carry_states, carry_seeds = [carries[:, :half]], [carries[:, half:]]
    for _ in range(SPAN - 1):
        carry_states.append(lax.ppermute(carry_states[-1], "seq", back))
        carry_seeds.append(lax.ppermute(carry_seeds[-1], "seq", around))

    x_t, dy_t, intra, dq_intra, dk_intra, flow, own_dots, _ = outcome

    def rates(places, sums, earlier):
        def place_of_step(s):
            return places[0] + s * (places[1] - places[0])

        parts, part_specs = [], []
        carry_spec = block((spans, half, N), lambda s: (0, 0, 0))
        for place in places:
            rank = SPAN - 1 - place
            parts += [carry_states[rank], recv_states[max(place, 1)], carry_seeds[place], recv_seeds[max(rank, 1)]]
            part_specs += [carry_spec, whole_message] * 2
        final = bool(earlier)
        sum_dims = (blocks, 1, 2 * H) if final else (1, 2 * H)
        group_of_step = lambda dims, index: placed_at(place_of_step, dims, index)
        low_rows = ((GP, N), lambda g: (g, 0))
        return pl.pallas_call(
            lambda *refs: rates_kernel(places, blocks, *refs),
            grid_spec=pltpu.PrefetchScalarGridSpec(
                num_scalar_prefetch=1,
                grid=(len(places),),
                in_specs=part_specs + [
                    group_of_step(*features), group_of_step(*features), group_of_step(*head_rows),
                    group_of_step(*cum_rows), per_head, group_of_step(*group_rows), group_of_step(*group_rows),
                    group_of_step(*head_rows), group_of_step(*head_rows), sums_row] + [anywhere] * len(earlier),
                out_specs=[group_of_step(*head_rows), group_of_step(*low_rows), group_of_step(*low_rows),
                           block(sum_dims, lambda s: (0,) * len(sum_dims))],
                scratch_shapes=[pltpu.VMEM((GP, N), f32), pltpu.VMEM((GP, N), f32), pltpu.VMEM((1, 2 * H), f32)],
            ),
            out_shape=[shape((H, length)), low_states, low_states, shape(sum_dims)],
            input_output_aliases={19 + i: i for i in range(len(earlier))},
            compiler_params=params,
            cost_estimate=pl.CostEstimate(flops=1_000_000_000, bytes_accessed=3_000_000, transcendentals=10_000),
            name="rates",
        )(position, *parts, x_t, dy_t, step, cum, rate, key_rows, query_rows, flow, own_dots, sums, *earlier)

    outcome = rates((1, 2), sums, ())
    d_steps, state_low, adjoint_low, sum_copies = rates((0, 3), outcome[-1], tuple(outcome[:-1]))

    d_inputs, d_keys, d_queries = pl.pallas_call(
        finish_kernel,
        grid=(G,),
        in_specs=[block((GP, N), lambda g: (g, 0)), block((GP, N), lambda g: (g, 0)), block(*features),
                  block(*features), block(*head_rows), block(*cum_rows), per_head, block(*group_rows),
                  block(*features), block(*group_rows), block(*group_rows)],
        out_specs=[block(*tokens), block(*group_rows), block(*group_rows)],
        out_shape=[shape((length, H * P_SIZE), bf16), shape((length, G * N), bf16), shape((length, G * N), bf16)],
        compiler_params=params,
        cost_estimate=pl.CostEstimate(flops=1_000_000_000, bytes_accessed=5_000_000, transcendentals=20_000),
        name="finish",
    )(state_low, adjoint_low, x_t, dy_t, step, cum, skip_row, key_rows, intra, dq_intra, dk_intra)

    totals = total_over_devices(sum_copies, d_keys)[0] / tokens_all
    return (d_inputs[None], d_steps[None], d_keys[None], d_queries[None], totals[:H], totals[H:])


def solution(mesh):
    placed = (
        P("dp", "seq", None),
        P("dp", None, "seq"),
        P("dp", "seq"),
        P(),
        P(),
        P("dp", "seq", None),
        P("dp", "seq", None),
        P("dp", "seq", None),
    )
    return jax.shard_map(
        on_device,
        mesh=mesh,
        in_specs=placed,
        out_specs=(
            P("dp", "seq", None),
            P("dp", None, "seq"),
            P("dp", "seq", None),
            P("dp", "seq", None),
            P(),
            P(),
        ),
        check_vma=False,
    )
```

time: 139 us -> 151 us (1.086)
  blocking collectives: 64 us -> 37.9 us
  starting transfers between devices: 20.6 us -> 40.3 us
  waiting for transfers between devices: 23.7 us -> 37 us
  Pallas kernels: 27.1 us -> 30.8 us
  local copies, waits for them, and re-layouts: 2.33 us -> 3.99 us
    all_to_all x2, blocking collectives: 64 us -> 37.9 us  [the longest x1 20.3 us: on_device(): carries = lax.all_to_all(scanned, 'seq', 0, 0, axis_index_groups=remainders)]
    ppermute x4 -> x12, starting transfers between devices: 13.6 us -> 31.6 us  [the longest x3 16.3 us: on_device(): carry_states.append(lax.ppermute(carry_states[-1], 'seq', back))]
    ppermute x4 -> x12, waiting for transfers between devices: 10.6 us -> 23.9 us  [the longest x3 12.9 us: on_device(): carry_seeds.append(lax.ppermute(carry_seeds[-1], 'seq', around))]
    pallas_call x3 -> x7, Pallas kernels: 16.4 us -> 20.4 us  [the longest x2 11.8 us: intra_half(): pl.pallas_call(lambda *refs: intra_kernel(first, *refs), grid=(steps,), i...]
    all_to_all x1, starting transfers between devices: 5.25 us -> 6.91 us  [total_over_devices(): lax.all_to_all(copies, 'seq', 0, 0)]
  transfers between devices with their start and end apart: 8 -> 16, of which waited for: 6 -> 10; matrix products, arithmetic and copies ran while one was open for 0% -> 0% of each run, Pallas kernels for 12% -> 16%
where the time goes in v6:
time: 151 us
  starting transfers between devices  40.3 us (27%)
  blocking collectives  37.9 us (25%)
  waiting for transfers between devices  37 us (25%)
  Pallas kernels  30.8 us (20%)
  local copies, waits for them, and re-layouts  3.99 us (3%)
    all_to_all x1, blocking collectives, on_device(): carries = lax.all_to_all(scanned, 'seq', 0, 0, axis_index_groups=remainders)  20.3 us
    all_to_all x1, blocking collectives, on_device(): recv = lax.all_to_all(send, 'seq', 0, 0, axis_index_groups=remainders)  17.5 us
    ppermute x3, starting transfers between devices, on_device(): carry_states.append(lax.ppermute(carry_states[-1], 'seq', back))  16.3 us
    ppermute x3, waiting for transfers between devices, on_device(): carry_seeds.append(lax.ppermute(carry_seeds[-1], 'seq', around))  12.9 us
    ppermute x3, starting transfers between devices, on_device(): recv_seeds.append(lax.ppermute(seed, 'seq', back))  12.7 us
    pallas_call x2, Pallas kernels, intra_half(): pl.pallas_call(lambda *refs: intra_kernel(first, *refs), grid=(steps,), i...  11.8 us
    ppermute x3, waiting for transfers between devices, on_device(): recv_states.append(lax.ppermute(state, 'seq', around))  10.9 us
    pallas_call x2, Pallas kernels, rates(): pl.pallas_call(lambda *refs: rates_kernel(places, blocks, *refs), grid_sp...  8.39 us
  transfers between devices with their start and end apart: 16, of which 10 were waited for; matrix products, arithmetic and copies ran while one was open for 0% of the time, Pallas kernels for 16%

profile of v6, /device:TPU:16, one launch (start us, length us, event | category | flops | bytes accessed | tf_op | source)
XLA Modules:
  0.0 150.9 jit_solution(10136116326416483038)
XLA Ops:
  0.7 2.7 %prepare.2 = (f32[1,528,128]{2,1,0:T(8,128)}, f32[1,528,128]{2,1,0:T(8,128)}) custom-call(s32[1]{0:T(128)} %bitcast.refs_0_.position_ref, bf16[128,2048]{1,0:T(8,128)(2,1)} %bitcast.44, f32[64,128]{1,0:T(8,128)} %bitcast.25, f32[1,64]{1,0:T(1,128)} %bitcast.40, bf16[128,512]{1,0:T(8,128)(2,1)} %bitcast.18, bf16[128,2048]{1,0:T(8,128)(2,1)} %bitcast.48, ...), custom_call_target="tpu_custom_call" | custom-call | flops 400000000 | bytes 1300000 | tf_op jit(solution)/shard_map/prepare/pallas_call | solution.py:304
  3.4 1.9 %collective-permute-start = (f32[1,528,128]{2,1,0:T(8,128)}, f32[1,528,128]{2,1,0:T(8,128)S(1)}, u32[]{:S(2)}, u32[]{:S(2)}) collective-permute-start(f32[1,528,128]{2,1,0:T(8,128)} %get-tuple-element.47), channel_id=1, source_target_pairs={{0,8},{8,16},{16,24},{24,32},{32,40},{40,48},{48,56},{56,64},{64,7... | collective-permute-start | bytes 811016 | tf_op jit(solution)/shard_map/ppermute | solution.py:349
  5.3 6.2 %collective-permute-start.1 = (f32[1,528,128]{2,1,0:T(8,128)}, f32[1,528,128]{2,1,0:T(8,128)S(1)}, u32[]{:S(2)}, u32[]{:S(2)}) collective-permute-start(f32[1,528,128]{2,1,0:T(8,128)} %get-tuple-element.49), channel_id=1, source_target_pairs={{8,0},{16,8},{24,16},{32,24},{40,32},{48,40},{56,48},{64,56},{72,6... | collective-permute-start | bytes 811016 | tf_op jit(solution)/shard_map/ppermute | solution.py:350
  11.6 2.9 %prepare.3 = (f32[3,528,128]{2,1,0:T(8,128)S(1)}, f32[3,528,128]{2,1,0:T(8,128)S(1)}, f32[4,16,128]{2,1,0:T(8,128)S(1)}) custom-call(s32[1]{0:T(128)} %bitcast.refs_0_.position_ref, bf16[128,2048]{1,0:T(8,128)(2,1)S(1)} %bitcast.47, f32[64,128]{1,0:T(8,128)S(1)} %bitcast.32, f32[1,64]{1,0:T(1,128)S(1)} %bitcast.43, bf16[128,512]{1,0:T(8,128)(2,1)S(1)} %bitcast.24, ...), custom_call_target="tpu_custom_call" | custom-call | flops 1200000000 | bytes 3900000 | tf_op jit(solution)/shard_map/prepare/pallas_call | solution.py:304
  14.5 3.6 %collective-permute-done.refs_1_.refs_2_ = f32[1,528,128]{2,1,0:T(8,128)S(1)} collective-permute-done((f32[1,528,128]{2,1,0:T(8,128)}, f32[1,528,128]{2,1,0:T(8,128)S(1)}, u32[]{:S(2)}, u32[]{:S(2)}) %collective-permute-start) | collective-permute-done | bytes 270368 | tf_op jit(solution)/shard_map/ppermute | solution.py:349
  18.2 0.6 copy-done
  18.9 5.1 %collective-permute-start.3 = (f32[1,528,128]{2,1,0:T(8,128)S(1)}, f32[1,528,128]{2,1,0:T(8,128)S(1)}, u32[]{:S(2)}, u32[]{:S(2)}) collective-permute-start(f32[1,528,128]{2,1,0:T(8,128)S(1)} %get-tuple-element.52), channel_id=1, source_target_pairs={{8,0},{16,8},{24,16},{32,24},{40,32},{48,40},{56,48},{64,56},{72,6... | collective-permute-start | bytes 811016 | tf_op jit(solution)/shard_map/ppermute | solution.py:350
  24.5 5.9 %intra.2 = (bf16[2048,128]{1,0:T(8,128)(2,1)}, bf16[2048,128]{1,0:T(8,128)(2,1)}, f32[2048,128]{1,0:T(8,128)}, f32[128,512]{1,0:T(8,128)}, f32[128,512]{1,0:T(8,...) custom-call(bf16[128,2048]{1,0:T(8,128)(2,1)} %bitcast.45, bf16[128,2048]{1,0:T(8,128)(2,1)} %bitcast.49, ...), custom_call_target="tpu_custom_call" | custom-call | flops 2000000000 | bytes 2500000 | tf_op jit(solution)/shard_map/intra/pallas_call | solution.py:330
  30.4 4.0 %collective-permute-done.2.refs_1_.refs_6_ = f32[1,528,128]{2,1,0:T(8,128)S(1)} collective-permute-done((f32[1,528,128]{2,1,0:T(8,128)S(1)}, f32[1,528,128]{2,1,0:T(8,128)S(1)}, u32[]{:S(2)}, u32[]{:S(2)}) %collective-permute-start.2) | collective-permute-done | bytes 270368 | tf_op jit(solution)/shard_map/ppermute | solution.py:349
  34.5 0.6 copy-done.6
  35.1 1.5 collective-permute-start.5
  37.1 5.9 %intra.3 = (bf16[2048,128]{1,0:T(8,128)(2,1)}, bf16[2048,128]{1,0:T(8,128)(2,1)}, f32[2048,128]{1,0:T(8,128)}, f32[128,512]{1,0:T(8,128)}, f32[128,512]{1,0:T(8,...) custom-call(bf16[128,2048]{1,0:T(8,128)(2,1)} %bitcast.46, ...), custom_call_target="tpu_custom_call", output_to_operand_aliasing={{0}: (7, {}), {1}: (8, {}), {2}: (9, {}), {3}: (10, {}), {4... | custom-call | flops 2000000000 | bytes 2500000 | tf_op jit(solution)/shard_map/intra/pallas_call | solution.py:330
  43.1 3.3 %collective-permute-done.4.refs_1_.refs_6_ = f32[1,528,128]{2,1,0:T(8,128)S(1)} collective-permute-done((f32[1,528,128]{2,1,0:T(8,128)S(1)}, f32[1,528,128]{2,1,0:T(8,128)S(1)}, u32[]{:S(2)}, u32[]{:S(2)}) %collective-permute-start.4) | collective-permute-done | bytes 270368 | tf_op jit(solution)/shard_map/ppermute | solution.py:349
  46.5 0.6 copy-done.3
  47.1 17.5 %all_to_all.15.recv_ref = f32[8,136,128]{2,1,0:T(8,128)S(1)} all-to-all(f32[8,136,128]{2,1,0:T(8,128)S(1)} %combine.1), channel_id=1, replica_groups={{0,32,64,96,128,160,192,224},{8,40,72,104,136,168,200,232},{16,48,80,11..., dimensions={0} | all-to-all | bytes 1114112 | tf_op jit(solution)/shard_map/all_to_all | solution.py:377
  64.7 20.3 %all_to_all.16 = f32[8,128,128]{2,1,0:T(8,128)S(1)} all-to-all(f32[8,128,128]{2,1,0:T(8,128)S(1)} %scan.1), channel_id=1, replica_groups={{0,32,64,96,128,160,192,224},{8,40,72,104,136,168,200,232},{16,48,80,11..., dimensions={0} | all-to-all | bytes 1048576 | tf_op jit(solution)/shard_map/all_to_all | solution.py:391
  85.2 5.3 %collective-permute-start.6 = (f32[8,64,128]{2,1,0:T(8,128)S(1)}, f32[8,64,128]{2,1,0:T(8,128)S(1)}, u32[]{:S(2)}, u32[]{:S(2)}) collective-permute-start(f32[8,64,128]{2,1,0:T(8,128)S(1)} %get-tuple-element.89.refs_5_), channel_id=1, source_target_pairs={{8,0},{16,8},{24,16},{32,24},{40,32},{48,40},{56,48},{64,56},{72,6... | collective-permute-start | bytes 786440 | tf_op jit(solution)/shard_map/ppermute | solution.py:394
  90.5 6.3 %collective-permute-done.9.refs_3_ = f32[8,64,128]{2,1,0:T(8,128)S(1)} collective-permute-done((f32[8,64,128]{2,1,0:T(8,128)S(1)}, f32[8,64,128]{2,1,0:T(8,128)S(1)}, u32[]{:S(2)}, u32[]{:S(2)}) %collective-permute-start.9) | collective-permute-done | bytes 262176 | tf_op jit(solution)/shard_map/ppermute | solution.py:395
  96.8 5.7 %collective-permute-start.7 = (f32[8,64,128]{2,1,0:T(8,128)S(1)}, f32[8,64,128]{2,1,0:T(8,128)S(1)}, u32[]{:S(2)}, u32[]{:S(2)}) collective-permute-start(f32[8,64,128]{2,1,0:T(8,128)S(1)} %collective-permute-done.6.refs_5_), channel_id=1, source_target_pairs={{8,0},{16,8},{24,16},{32,24},{40,32},{48,40},{56,48},{64,56},{72,6... | collective-permute-start | bytes 786440 | tf_op jit(solution)/shard_map/ppermute | solution.py:394
  102.5 6.5 %collective-permute-done.10.refs_7_ = f32[8,64,128]{2,1,0:T(8,128)S(1)} collective-permute-done((f32[8,64,128]{2,1,0:T(8,128)S(1)}, f32[8,64,128]{2,1,0:T(8,128)S(1)}, u32[]{:S(2)}, u32[]{:S(2)}) %collective-permute-start.10) | collective-permute-done | bytes 262176 | tf_op jit(solution)/shard_map/ppermute | solution.py:395
  109.1 5.3 %collective-permute-start.8 = (f32[8,64,128]{2,1,0:T(8,128)S(1)}, f32[8,64,128]{2,1,0:T(8,128)S(1)}, u32[]{:S(2)}, u32[]{:S(2)}) collective-permute-start(f32[8,64,128]{2,1,0:T(8,128)S(1)} %collective-permute-done.7.refs_1_), channel_id=1, source_target_pairs={{8,0},{16,8},{24,16},{32,24},{40,32},{48,40},{56,48},{64,56},{72,6... | collective-permute-start | bytes 786440 | tf_op jit(solution)/shard_map/ppermute | solution.py:394
  114.4 4.2 %rates.2 = (f32[64,128]{1,0:T(8,128)}, bf16[2048,128]{1,0:T(8,128)(2,1)}, bf16[2048,128]{1,0:T(8,128)(2,1)}, f32[1,128]{1,0:T(1,128)}) custom-call(s32[1]{0:T(128)} %bitcast.refs_0_.position_ref, f32[8,64,128]{2,1,0:T(8,128)} %copy-done.21, f32[1,528,128]{2,1,0:T(8,128)} %copy-done, f32[8,64,128]{2,1,0:T(8,128)} %copy-done.18, f32[1,528,128]{2,1,0:T(8,128)} %copy-done.5, ...), custom_call_target="tpu_custom_call" | custom-call | flops 1000000000 | bytes 3000000 | tf_op jit(solution)/shard_map/rates/pallas_call | solution.py:413
  118.8 0.7 copy-done.16
  119.6 4.2 %rates.3 = (f32[64,128]{1,0:T(8,128)}, bf16[2048,128]{1,0:T(8,128)(2,1)}, bf16[2048,128]{1,0:T(8,128)(2,1)}, f32[32,1,128]{2,1,0:T(1,128)}) custom-call(s32[1]{0:T(128)} %bitcast.refs_0_.position_ref, f32[8,64,128]{2,1,0:T(8,128)} %copy-done.17, f32[1,528,128]{2,1,0:T(8,128)} %copy-done, ...), custom_call_target="tpu_custom_call", output_to_operand_aliasing={{0}: (19, {}), {1}: (20, {}), {2}: (21, {})} | custom-call | flops 1000000000 | bytes 3000000 | tf_op jit(solution)/shard_map/rates/pallas_call | solution.py:413
  123.7 6.9 %all-to-all-start.2 = ((f32[32,1,128]{2,1,0:T(1,128)}), f32[32,1,128]{2,1,0:T(1,128)S(1)}, u32[]{:S(2)}, u32[]{:S(2)}) async-start(f32[32,1,128]{2,1,0:T(1,128)} %get-tuple-element.86), calls=%async_computation.2 | async-start | bytes 32768 | tf_op jit(solution)/shard_map/all_to_all | solution.py:251
  130.7 4.7 %finish.1 = (bf16[128,2048]{1,0:T(8,128)(2,1)}, bf16[128,512]{1,0:T(8,128)(2,1)}, bf16[128,512]{1,0:T(8,128)(2,1)}) custom-call(bf16[2048,128]{1,0:T(8,128)(2,1)} %get-tuple-element.77.state_low_ref, bf16[2048,128]{1,0:T(8,128)(2,1)} %get-tuple-element.78.adjoint_low_ref, bf16[2048,128]{1,0:T(8,128)(2,1)} %get-tuple-element.68.refs_9_.xt_ref, ...), custom_call_target="tpu_custom_call" | custom-call | flops 1000000000 | bytes 5000000 | tf_op jit(solution)/shard_map/finish/pallas_call | solution.py:436
  135.4 5.0 %all-to-all-done.2 = f32[32,1,128]{2,1,0:T(1,128)S(1)} async-done(((f32[32,1,128]{2,1,0:T(1,128)}), f32[32,1,128]{2,1,0:T(1,128)S(1)}, u32[]{:S(2)}, u32[]{:S(2)}) %all-to-all-start.2) | async-done | bytes 16416 | tf_op jit(solution)/shard_map/all_to_all | solution.py:251
  140.6 1.1 collective-permute-done.12
  141.7 1.3 collective-permute-start.13
  143.0 2.3 %collective-permute-done.13 = f32[1,128]{1,0:T(1,128)S(1)} collective-permute-done((f32[1,128]{1,0:T(1,128)S(1)}, f32[1,128]{1,0:T(1,128)S(1)}, u32[]{:S(2)}, u32[]{:S(2)}) %collective-permute-start.13) | collective-permute-done | bytes 544 | tf_op jit(solution)/shard_map/ppermute | solution.py:255
  145.6 4.7 %collective-permute-done.14 = f32[1,128]{1,0:T(1,128)S(1)} collective-permute-done((f32[1,128]{1,0:T(1,128)S(1)}, f32[1,128]{1,0:T(1,128)S(1)}, u32[]{:S(2)}, u32[]{:S(2)}) %collective-permute-start.14) | collective-permute-done | bytes 544 | tf_op jit(solution)/shard_map/ppermute | solution.py:255
  150.3 0.6 slice_bitcast_fusion
  (64 shorter events, 2.3 us)
Async XLA Ops:
  0.6 10.9 %copy-start.4 = (bf16[1,128,512]{2,1,0:T(8,128)(2,1)S(1)}, bf16[1,128,512]{2,1,0:T(8,128)(2,1)}, u32[]{:S(2)}) copy-start(bf16[1,128,512]{2,1,0:T(8,128)(2,1)} %param.13) | copy-start | bytes 393220
  0.6 10.9 %copy-start.7 = (f32[1,64,128]{2,1,0:T(8,128)S(1)}, f32[1,64,128]{2,1,0:T(8,128)}, u32[]{:S(2)}) copy-start(f32[1,64,128]{2,1,0:T(8,128)} %param.9) | copy-start | bytes 98308
  0.7 10.9 %copy-start.9 = (bf16[1,128,512]{2,1,0:T(8,128)(2,1)S(1)}, bf16[1,128,512]{2,1,0:T(8,128)(2,1)}, u32[]{:S(2)}) copy-start(bf16[1,128,512]{2,1,0:T(8,128)(2,1)} %param.14) | copy-start | bytes 393220
  0.7 10.9 %copy-start.11 = (bf16[1,128,2048]{2,1,0:T(8,128)(2,1)S(1)}, bf16[1,128,2048]{2,1,0:T(8,128)(2,1)}, u32[]{:S(2)}) copy-start(bf16[1,128,2048]{2,1,0:T(8,128)(2,1)} %param.8) | copy-start | bytes 1572868
  0.7 10.9 %copy-start.12 = (bf16[1,128,2048]{2,1,0:T(8,128)(2,1)S(1)}, bf16[1,128,2048]{2,1,0:T(8,128)(2,1)}, u32[]{:S(2)}) copy-start(bf16[1,128,2048]{2,1,0:T(8,128)(2,1)} %param.15) | copy-start | bytes 1572868
  3.4 8.2 %copy-start.10 = (f32[64]{0:T(128)S(1)}, f32[64]{0:T(128)}, u32[]{:S(2)}) copy-start(f32[64]{0:T(128)} %param.11) | copy-start | bytes 772
  3.4 8.2 %copy-start.13 = (f32[1,128]{1,0:T(1,128)S(1)}, f32[1,128]{1,0:T(1,128)}, u32[]{:S(2)}) copy-start(f32[1,128]{1,0:T(1,128)} %refs_7_.3) | copy-start | bytes 1540
  3.4 14.7 %collective-permute-start = (f32[1,528,128]{2,1,0:T(8,128)}, f32[1,528,128]{2,1,0:T(8,128)S(1)}, u32[]{:S(2)}, u32[]{:S(2)}) collective-permute-start(f32[1,528,128]{2,1,0:T(8,128)} %get-tuple-element.47), channel_id=1, source_target_pairs={{0,8},{8,16},{16,24},{24,32},{32,40},{40,48},{48,56},{56,64},{64,7... | collective-permute-start | bytes 811016 | tf_op jit(solution)/shard_map/ppermute | solution.py:349
  5.3 12.8 %collective-permute-start.1 = (f32[1,528,128]{2,1,0:T(8,128)}, f32[1,528,128]{2,1,0:T(8,128)S(1)}, u32[]{:S(2)}, u32[]{:S(2)}) collective-permute-start(f32[1,528,128]{2,1,0:T(8,128)} %get-tuple-element.49), channel_id=1, source_target_pairs={{8,0},{16,8},{24,16},{32,24},{40,32},{48,40},{56,48},{64,56},{72,6... | collective-permute-start | bytes 811016 | tf_op jit(solution)/shard_map/ppermute | solution.py:350
  14.5 3.7 %copy-start.8 = (f32[4,16,128]{2,1,0:T(8,128)}, f32[4,16,128]{2,1,0:T(8,128)S(1)}, u32[]{:S(2)}) copy-start(f32[4,16,128]{2,1,0:T(8,128)S(1)} %get-tuple-element.53.refs_3_.refs_12_.cum_ref) | copy-start | bytes 98308
  18.9 11.5 %collective-permute-start.3 = (f32[1,528,128]{2,1,0:T(8,128)S(1)}, f32[1,528,128]{2,1,0:T(8,128)S(1)}, u32[]{:S(2)}, u32[]{:S(2)}) collective-permute-start(f32[1,528,128]{2,1,0:T(8,128)S(1)} %get-tuple-element.52), channel_id=1, source_target_pairs={{8,0},{16,8},{24,16},{32,24},{40,32},{48,40},{56,48},{64,56},{72,6... | collective-permute-start | bytes 811016 | tf_op jit(solution)/shard_map/ppermute | solution.py:350
  24.0 10.4 %collective-permute-start.2 = (f32[1,528,128]{2,1,0:T(8,128)S(1)}, f32[1,528,128]{2,1,0:T(8,128)S(1)}, u32[]{:S(2)}, u32[]{:S(2)}) collective-permute-start(f32[1,528,128]{2,1,0:T(8,128)S(1)} %get-tuple-element.51), channel_id=1, source_target_pairs={{0,8},{8,16},{16,24},{24,32},{32,40},{40,48},{48,56},{56,64},{64,7... | collective-permute-start | bytes 811016 | tf_op jit(solution)/shard_map/ppermute | solution.py:349
  30.4 4.0 %copy-start.5 = (f32[1,528,128]{2,1,0:T(8,128)}, f32[1,528,128]{2,1,0:T(8,128)S(1)}, u32[]{:S(2)}) copy-start(f32[1,528,128]{2,1,0:T(8,128)S(1)} %collective-permute-done.3.refs_3_.refs_4_) | copy-start | bytes 811012
  35.1 7.9 %collective-permute-start.5 = (f32[1,528,128]{2,1,0:T(8,128)S(1)}, f32[1,528,128]{2,1,0:T(8,128)S(1)}, u32[]{:S(2)}, u32[]{:S(2)}) collective-permute-start(f32[1,528,128]{2,1,0:T(8,128)S(1)} %get-tuple-element.57), channel_id=1, source_target_pairs={{8,0},{16,8},{24,16},{32,24},{40,32},{48,40},{56,48},{64,56},{72,6... | collective-permute-start | bytes 811016 | tf_op jit(solution)/shard_map/ppermute | solution.py:350
  36.6 9.8 %collective-permute-start.4 = (f32[1,528,128]{2,1,0:T(8,128)S(1)}, f32[1,528,128]{2,1,0:T(8,128)S(1)}, u32[]{:S(2)}, u32[]{:S(2)}) collective-permute-start(f32[1,528,128]{2,1,0:T(8,128)S(1)} %get-tuple-element.56), channel_id=1, source_target_pairs={{0,8},{8,16},{16,24},{24,32},{32,40},{40,48},{48,56},{56,64},{64,7... | collective-permute-start | bytes 811016 | tf_op jit(solution)/shard_map/ppermute | solution.py:349
  43.1 3.4 %copy-start.2 = (f32[1,528,128]{2,1,0:T(8,128)}, f32[1,528,128]{2,1,0:T(8,128)S(1)}, u32[]{:S(2)}) copy-start(f32[1,528,128]{2,1,0:T(8,128)S(1)} %collective-permute-done.5.refs_3_.refs_4_) | copy-start | bytes 811012
  85.1 33.5 %copy-start.14 = (f32[8,64,128]{2,1,0:T(8,128)}, f32[8,64,128]{2,1,0:T(8,128)S(1)}, u32[]{:S(2)}) copy-start(f32[8,64,128]{2,1,0:T(8,128)S(1)} %get-tuple-element.88.refs_3_) | copy-start | bytes 786436
  85.1 33.5 %copy-start.15 = (f32[8,64,128]{2,1,0:T(8,128)}, f32[8,64,128]{2,1,0:T(8,128)S(1)}, u32[]{:S(2)}) copy-start(f32[8,64,128]{2,1,0:T(8,128)S(1)} %get-tuple-element.89.refs_5_) | copy-start | bytes 786436
  85.1 11.7 %collective-permute-start.9 = (f32[8,64,128]{2,1,0:T(8,128)S(1)}, f32[8,64,128]{2,1,0:T(8,128)S(1)}, u32[]{:S(2)}, u32[]{:S(2)}) collective-permute-start(f32[8,64,128]{2,1,0:T(8,128)S(1)} %get-tuple-element.88.refs_3_), channel_id=1, source_target_pairs={{0,8},{8,16},{16,24},{24,32},{32,40},{40,48},{48,56},{56,64},{64,7... | collective-permute-start | bytes 786440 | tf_op jit(solution)/shard_map/ppermute | solution.py:395
  85.2 11.6 %collective-permute-start.6 = (f32[8,64,128]{2,1,0:T(8,128)S(1)}, f32[8,64,128]{2,1,0:T(8,128)S(1)}, u32[]{:S(2)}, u32[]{:S(2)}) collective-permute-start(f32[8,64,128]{2,1,0:T(8,128)S(1)} %get-tuple-element.89.refs_5_), channel_id=1, source_target_pairs={{8,0},{16,8},{24,16},{32,24},{40,32},{48,40},{56,48},{64,56},{72,6... | collective-permute-start | bytes 786440 | tf_op jit(solution)/shard_map/ppermute | solution.py:394
  96.8 17.6 %copy-start.18 = (f32[8,64,128]{2,1,0:T(8,128)}, f32[8,64,128]{2,1,0:T(8,128)S(1)}, u32[]{:S(2)}) copy-start(f32[8,64,128]{2,1,0:T(8,128)S(1)} %collective-permute-done.9.refs_3_) | copy-start | bytes 786436
  96.8 12.2 %collective-permute-start.10 = (f32[8,64,128]{2,1,0:T(8,128)S(1)}, f32[8,64,128]{2,1,0:T(8,128)S(1)}, u32[]{:S(2)}, u32[]{:S(2)}) collective-permute-start(f32[8,64,128]{2,1,0:T(8,128)S(1)} %collective-permute-done.9.refs_3_), channel_id=1, source_target_pairs={{0,8},{8,16},{16,24},{24,32},{32,40},{40,48},{48,56},{56,64},{64,7... | collective-permute-start | bytes 786440 | tf_op jit(solution)/shard_map/ppermute | solution.py:395
  96.8 17.6 %copy-start.19 = (f32[8,64,128]{2,1,0:T(8,128)}, f32[8,64,128]{2,1,0:T(8,128)S(1)}, u32[]{:S(2)}) copy-start(f32[8,64,128]{2,1,0:T(8,128)S(1)} %collective-permute-done.6.refs_5_) | copy-start | bytes 786436
  96.8 12.2 %collective-permute-start.7 = (f32[8,64,128]{2,1,0:T(8,128)S(1)}, f32[8,64,128]{2,1,0:T(8,128)S(1)}, u32[]{:S(2)}, u32[]{:S(2)}) collective-permute-start(f32[8,64,128]{2,1,0:T(8,128)S(1)} %collective-permute-done.6.refs_5_), channel_id=1, source_target_pairs={{8,0},{16,8},{24,16},{32,24},{40,32},{48,40},{56,48},{64,56},{72,6... | collective-permute-start | bytes 786440 | tf_op jit(solution)/shard_map/ppermute | solution.py:394
  109.0 5.4 %copy-start.20 = (f32[8,64,128]{2,1,0:T(8,128)}, f32[8,64,128]{2,1,0:T(8,128)S(1)}, u32[]{:S(2)}) copy-start(f32[8,64,128]{2,1,0:T(8,128)S(1)} %collective-permute-done.10.refs_7_) | copy-start | bytes 786436
  109.1 9.7 %collective-permute-start.11 = (f32[8,64,128]{2,1,0:T(8,128)S(1)}, f32[8,64,128]{2,1,0:T(8,128)S(1)}, u32[]{:S(2)}, u32[]{:S(2)}) collective-permute-start(f32[8,64,128]{2,1,0:T(8,128)S(1)} %collective-permute-done.10.refs_7_), channel_id=1, source_target_pairs={{0,8},{8,16},{16,24},{24,32},{32,40},{40,48},{48,56},{56,64},{64,7... | collective-permute-start | bytes 786440 | tf_op jit(solution)/shard_map/ppermute | solution.py:395
  109.1 5.4 %copy-start.21 = (f32[8,64,128]{2,1,0:T(8,128)}, f32[8,64,128]{2,1,0:T(8,128)S(1)}, u32[]{:S(2)}) copy-start(f32[8,64,128]{2,1,0:T(8,128)S(1)} %collective-permute-done.7.refs_1_) | copy-start | bytes 786436
  109.1 9.7 %collective-permute-start.8 = (f32[8,64,128]{2,1,0:T(8,128)S(1)}, f32[8,64,128]{2,1,0:T(8,128)S(1)}, u32[]{:S(2)}, u32[]{:S(2)}) collective-permute-start(f32[8,64,128]{2,1,0:T(8,128)S(1)} %collective-permute-done.7.refs_1_), channel_id=1, source_target_pairs={{8,0},{16,8},{24,16},{32,24},{40,32},{48,40},{56,48},{64,56},{72,6... | collective-permute-start | bytes 786440 | tf_op jit(solution)/shard_map/ppermute | solution.py:394
  123.7 16.7 %all-to-all-start.2 = ((f32[32,1,128]{2,1,0:T(1,128)}), f32[32,1,128]{2,1,0:T(1,128)S(1)}, u32[]{:S(2)}, u32[]{:S(2)}) async-start(f32[32,1,128]{2,1,0:T(1,128)} %get-tuple-element.86), calls=%async_computation.2 | async-start | bytes 32768 | tf_op jit(solution)/shard_map/all_to_all | solution.py:251
  140.5 1.2 collective-permute-start.12
  141.7 3.5 %collective-permute-start.13 = (f32[1,128]{1,0:T(1,128)S(1)}, f32[1,128]{1,0:T(1,128)S(1)}, u32[]{:S(2)}, u32[]{:S(2)}) collective-permute-start(f32[1,128]{1,0:T(1,128)S(1)} %bitcast_add_fusion), channel_id=1, source_target_pairs={{0,2},{1,3},{2,0},{3,1},{4,6},{5,7},{6,4},{7,5},{8,10},{9,11},{10,... | collective-permute-start | bytes 1544 | tf_op jit(solution)/shard_map/ppermute | solution.py:255
  145.2 5.0 %collective-permute-start.14 = (f32[1,128]{1,0:T(1,128)S(1)}, f32[1,128]{1,0:T(1,128)S(1)}, u32[]{:S(2)}, u32[]{:S(2)}) collective-permute-start(f32[1,128]{1,0:T(1,128)S(1)} %add.10), channel_id=1, source_target_pairs={{0,4},{1,5},{2,6},{3,7},{4,0},{5,1},{6,2},{7,3},{8,12},{9,13},{10,... | collective-permute-start | bytes 1544 | tf_op jit(solution)/shard_map/ppermute | solution.py:255
  (6 other events, 4.4 us)

commit v7 on v5

--- a/solution.py
+++ b/solution.py
@@ -129,8 +129,24 @@
     out_ref[pairs - 1, half:, :] = jnp.where(parity == 1, adjoint, 0.0)
 
 
-def intra_kernel(x_ref, dy_ref, step_ref, cum_ref, key_ref, query_ref,
-                 xt_ref, dyt_ref, intra_ref, dq_ref, dk_ref, flow_ref, own_ref, skip_ref):
+def moments_kernel(x_ref, dy_ref, step_ref, cum_ref, rate_ref, key_ref, query_ref, state_ref, adjoint_ref, cross_ref):
+    length = x_ref.shape[0]
+    cum, step, rate = cum_ref[0, 0], step_ref[...], column_of_group(rate_ref, pl.program_id(0))
+    passed = jnp.dot(step, triangle(length, True).astype(f32), precision=highest)
+    last, steps_all = cum[:, length - 1:], passed[:, length - 1:]
+    sides = ((dy_ref, passed * jnp.exp(cum), query_ref, state_ref),
+             (x_ref, (steps_all - passed) * step * jnp.exp(last - cum), key_ref, adjoint_ref))
+    scale = per_feature(jnp.broadcast_to(-rate, (K, N)))
+    for features_ref, weight, rows_ref, out_ref in sides:
+        weighted = features_ref[...].astype(f32).T * per_feature(weight)
+        high = weighted.astype(bf16)
+        low = (weighted - high.astype(f32)).astype(bf16)
+        out_ref[...] = scale * (contract(high, rows_ref[...], (1, 0)) + contract(low, rows_ref[...], (1, 0)))
+    cross_ref[...] = jnp.broadcast_to(-rate * steps_all * jnp.exp(last), (K, N))
+
+
+def intra_kernel(first, x_ref, dy_ref, step_ref, cum_ref, rate_ref, key_ref, query_ref, sums_in_ref, *refs):
+    xt_ref, dyt_ref, intra_ref, dq_ref, dk_ref, flow_ref, own_ref, sums_ref = refs[-8:]
     length = dy_ref.shape[0]
     x_full = x_ref[...].astype(f32).T
     dy_full = dy_ref[...].astype(f32).T
@@ -167,21 +183,24 @@
     shared_low = shared.astype(bf16)
     dq_ref[...] = contract(shared_low, keys, (1, 0))
     dk_ref[...] = contract(shared_low, queries, (0, 0))
-    flow_ref[...] = jnp.concatenate(row_sums, axis=1).T - jnp.concatenate(col_sums, axis=0)
+    flow = jnp.concatenate(row_sums, axis=1).T - jnp.concatenate(col_sums, axis=0)
+    flow_ref[...] = flow
     own_ref[...] = head_sum(x_full * intra_ref[...])
     skip_part = jnp.sum(head_sum(x_full * dy_full), axis=1, keepdims=True)
-    accumulate(skip_ref, jnp.zeros(skip_ref.shape, f32), row_of_group(skip_part, pl.program_id(0), H))
+    group = first + pl.program_id(0)
+    passed = jnp.dot(step, triangle(length, True).astype(f32), precision=highest)
+    rate_part = -column_of_group(rate_ref, group) * jnp.sum(passed * flow, axis=1, keepdims=True)
+    parts = row_of_group(skip_part, group, H) + row_of_group(rate_part, group, 0)
+    accumulate(sums_ref, sums_in_ref[...], parts)
 
 
 def rates_kernel(position_ref, carry_ref, state_in_ref, adjoint_in_ref, recv_state_ref, recv_seed_ref,
-                 xt_ref, dyt_ref, step_ref, cum_ref, rate_ref, key_ref, query_ref,
-                 flow_ref, own_ref, sums_in_ref,
-                 dstep_ref, sums_ref, state_low_ref, adjoint_low_ref,
+                 state_moment_ref, adjoint_moment_ref, cross_weight_ref, sums_in_ref,
+                 cross_ref, sums_ref, state_low_ref, adjoint_low_ref,
                  state_scratch, adjoint_scratch, sums_scratch, *, blocks):
     grid_step = pl.program_id(0)
     position = position_ref[0]
     group = group_of(grid_step, position)
-    length = step_ref.shape[1]
 
     def advanced(recv_ref, carry, inside):
         moved = per_feature(recv_ref[0, GP:, :]) * carry.reshape(GP, N) + recv_ref[0, :GP, :]
@@ -201,41 +220,42 @@
     state_low, adjoint_low = state.astype(bf16), adjoint.astype(bf16)
     state_low_ref[...] = state_low
     adjoint_low_ref[...] = adjoint_low
+    cross = head_sum(adjoint * state)
+    cross_ref[...] = cross
+    products = state_low.astype(f32) * state_moment_ref[...] + adjoint_low.astype(f32) * adjoint_moment_ref[...]
+    rate_part = jnp.sum(head_sum(products) + cross_weight_ref[...] * cross, axis=1, keepdims=True)
+    accumulate(sums_scratch, sums_in_ref[...], row_of_group(rate_part, group, 0))
+
+    @pl.when(grid_step == G - 1)
+    def _():
+        sums_ref[...] = jnp.broadcast_to(sums_scratch[...][None], sums_ref.shape)
+
+
+def finish_kernel(state_low_ref, adjoint_low_ref, cross_ref, xt_ref, dyt_ref, step_ref, cum_ref, rate_ref, skip_ref,
+                  key_ref, query_ref, intra_ref, dq_in_ref, dk_in_ref, flow_ref, own_ref,
+                  dx_ref, dk_ref, dq_ref, dstep_ref):
+    group = pl.program_id(0)
+    length = step_ref.shape[1]
+    cum, step, rate = cum_ref[0, 0], step_ref[...], column_of_group(rate_ref, group)
+    last = cum[:, length - 1:]
+    growth, tail = jnp.exp(cum), jnp.exp(last - cum)
+    exit_weight = step * tail
+    x_t, dy_t = xt_ref[...].astype(f32), dyt_ref[...].astype(f32)
+    state_low, adjoint_low = state_low_ref[...], adjoint_low_ref[...]
+    weighted_grads = (dy_t * per_feature(growth)).astype(bf16)
+    weighted_inputs = (x_t * per_feature(exit_weight)).astype(bf16)
+    dq_ref[...] = (dq_in_ref[...] + contract(weighted_grads, state_low, (0, 0))).astype(bf16)
+    dk_ref[...] = (dk_in_ref[...] + contract(weighted_inputs, adjoint_low, (0, 0))).astype(bf16)
     state_term = contract(adjoint_low, key_ref[...], (1, 1))
     carried = contract(state_low, query_ref[...], (1, 1))
-    cum, step, rate = cum_ref[0, 0], step_ref[...], column_of_group(rate_ref, group)
-    last = cum[:, length - 1:]
-    tail = jnp.exp(last - cum)
-    entry_term = jnp.exp(cum) * head_sum(dyt_ref[...].astype(f32) * carried)
-    outside = tail * head_sum(xt_ref[...].astype(f32) * state_term)
+    entry_term = growth * head_sum(dy_t * carried)
+    outside = tail * head_sum(x_t * state_term)
     exit_term = step * outside
-    closing = jnp.exp(last) * jnp.sum(head_sum(adjoint * state), axis=1, keepdims=True) + jnp.sum(
-        exit_term, axis=1, keepdims=True)
+    closing = jnp.exp(last) * jnp.sum(cross_ref[...], axis=1, keepdims=True) + jnp.sum(exit_term, axis=1, keepdims=True)
     final_slot = lax.broadcasted_iota(jnp.int32, (K, length), 1) == length - 1
     d_cum = flow_ref[...] + entry_term - exit_term + jnp.where(final_slot, closing, 0.0)
     d_logs = jnp.dot(d_cum, triangle(length, False).astype(f32), precision=highest)
     dstep_ref[...] = own_ref[...] + outside - rate * d_logs
-    rate_part = -rate * jnp.sum(step * d_logs, axis=1, keepdims=True)
-    accumulate(sums_scratch, sums_in_ref[...], row_of_group(rate_part, group, 0))
-
-    @pl.when(grid_step == G - 1)
-    def _():
-        sums_ref[...] = jnp.broadcast_to(sums_scratch[...][None], sums_ref.shape)
-
-
-def finish_kernel(state_low_ref, adjoint_low_ref, xt_ref, dyt_ref, step_ref, cum_ref, skip_ref, key_ref,
-                  intra_ref, dq_in_ref, dk_in_ref, dx_ref, dk_ref, dq_ref):
-    group = pl.program_id(0)
-    length = step_ref.shape[1]
-    cum, step = cum_ref[0, 0], step_ref[...]
-    growth, tail = jnp.exp(cum), jnp.exp(cum[:, length - 1:] - cum)
-    x_t, dy_t = xt_ref[...].astype(f32), dyt_ref[...].astype(f32)
-    state_low, adjoint_low = state_low_ref[...], adjoint_low_ref[...]
-    weighted_grads = (dy_t * per_feature(growth)).astype(bf16)
-    weighted_inputs = (x_t * per_feature(step * tail)).astype(bf16)
-    dq_ref[...] = (dq_in_ref[...] + contract(weighted_grads, state_low, (0, 0))).astype(bf16)
-    dk_ref[...] = (dk_in_ref[...] + contract(weighted_inputs, adjoint_low, (0, 0))).astype(bf16)
-    state_term = contract(adjoint_low, key_ref[...], (1, 1))
     d_scaled = intra_ref[...] + per_feature(tail) * state_term
     skips = jnp.broadcast_to(column_of_group(skip_ref, group), (K, length))
     dx_ref[...] = (per_feature(step) * d_scaled + per_feature(skips) * dy_t).T.astype(bf16)
@@ -324,6 +344,42 @@
     recv_state = lax.ppermute(first_states, "seq", around)
     recv_seed = lax.ppermute(second_seeds, "seq", back)
     second_states, first_seeds = prepare(1)
+
+    low_rows = ((GP, N), lambda g: (g, 0))
+    state_moment, adjoint_moment, cross_weight = pl.pallas_call(
+        moments_kernel,
+        grid=(G,),
+        in_specs=[block(*tokens), block(*tokens), block(*head_rows), block(*cum_rows), per_head, block(*group_rows),
+                  block(*group_rows)],
+        out_specs=[block(*low_rows), block(*low_rows), block((K, N), lambda g: (g, 0))],
+        out_shape=[shape((H * P_SIZE, N)), shape((H * P_SIZE, N)), shape((H, N))],
+        compiler_params=params,
+        cost_estimate=pl.CostEstimate(flops=1_000_000_000, bytes_accessed=4_000_000, transcendentals=20_000),
+        name="moments",
+    )(x, dy, step, cum, rate, key_rows, query_rows)
+
+    def intra_half(first, sums, earlier):
+        def at(dims, index):
+            return block(dims, lambda s: index(first + s))
+
+        return pl.pallas_call(
+            lambda *refs: intra_kernel(first, *refs),
+            grid=(G // 2,),
+            in_specs=[at(*tokens), at(*tokens), at(*head_rows), at(*cum_rows), per_head, at(*group_rows),
+                      at(*group_rows), sums_row] + [pl.BlockSpec(memory_space=pl.ANY)] * len(earlier),
+            out_specs=[at(*features), at(*features), at(*features), at(*group_rows), at(*group_rows),
+                       at(*head_rows), at(*head_rows), sums_row],
+            out_shape=[shape((H * P_SIZE, length), bf16), shape((H * P_SIZE, length), bf16),
+                       shape((H * P_SIZE, length)), shape((length, G * N)), shape((length, G * N)),
+                       shape((H, length)), shape((H, length)), shape((1, 2 * H))],
+            input_output_aliases={8 + i: i for i in range(len(earlier))},
+            compiler_params=params,
+            cost_estimate=pl.CostEstimate(flops=2_000_000_000, bytes_accessed=2_500_000, transcendentals=500_000),
+            name="intra",
+        )(x, dy, step, cum, rate, key_rows, query_rows, sums, *earlier)
+
+    outcome = intra_half(0, jnp.zeros((1, 2 * H), f32), ())
+    recv_seed, state_moment, sums = lax.optimization_barrier((recv_seed, state_moment, outcome[-1]))
 
     slot = 2 * half + 8
     send = pl.pallas_call(
@@ -357,22 +413,10 @@
     state_in = lax.ppermute(carries[:, :half], "seq", back)
     adjoint_in = lax.ppermute(carries[:, half:], "seq", around)
 
-    x_t, dy_t, intra, dq_intra, dk_intra, flow, own, sums = pl.pallas_call(
-        intra_kernel,
-        grid=(G,),
-        in_specs=[block(*tokens), block(*tokens), block(*head_rows), block(*cum_rows), block(*group_rows),
-                  block(*group_rows)],
-        out_specs=[block(*features), block(*features), block(*features), block(*group_rows), block(*group_rows),
-                   block(*head_rows), block(*head_rows), sums_row],
-        out_shape=[shape((H * P_SIZE, length), bf16), shape((H * P_SIZE, length), bf16),
-                   shape((H * P_SIZE, length)), shape((length, G * N)), shape((length, G * N)),
-                   shape((H, length)), shape((H, length)), shape((1, 2 * H))],
-        compiler_params=params,
-        cost_estimate=pl.CostEstimate(flops=2_000_000_000, bytes_accessed=5_000_000, transcendentals=1_000_000),
-        name="intra",
-    )(x, dy, step, cum, key_rows, query_rows)
-
-    d_steps, sum_copies, state_low, adjoint_low = pl.pallas_call(
+    outcome = intra_half(G // 2, sums, tuple(outcome[:-1]))
+    x_t, dy_t, intra, dq_intra, dk_intra, flow, own, sums = outcome
+
+    cross, sum_copies, state_low, adjoint_low = pl.pallas_call(
         lambda *refs: rates_kernel(*refs, blocks=blocks),
         grid_spec=pltpu.PrefetchScalarGridSpec(
             num_scalar_prefetch=1,
@@ -381,33 +425,32 @@
                 block((owners, 2 * half, N), lambda s: (lax.rem(s, PG), 0, 0)),
                 stepped((owners, half, N), 0), stepped((owners, half, N), 1),
                 stepped((1, MSG, N), 1), stepped((1, MSG, N), 0),
-                ordered(*features), ordered(*features), ordered(*head_rows),
-                ordered((1, 1, K, length), lambda g: (lax.div(g, PG), lax.rem(g, PG), 0, 0)),
-                per_head, ordered(*group_rows), ordered(*group_rows),
-                ordered(*head_rows), ordered(*head_rows), sums_row],
-            out_specs=[ordered(*head_rows), block((blocks, 1, 2 * H), lambda s: (0, 0, 0)),
-                       ordered((GP, N), lambda g: (g, 0)), ordered((GP, N), lambda g: (g, 0))],
+                ordered(*low_rows), ordered(*low_rows), ordered((K, N), lambda g: (g, 0)), sums_row],
+            out_specs=[ordered((K, N), lambda g: (g, 0)), block((blocks, 1, 2 * H), lambda s: (0, 0, 0)),
+                       ordered(*low_rows), ordered(*low_rows)],
             scratch_shapes=[pltpu.VMEM((GP, N), f32), pltpu.VMEM((GP, N), f32), pltpu.VMEM((1, 2 * H), f32)],
         ),
-        out_shape=[shape((H, length)), shape((blocks, 1, 2 * H)), low_states, low_states],
+        out_shape=[shape((H, N)), shape((blocks, 1, 2 * H)), low_states, low_states],
         compiler_params=params,
-        cost_estimate=pl.CostEstimate(flops=140_000_000, bytes_accessed=6_000_000, transcendentals=20_000),
+        cost_estimate=pl.CostEstimate(flops=10_000_000, bytes_accessed=6_000_000, transcendentals=0),
         name="rates",
-    )(position, carries, state_in, adjoint_in, recv_state, recv_seed, x_t, dy_t, step, cum, rate,
-      key_rows, query_rows, flow, own, sums)
-
-    d_inputs, d_keys, d_queries = pl.pallas_call(
+    )(position, carries, state_in, adjoint_in, recv_state, recv_seed, state_moment, adjoint_moment, cross_weight, sums)
+
+    d_inputs, d_keys, d_queries, d_steps = pl.pallas_call(
         finish_kernel,
         grid=(G,),
-        in_specs=[block((GP, N), lambda g: (g, 0)), block((GP, N), lambda g: (g, 0)), block(*features),
-                  block(*features), block(*head_rows), block(*cum_rows), per_head, block(*group_rows),
-                  block(*features), block(*group_rows), block(*group_rows)],
-        out_specs=[block(*tokens), block(*group_rows), block(*group_rows)],
-        out_shape=[shape((length, H * P_SIZE), bf16), shape((length, G * N), bf16), shape((length, G * N), bf16)],
+        in_specs=[block(*low_rows), block(*low_rows), block((K, N), lambda g: (g, 0)), block(*features),
+                  block(*features), block(*head_rows), block(*cum_rows), per_head, per_head, block(*group_rows),
+                  block(*group_rows), block(*features), block(*group_rows), block(*group_rows), block(*head_rows),
+                  block(*head_rows)],
+        out_specs=[block(*tokens), block(*group_rows), block(*group_rows), block(*head_rows)],
+        out_shape=[shape((length, H * P_SIZE), bf16), shape((length, G * N), bf16), shape((length, G * N), bf16),
+                   shape((H, length))],
         compiler_params=params,
-        cost_estimate=pl.CostEstimate(flops=1_000_000_000, bytes_accessed=5_000_000, transcendentals=20_000),
+        cost_estimate=pl.CostEstimate(flops=1_500_000_000, bytes_accessed=5_000_000, transcendentals=20_000),
         name="finish",
-    )(state_low, adjoint_low, x_t, dy_t, step, cum, skip_row, key_rows, intra, dq_intra, dk_intra)
+    )(state_low, adjoint_low, cross, x_t, dy_t, step, cum, rate, skip_row, key_rows, query_rows, intra, dq_intra,
+      dk_intra, flow, own)
 
     totals = total_over_devices(sum_copies, d_keys)[0] / tokens_all
     return (d_inputs[None], d_steps[None], d_keys[None], d_queries[None], totals[:H], totals[H:])

time: 139 us -> 141 us (1.014)
  Pallas kernels: 27.1 us -> 32.3 us
  starting transfers between devices: 20.6 us -> 17.6 us
  blocking collectives: 64 us -> 61.1 us
  waiting for transfers between devices: 23.7 us -> 25.5 us
    pallas_call x2 -> x4, Pallas kernels: 14.7 us -> 21.2 us  [the longest x2 11.3 us: intra_half(): pl.pallas_call(lambda *refs: intra_kernel(first, *refs), grid=(G // 2,),...]
    ppermute x1, waiting for transfers between devices: 10.3 us -> 4.37 us  [on_device(): recv_state = lax.ppermute(first_states, 'seq', around)]
    ppermute x1, waiting for transfers between devices: 0.28 us -> 4.45 us  [on_device(): state_in = lax.ppermute(carries[:, :half], 'seq', back)]
    ppermute x1, waiting for transfers between devices: 0.01 us -> 4.15 us  [on_device(): adjoint_in = lax.ppermute(carries[:, half:], 'seq', around)]
    all_to_all x1, blocking collectives: 30.6 us -> 27.9 us  [on_device(): carries = lax.all_to_all(scanned, 'seq', 0, 0, axis_index_groups=parities)]
    ppermute x1, starting transfers between devices: 1.98 us -> 0.01 us  [on_device(): recv_state = lax.ppermute(first_states, 'seq', around)]
    ppermute x1, starting transfers between devices: 3.93 us -> 1.96 us  [on_device(): adjoint_in = lax.ppermute(carries[:, half:], 'seq', around)]
    ppermute x1, starting transfers between devices: 6.22 us -> 8.11 us  [on_device(): recv_seed = lax.ppermute(second_seeds, 'seq', back)]
  transfers between devices with their start and end apart: 8 -> 8, of which waited for: 6 -> 7; matrix products, arithmetic and copies ran while one was open for 0% -> 0% of each run, Pallas kernels for 12% -> 17%
where the time goes in v7:
time: 141 us; the launch traced here: 140 us
  blocking collectives  61.1 us (43%)
  Pallas kernels  32.3 us (23%)
  waiting for transfers between devices  25.5 us (18%)
  starting transfers between devices  17.6 us (12%)
  local copies, waits for them, and re-layouts  2.65 us (2%)
    all_to_all x1, blocking collectives, on_device(): recv = lax.all_to_all(send, 'seq', 0, 0, axis_index_groups=parities)  33.3 us
    all_to_all x1, blocking collectives, on_device(): carries = lax.all_to_all(scanned, 'seq', 0, 0, axis_index_groups=parities)  27.9 us
    pallas_call x2, Pallas kernels, intra_half(): pl.pallas_call(lambda *refs: intra_kernel(first, *refs), grid=(G // 2,),...  11.3 us
    ppermute x1, starting transfers between devices, on_device(): recv_seed = lax.ppermute(second_seeds, 'seq', back)  8.11 us
    ppermute x3, waiting for transfers between devices, total_over_devices(): row = row + lax.ppermute(row, 'dp', [(i, i ^ reach) for i in range(size)])  8.07 us
    pallas_call x2, Pallas kernels, prepare(): pl.pallas_call(lambda *refs: prepare_kernel(first, *refs), grid_spec=pltp...  5.85 us
    pallas_call x1, Pallas kernels, on_device(): pl.pallas_call(finish_kernel, grid=(G,), in_specs=[block(*low_rows), bloc...  5.37 us
    pallas_call x1, Pallas kernels, on_device(): pl.pallas_call(lambda *refs: rates_kernel(*refs, blocks=blocks), grid_spe...  4.94 us
  transfers between devices with their start and end apart: 8, of which 7 were waited for; matrix products, arithmetic and copies ran while one was open for 0% of the time, Pallas kernels for 17%

profile of v7, /device:TPU:16, one launch (start us, length us, event | category | flops | bytes accessed | tf_op | source)
XLA Modules:
  0.0 140.1 jit_solution(2301040494218809898)
XLA Ops:
  0.7 0.0 copy-start.3
  0.7 3.8 %prepare.2 = (f32[2,528,128]{2,1,0:T(8,128)}, f32[2,528,128]{2,1,0:T(8,128)}, f32[2,2,16,128]{3,2,1,0:T(8,128)}) custom-call(s32[1]{0:T(128)} %bitcast.refs_0_.position_ref, bf16[128,2048]{1,0:T(8,128)(2,1)} %bitcast.18, f32[64,128]{1,0:T(8,128)} %bitcast.40, f32[1,64]{1,0:T(1,128)} %bitcast.48, bf16[128,512]{1,0:T(8,128)(2,1)} %bitcast.28, ...), custom_call_target="tpu_custom_call" | custom-call | flops 500000000 | bytes 2500000 | tf_op jit(solution)/shard_map/prepare/pallas_call | solution.py:325
  4.5 8.1 %collective-permute-start.1 = (f32[2,528,128]{2,1,0:T(8,128)}, f32[2,528,128]{2,1,0:T(8,128)S(1)}, u32[]{:S(2)}, u32[]{:S(2)}) collective-permute-start(f32[2,528,128]{2,1,0:T(8,128)} %get-tuple-element.44), channel_id=1, source_target_pairs={{8,0},{16,8},{24,16},{32,24},{40,32},{48,40},{56,48},{64,56},{72,6... | collective-permute-start | bytes 1622024 | tf_op jit(solution)/shard_map/ppermute | solution.py:345
  12.7 2.1 %prepare.3 = (f32[2,528,128]{2,1,0:T(8,128)S(1)}, f32[2,528,128]{2,1,0:T(8,128)S(1)}) custom-call(s32[1]{0:T(128)} %bitcast.refs_0_.position_ref, bf16[128,2048]{1,0:T(8,128)(2,1)S(1)} %bitcast.22, f32[64,128]{1,0:T(8,128)S(1)} %bitcast.46, f32[1,64]{1,0:T(1,128)S(1)} %bitcast.53, bf16[128,512]{1,0:T(8,128)(2,1)S(1)} %bitcast.33, ...), custom_call_target="tpu_custom_call" | custom-call | flops 500000000 | bytes 2500000 | tf_op jit(solution)/shard_map/prepare/pallas_call | solution.py:325
  14.8 4.6 %moments.1 = (f32[2048,128]{1,0:T(8,128)}, f32[2048,128]{1,0:T(8,128)}, f32[64,128]{1,0:T(8,128)}) custom-call(bf16[128,2048]{1,0:T(8,128)(2,1)} %bitcast.19, bf16[128,2048]{1,0:T(8,128)(2,1)} %bitcast.24, f32[64,128]{1,0:T(8,128)} %bitcast.42, f32[2,2,16,128]{3,2,1,0:T(8,128)} %get-tuple-element.45.cum_ref.refs_3_, f32[1,64]{1,0:T(1,128)} %bitcast.49, ...), custom_call_target="tpu_custom_call" | custom-call | flops 1000000000 | bytes 4000000 | tf_op jit(solution)/shard_map/moments/pallas_call | solution.py:349
  19.4 0.5 broadcast_in_dim.15.refs_7_
  19.9 5.6 %intra.2 = (bf16[2048,128]{1,0:T(8,128)(2,1)}, bf16[2048,128]{1,0:T(8,128)(2,1)}, f32[2048,128]{1,0:T(8,128)}, f32[128,512]{1,0:T(8,128)}, f32[128,512]{1,0:T(8,...) custom-call(bf16[128,2048]{1,0:T(8,128)(2,1)} %bitcast.20, bf16[128,2048]{1,0:T(8,128)(2,1)} %bitcast.25, ...), custom_call_target="tpu_custom_call" | custom-call | flops 2000000000 | bytes 2500000 | tf_op jit(solution)/shard_map/intra/pallas_call | solution.py:365
  25.5 4.4 %collective-permute-done.refs_1_.refs_4_ = f32[2,528,128]{2,1,0:T(8,128)S(1)} collective-permute-done((f32[2,528,128]{2,1,0:T(8,128)}, f32[2,528,128]{2,1,0:T(8,128)S(1)}, u32[]{:S(2)}, u32[]{:S(2)}) %collective-permute-start) | collective-permute-done | bytes 540704 | tf_op jit(solution)/shard_map/ppermute | solution.py:344
  29.9 0.2 combine.1
  30.1 0.6 copy-done.1
  30.7 33.3 %all_to_all.15.recv_ref = f32[16,136,128]{2,1,0:T(8,128)S(1)} all-to-all(f32[16,136,128]{2,1,0:T(8,128)S(1)} %combine.1), channel_id=1, replica_groups={{0,16,32,48,64,80,96,112,128,144,160,176,192,208,224,240},{8,24,40,56,7..., dimensions={0} | all-to-all | bytes 2228224 | tf_op jit(solution)/shard_map/all_to_all | solution.py:398
  64.0 0.1 scan.1
  64.1 27.9 %all_to_all.16.refs_1_ = f32[16,128,128]{2,1,0:T(8,128)S(1)} all-to-all(f32[16,128,128]{2,1,0:T(8,128)S(1)} %scan.1), channel_id=1, replica_groups={{0,16,32,48,64,80,96,112,128,144,160,176,192,208,224,240},{8,24,40,56,7..., dimensions={0} | all-to-all | bytes 2097152 | tf_op jit(solution)/shard_map/all_to_all | solution.py:412
  91.9 0.1 fusion
  92.0 1.0 collective-permute-start.2
  93.0 2.0 %collective-permute-start.3 = (f32[16,64,128]{2,1,0:T(8,128)S(1)}, f32[16,64,128]{2,1,0:T(8,128)S(1)}, u32[]{:S(2)}, u32[]{:S(2)}) collective-permute-start(f32[16,64,128]{2,1,0:T(8,128)S(1)} %get-tuple-element.78), channel_id=1, source_target_pairs={{0,8},{8,16},{16,24},{24,32},{32,40},{40,48},{48,56},{56,64},{64,7... | collective-permute-start | bytes 1572872 | tf_op jit(solution)/shard_map/ppermute | solution.py:414
  95.0 5.7 %intra.3 = (bf16[2048,128]{1,0:T(8,128)(2,1)}, bf16[2048,128]{1,0:T(8,128)(2,1)}, f32[2048,128]{1,0:T(8,128)}, f32[128,512]{1,0:T(8,128)}, f32[128,512]{1,0:T(8,...) custom-call(bf16[128,2048]{1,0:T(8,128)(2,1)} %bitcast.21, ...), custom_call_target="tpu_custom_call", output_to_operand_aliasing={{0}: (8, {}), {1}: (9, {}), {2}: (10, {}), {3}: (11, {}), {... | custom-call | flops 2000000000 | bytes 2500000 | tf_op jit(solution)/shard_map/intra/pallas_call | solution.py:365
  100.6 4.5 %collective-permute-done.2.refs_2_ = f32[16,64,128]{2,1,0:T(8,128)S(1)} collective-permute-done((f32[16,64,128]{2,1,0:T(8,128)S(1)}, f32[16,64,128]{2,1,0:T(8,128)S(1)}, u32[]{:S(2)}, u32[]{:S(2)}) %collective-permute-start.2) | collective-permute-done | bytes 524320 | tf_op jit(solution)/shard_map/ppermute | solution.py:413
  105.1 4.2 %collective-permute-done.3.refs_3_ = f32[16,64,128]{2,1,0:T(8,128)S(1)} collective-permute-done((f32[16,64,128]{2,1,0:T(8,128)S(1)}, f32[16,64,128]{2,1,0:T(8,128)S(1)}, u32[]{:S(2)}, u32[]{:S(2)}) %collective-permute-start.3) | collective-permute-done | bytes 524320 | tf_op jit(solution)/shard_map/ppermute | solution.py:414
  109.2 0.8 copy-done.11
  110.0 4.9 %rates.1 = (f32[64,128]{1,0:T(8,128)}, f32[32,1,128]{2,1,0:T(1,128)}, bf16[2048,128]{1,0:T(8,128)(2,1)}, bf16[2048,128]{1,0:T(8,128)(2,1)}) custom-call(s32[1]{0:T(128)} %bitcast.refs_0_.position_ref, f32[16,128,128]{2,1,0:T(8,128)} %copy-done.9, f32[16,64,128]{2,1,0:T(8,128)} %copy-done.10, f32[16,64,128]{2,1,0:T(8,128)} %copy-done.11, ...), custom_call_target="tpu_custom_call" | custom-call | flops 10000000 | bytes 6000000 | tf_op jit(solution)/shard_map/rates/pallas_call | solution.py:419
  115.0 4.9 %all-to-all-start.2 = ((f32[32,1,128]{2,1,0:T(1,128)}), f32[32,1,128]{2,1,0:T(1,128)S(1)}, u32[]{:S(2)}, u32[]{:S(2)}) async-start(f32[32,1,128]{2,1,0:T(1,128)} %get-tuple-element.76), calls=%async_computation.2 | async-start | bytes 32768 | tf_op jit(solution)/shard_map/all_to_all | solution.py:265
  119.9 5.4 %finish.1 = (bf16[128,2048]{1,0:T(8,128)(2,1)}, bf16[128,512]{1,0:T(8,128)(2,1)}, bf16[128,512]{1,0:T(8,128)(2,1)}, f32[64,128]{1,0:T(8,128)}) custom-call(bf16[2048,128]{1,0:T(8,128)(2,1)} %get-tuple-element.62.state_low_ref, bf16[2048,128]{1,0:T(8,128)(2,1)} %get-tuple-element.63.adjoint_low_ref, f32[64,128]{1,0:T(8,128)} %get-tuple-element.64.cross_ref, ...), custom_call_target="tpu_custom_call" | custom-call | flops 1500000000 | bytes 5000000 | tf_op jit(solution)/shard_map/finish/pallas_call | solution.py:439
  125.2 4.4 %all-to-all-done.2 = f32[32,1,128]{2,1,0:T(1,128)S(1)} async-done(((f32[32,1,128]{2,1,0:T(1,128)}), f32[32,1,128]{2,1,0:T(1,128)S(1)}, u32[]{:S(2)}, u32[]{:S(2)}) %all-to-all-start.2) | async-done | bytes 16416 | tf_op jit(solution)/shard_map/all_to_all | solution.py:265
  129.7 0.1 reduce_sum.11
  129.7 0.1 collective-permute-start.4
  129.8 1.1 collective-permute-done.4
  130.9 1.3 collective-permute-start.5
  132.2 2.3 %collective-permute-done.5 = f32[1,128]{1,0:T(1,128)S(1)} collective-permute-done((f32[1,128]{1,0:T(1,128)S(1)}, f32[1,128]{1,0:T(1,128)S(1)}, u32[]{:S(2)}, u32[]{:S(2)}) %collective-permute-start.5) | collective-permute-done | bytes 544 | tf_op jit(solution)/shard_map/ppermute | solution.py:269
  134.5 0.3 collective-permute-start.6
  134.8 4.7 %collective-permute-done.6 = f32[1,128]{1,0:T(1,128)S(1)} collective-permute-done((f32[1,128]{1,0:T(1,128)S(1)}, f32[1,128]{1,0:T(1,128)S(1)}, u32[]{:S(2)}, u32[]{:S(2)}) %collective-permute-start.6) | collective-permute-done | bytes 544 | tf_op jit(solution)/shard_map/ppermute | solution.py:269
  139.5 0.6 slice_bitcast_fusion
  (26 shorter events, 0.1 us)
Async XLA Ops:
  0.6 12.0 %copy-start.6 = (f32[1,64,128]{2,1,0:T(8,128)S(1)}, f32[1,64,128]{2,1,0:T(8,128)}, u32[]{:S(2)}) copy-start(f32[1,64,128]{2,1,0:T(8,128)} %param.9) | copy-start | bytes 98308
  0.6 12.0 %copy-start.8 = (f32[64]{0:T(128)S(1)}, f32[64]{0:T(128)}, u32[]{:S(2)}) copy-start(f32[64]{0:T(128)} %param.11) | copy-start | bytes 772
  0.7 12.0 %copy-start.4 = (bf16[1,128,512]{2,1,0:T(8,128)(2,1)S(1)}, bf16[1,128,512]{2,1,0:T(8,128)(2,1)}, u32[]{:S(2)}) copy-start(bf16[1,128,512]{2,1,0:T(8,128)(2,1)} %param.13) | copy-start | bytes 393220
  0.7 12.0 %copy-start.5 = (bf16[1,128,512]{2,1,0:T(8,128)(2,1)S(1)}, bf16[1,128,512]{2,1,0:T(8,128)(2,1)}, u32[]{:S(2)}) copy-start(bf16[1,128,512]{2,1,0:T(8,128)(2,1)} %param.14) | copy-start | bytes 393220
  0.7 12.0 %copy-start.2 = (bf16[1,128,2048]{2,1,0:T(8,128)(2,1)S(1)}, bf16[1,128,2048]{2,1,0:T(8,128)(2,1)}, u32[]{:S(2)}) copy-start(bf16[1,128,2048]{2,1,0:T(8,128)(2,1)} %param.8) | copy-start | bytes 1572868
  0.7 12.0 %copy-start.3 = (bf16[1,128,2048]{2,1,0:T(8,128)(2,1)S(1)}, bf16[1,128,2048]{2,1,0:T(8,128)(2,1)}, u32[]{:S(2)}) copy-start(bf16[1,128,2048]{2,1,0:T(8,128)(2,1)} %param.15) | copy-start | bytes 1572868
  0.7 12.0 %copy-start.7 = (f32[1,128]{1,0:T(1,128)S(1)}, f32[1,128]{1,0:T(1,128)}, u32[]{:S(2)}) copy-start(f32[1,128]{1,0:T(1,128)} %refs_7_.3) | copy-start | bytes 1540
  4.5 21.0 %collective-permute-start.1 = (f32[2,528,128]{2,1,0:T(8,128)}, f32[2,528,128]{2,1,0:T(8,128)S(1)}, u32[]{:S(2)}, u32[]{:S(2)}) collective-permute-start(f32[2,528,128]{2,1,0:T(8,128)} %get-tuple-element.44), channel_id=1, source_target_pairs={{8,0},{16,8},{24,16},{32,24},{40,32},{48,40},{56,48},{64,56},{72,6... | collective-permute-start | bytes 1622024 | tf_op jit(solution)/shard_map/ppermute | solution.py:345
  12.6 17.3 %collective-permute-start = (f32[2,528,128]{2,1,0:T(8,128)}, f32[2,528,128]{2,1,0:T(8,128)S(1)}, u32[]{:S(2)}, u32[]{:S(2)}) collective-permute-start(f32[2,528,128]{2,1,0:T(8,128)} %get-tuple-element.42), channel_id=1, source_target_pairs={{0,8},{8,16},{16,24},{24,32},{32,40},{40,48},{48,56},{56,64},{64,7... | collective-permute-start | bytes 1622024 | tf_op jit(solution)/shard_map/ppermute | solution.py:344
  25.5 4.6 %copy-start = (f32[2,528,128]{2,1,0:T(8,128)}, f32[2,528,128]{2,1,0:T(8,128)S(1)}, u32[]{:S(2)}) copy-start(f32[2,528,128]{2,1,0:T(8,128)S(1)} %collective-permute-done.1.refs_3_.refs_5_) | copy-start | bytes 1622020
  29.9 0.8 copy-start.1
  91.9 8.7 %copy-start.9 = (f32[16,128,128]{2,1,0:T(8,128)}, f32[16,128,128]{2,1,0:T(8,128)S(1)}, u32[]{:S(2)}) copy-start(f32[16,128,128]{2,1,0:T(8,128)S(1)} %all_to_all.16.refs_1_) | copy-start | bytes 3145732
  92.0 13.1 %collective-permute-start.2 = (f32[16,64,128]{2,1,0:T(8,128)S(1)}, f32[16,64,128]{2,1,0:T(8,128)S(1)}, u32[]{:S(2)}, u32[]{:S(2)}) collective-permute-start(f32[16,64,128]{2,1,0:T(8,128)S(1)} %get-tuple-element.79), channel_id=1, source_target_pairs={{8,0},{16,8},{24,16},{32,24},{40,32},{48,40},{56,48},{64,56},{72,6... | collective-permute-start | bytes 1572872 | tf_op jit(solution)/shard_map/ppermute | solution.py:413
  93.0 16.2 %collective-permute-start.3 = (f32[16,64,128]{2,1,0:T(8,128)S(1)}, f32[16,64,128]{2,1,0:T(8,128)S(1)}, u32[]{:S(2)}, u32[]{:S(2)}) collective-permute-start(f32[16,64,128]{2,1,0:T(8,128)S(1)} %get-tuple-element.78), channel_id=1, source_target_pairs={{0,8},{8,16},{16,24},{24,32},{32,40},{40,48},{48,56},{56,64},{64,7... | collective-permute-start | bytes 1572872 | tf_op jit(solution)/shard_map/ppermute | solution.py:414
  105.1 4.2 %copy-start.10 = (f32[16,64,128]{2,1,0:T(8,128)}, f32[16,64,128]{2,1,0:T(8,128)S(1)}, u32[]{:S(2)}) copy-start(f32[16,64,128]{2,1,0:T(8,128)S(1)} %collective-permute-done.2.refs_2_) | copy-start | bytes 1572868
  109.2 0.8 copy-start.11
  115.0 14.7 %all-to-all-start.2 = ((f32[32,1,128]{2,1,0:T(1,128)}), f32[32,1,128]{2,1,0:T(1,128)S(1)}, u32[]{:S(2)}, u32[]{:S(2)}) async-start(f32[32,1,128]{2,1,0:T(1,128)} %get-tuple-element.76), calls=%async_computation.2 | async-start | bytes 32768 | tf_op jit(solution)/shard_map/all_to_all | solution.py:265
  129.7 1.2 collective-permute-start.4
  130.9 3.5 %collective-permute-start.5 = (f32[1,128]{1,0:T(1,128)S(1)}, f32[1,128]{1,0:T(1,128)S(1)}, u32[]{:S(2)}, u32[]{:S(2)}) collective-permute-start(f32[1,128]{1,0:T(1,128)S(1)} %bitcast_add_fusion), channel_id=1, source_target_pairs={{0,2},{1,3},{2,0},{3,1},{4,6},{5,7},{6,4},{7,5},{8,10},{9,11},{10,... | collective-permute-start | bytes 1544 | tf_op jit(solution)/shard_map/ppermute | solution.py:269
  134.5 5.0 %collective-permute-start.6 = (f32[1,128]{1,0:T(1,128)S(1)}, f32[1,128]{1,0:T(1,128)S(1)}, u32[]{:S(2)}, u32[]{:S(2)}) collective-permute-start(f32[1,128]{1,0:T(1,128)S(1)} %add.10), channel_id=1, source_target_pairs={{0,4},{1,5},{2,6},{3,7},{4,0},{5,1},{6,2},{7,3},{8,12},{9,13},{10,... | collective-permute-start | bytes 1544 | tf_op jit(solution)/shard_map/ppermute | solution.py:269

commit v8 on v7

--- a/solution.py
+++ b/solution.py
@@ -19,6 +19,7 @@
 f32 = jnp.float32
 bf16 = jnp.bfloat16
 VMEM_LIMIT = 60 * 1024 * 1024
+ROOMY_LIMIT = 48 * 1024 * 1024
 SMALL_LIMIT = 16 * 1024 * 1024
 
 
@@ -145,8 +146,8 @@
     cross_ref[...] = jnp.broadcast_to(-rate * steps_all * jnp.exp(last), (K, N))
 
 
-def intra_kernel(first, x_ref, dy_ref, step_ref, cum_ref, rate_ref, key_ref, query_ref, sums_in_ref, *refs):
-    xt_ref, dyt_ref, intra_ref, dq_ref, dk_ref, flow_ref, own_ref, sums_ref = refs[-8:]
+def intra_kernel(x_ref, dy_ref, step_ref, cum_ref, rate_ref, key_ref, query_ref,
+                 xt_ref, dyt_ref, intra_ref, dq_ref, dk_ref, flow_ref, own_ref, sums_ref):
     length = dy_ref.shape[0]
     x_full = x_ref[...].astype(f32).T
     dy_full = dy_ref[...].astype(f32).T
@@ -187,11 +188,11 @@
     flow_ref[...] = flow
     own_ref[...] = head_sum(x_full * intra_ref[...])
     skip_part = jnp.sum(head_sum(x_full * dy_full), axis=1, keepdims=True)
-    group = first + pl.program_id(0)
+    group = pl.program_id(0)
     passed = jnp.dot(step, triangle(length, True).astype(f32), precision=highest)
     rate_part = -column_of_group(rate_ref, group) * jnp.sum(passed * flow, axis=1, keepdims=True)
     parts = row_of_group(skip_part, group, H) + row_of_group(rate_part, group, 0)
-    accumulate(sums_ref, sums_in_ref[...], parts)
+    accumulate(sums_ref, jnp.zeros(sums_ref.shape, f32), parts)
 
 
 def rates_kernel(position_ref, carry_ref, state_in_ref, adjoint_in_ref, recv_state_ref, recv_seed_ref,
@@ -301,6 +302,7 @@
         return jax.ShapeDtypeStruct(dims, dtype)
 
     params = pltpu.CompilerParams(vmem_limit_bytes=VMEM_LIMIT)
+    roomy = pltpu.CompilerParams(vmem_limit_bytes=ROOMY_LIMIT)
     small = pltpu.CompilerParams(vmem_limit_bytes=SMALL_LIMIT)
     tokens = ((length, GP), lambda g: (0, g))
     features = ((GP, length), lambda g: (g, 0))
@@ -313,7 +315,7 @@
     one_message = block((1, MSG, N), lambda s: (s, 0, 0))
     message = shape((PG, MSG, N))
     cums = shape((PAIR, PG, K, length))
-    low_states = shape((H * P_SIZE, N), bf16)
+    low_states = pltpu.HBM((H * P_SIZE, N), bf16)
 
     def prepare(first):
         other = 1 - first
@@ -345,42 +347,6 @@
     recv_seed = lax.ppermute(second_seeds, "seq", back)
     second_states, first_seeds = prepare(1)
 
-    low_rows = ((GP, N), lambda g: (g, 0))
-    state_moment, adjoint_moment, cross_weight = pl.pallas_call(
-        moments_kernel,
-        grid=(G,),
-        in_specs=[block(*tokens), block(*tokens), block(*head_rows), block(*cum_rows), per_head, block(*group_rows),
-                  block(*group_rows)],
-        out_specs=[block(*low_rows), block(*low_rows), block((K, N), lambda g: (g, 0))],
-        out_shape=[shape((H * P_SIZE, N)), shape((H * P_SIZE, N)), shape((H, N))],
-        compiler_params=params,
-        cost_estimate=pl.CostEstimate(flops=1_000_000_000, bytes_accessed=4_000_000, transcendentals=20_000),
-        name="moments",
-    )(x, dy, step, cum, rate, key_rows, query_rows)
-
-    def intra_half(first, sums, earlier):
-        def at(dims, index):
-            return block(dims, lambda s: index(first + s))
-
-        return pl.pallas_call(
-            lambda *refs: intra_kernel(first, *refs),
-            grid=(G // 2,),
-            in_specs=[at(*tokens), at(*tokens), at(*head_rows), at(*cum_rows), per_head, at(*group_rows),
-                      at(*group_rows), sums_row] + [pl.BlockSpec(memory_space=pl.ANY)] * len(earlier),
-            out_specs=[at(*features), at(*features), at(*features), at(*group_rows), at(*group_rows),
-                       at(*head_rows), at(*head_rows), sums_row],
-            out_shape=[shape((H * P_SIZE, length), bf16), shape((H * P_SIZE, length), bf16),
-                       shape((H * P_SIZE, length)), shape((length, G * N)), shape((length, G * N)),
-                       shape((H, length)), shape((H, length)), shape((1, 2 * H))],
-            input_output_aliases={8 + i: i for i in range(len(earlier))},
-            compiler_params=params,
-            cost_estimate=pl.CostEstimate(flops=2_000_000_000, bytes_accessed=2_500_000, transcendentals=500_000),
-            name="intra",
-        )(x, dy, step, cum, rate, key_rows, query_rows, sums, *earlier)
-
-    outcome = intra_half(0, jnp.zeros((1, 2 * H), f32), ())
-    recv_seed, state_moment, sums = lax.optimization_barrier((recv_seed, state_moment, outcome[-1]))
-
     slot = 2 * half + 8
     send = pl.pallas_call(
         lambda *refs: combine_kernel(*refs, blocks=blocks),
@@ -395,7 +361,22 @@
         cost_estimate=pl.CostEstimate(flops=1_000_000, bytes_accessed=3_300_000, transcendentals=0),
         name="combine",
     )(position, recv_state, second_states, recv_seed, first_seeds)
+    send, later_cum = lax.optimization_barrier((send, cum))
     recv = lax.all_to_all(send, "seq", 0, 0, axis_index_groups=parities)
+    low_rows = ((GP, N), lambda g: (g, 0))
+    state_moment, adjoint_moment, cross_weight = pl.pallas_call(
+        moments_kernel,
+        grid=(G,),
+        in_specs=[block(*tokens), block(*tokens), block(*head_rows), block(*cum_rows), per_head, block(*group_rows),
+                  block(*group_rows)],
+        out_specs=[block(*low_rows), block(*low_rows), block((K, N), lambda g: (g, 0))],
+        out_shape=[pltpu.VMEM((H * P_SIZE, N), f32), pltpu.VMEM((H * P_SIZE, N), f32), pltpu.VMEM((H, N), f32)],
+        compiler_params=roomy,
+        cost_estimate=pl.CostEstimate(flops=1_000_000_000, bytes_accessed=4_000_000, transcendentals=20_000),
+        name="moments",
+    )(x, dy, step, later_cum, rate, key_rows, query_rows)
+
+    recv, cross_weight = lax.optimization_barrier((recv, cross_weight))
     scanned = pl.pallas_call(
         scan_kernel,
         grid_spec=pltpu.PrefetchScalarGridSpec(
@@ -413,8 +394,21 @@
     state_in = lax.ppermute(carries[:, :half], "seq", back)
     adjoint_in = lax.ppermute(carries[:, half:], "seq", around)
 
-    outcome = intra_half(G // 2, sums, tuple(outcome[:-1]))
-    x_t, dy_t, intra, dq_intra, dk_intra, flow, own, sums = outcome
+    x_t, dy_t, intra, dq_intra, dk_intra, flow, own, sums = pl.pallas_call(
+        intra_kernel,
+        grid=(G,),
+        in_specs=[block(*tokens), block(*tokens), block(*head_rows), block(*cum_rows), per_head, block(*group_rows),
+                  block(*group_rows)],
+        out_specs=[block(*features), block(*features), block(*features), block(*group_rows), block(*group_rows),
+                   block(*head_rows), block(*head_rows), sums_row],
+        out_shape=[pltpu.HBM((H * P_SIZE, length), bf16), pltpu.HBM((H * P_SIZE, length), bf16),
+                   pltpu.HBM((H * P_SIZE, length), f32), pltpu.HBM((length, G * N), f32),
+                   pltpu.HBM((length, G * N), f32), pltpu.HBM((H, length), f32), pltpu.HBM((H, length), f32),
+                   shape((1, 2 * H))],
+        compiler_params=roomy,
+        cost_estimate=pl.CostEstimate(flops=4_000_000_000, bytes_accessed=5_000_000, transcendentals=1_000_000),
+        name="intra",
+    )(x, dy, step, cum, rate, key_rows, query_rows)
 
     cross, sum_copies, state_low, adjoint_low = pl.pallas_call(
         lambda *refs: rates_kernel(*refs, blocks=blocks),
@@ -430,8 +424,8 @@
                        ordered(*low_rows), ordered(*low_rows)],
             scratch_shapes=[pltpu.VMEM((GP, N), f32), pltpu.VMEM((GP, N), f32), pltpu.VMEM((1, 2 * H), f32)],
         ),
-        out_shape=[shape((H, N)), shape((blocks, 1, 2 * H)), low_states, low_states],
-        compiler_params=params,
+        out_shape=[pltpu.HBM((H, N), f32), shape((blocks, 1, 2 * H)), low_states, low_states],
+        compiler_params=small,
         cost_estimate=pl.CostEstimate(flops=10_000_000, bytes_accessed=6_000_000, transcendentals=0),
         name="rates",
     )(position, carries, state_in, adjoint_in, recv_state, recv_seed, state_moment, adjoint_moment, cross_weight, sums)

time: 141 us -> 138 us (0.979)
  blocking collectives: 61.1 us -> 24.4 us
  waiting for transfers between devices: 25.5 us -> 50.6 us
  starting transfers between devices: 17.6 us -> 30.5 us
  Pallas kernels: 32.3 us -> 25.6 us
  local copies, waits for them, and re-layouts: 2.65 us -> 5.29 us
    all_to_all x1 -> x0, blocking collectives: 33.3 us -> none  [on_device(): recv = lax.all_to_all(send, 'seq', 0, 0, axis_index_groups=parities)]
    all_to_all x0 -> x1, waiting for transfers between devices: none -> 24.4 us  [on_device(): recv = lax.all_to_all(send, 'seq', 0, 0, axis_index_groups=parities)]
    all_to_all x0 -> x1, starting transfers between devices: none -> 5.93 us  [on_device(): recv = lax.all_to_all(send, 'seq', 0, 0, axis_index_groups=parities)]
    ppermute x1, waiting for transfers between devices: 4.37 us -> 10.3 us  [on_device(): recv_state = lax.ppermute(first_states, 'seq', around)]
    ppermute x1, starting transfers between devices: 1.96 us -> 7.48 us  [on_device(): adjoint_in = lax.ppermute(carries[:, half:], 'seq', around)]
    ppermute x1, waiting for transfers between devices: 4.45 us -> 0.01 us  [on_device(): state_in = lax.ppermute(carries[:, :half], 'seq', back)]
    all_to_all x1, blocking collectives: 27.9 us -> 24.4 us  [on_device(): carries = lax.all_to_all(scanned, 'seq', 0, 0, axis_index_groups=parities)]
    unnamed x24 -> x34, local copies, waits for them, and re-layouts: 1.48 us -> 4.63 us
  transfers between devices with their start and end apart: 8 -> 9, of which waited for: 7 -> 7; matrix products, arithmetic and copies ran while one was open for 0% -> 0% of each run, Pallas kernels for 17% -> 13%
where the time goes in v8:
time: 138 us; the launch traced here: 137 us
  waiting for transfers between devices  50.6 us (37%)
  starting transfers between devices  30.5 us (22%)
  Pallas kernels  25.6 us (19%)
  blocking collectives  24.4 us (18%)
  local copies, waits for them, and re-layouts  5.29 us (4%)
    all_to_all x1, waiting for transfers between devices, on_device(): recv = lax.all_to_all(send, 'seq', 0, 0, axis_index_groups=parities)  24.4 us
    all_to_all x1, blocking collectives, on_device(): carries = lax.all_to_all(scanned, 'seq', 0, 0, axis_index_groups=parities)  24.4 us
    ppermute x1, waiting for transfers between devices, on_device(): recv_state = lax.ppermute(first_states, 'seq', around)  10.3 us
    pallas_call x1, Pallas kernels, on_device(): pl.pallas_call(intra_kernel, grid=(G,), in_specs=[block(*tokens), block(*...  8.6 us
    ppermute x3, waiting for transfers between devices, total_over_devices(): row = row + lax.ppermute(row, 'dp', [(i, i ^ reach) for i in range(size)])  8.08 us
    ppermute x1, starting transfers between devices, on_device(): adjoint_in = lax.ppermute(carries[:, half:], 'seq', around)  7.48 us
    all_to_all x1, starting transfers between devices, total_over_devices(): lax.all_to_all(copies, 'seq', 0, 0)  6.74 us
    ppermute x1, starting transfers between devices, on_device(): recv_seed = lax.ppermute(second_seeds, 'seq', back)  6.22 us
  transfers between devices with their start and end apart: 9, of which 7 were waited for; matrix products, arithmetic and copies ran while one was open for 0% of the time, Pallas kernels for 13%

profile of v8, /device:TPU:16, one launch (start us, length us, event | category | flops | bytes accessed | tf_op | source)
XLA Modules:
  0.0 137.2 jit_solution(4616004447189558587)
XLA Ops:
  0.7 3.7 %prepare.2 = (f32[2,528,128]{2,1,0:T(8,128)}, f32[2,528,128]{2,1,0:T(8,128)}, f32[2,2,16,128]{3,2,1,0:T(8,128)}) custom-call(s32[1]{0:T(128)} %bitcast.refs_0_.position_ref, bf16[128,2048]{1,0:T(8,128)(2,1)} %bitcast.18, f32[64,128]{1,0:T(8,128)} %bitcast.36, f32[1,64]{1,0:T(1,128)} %bitcast.43, bf16[128,512]{1,0:T(8,128)(2,1)} %bitcast.26, ...), custom_call_target="tpu_custom_call" | custom-call | flops 500000000 | bytes 2500000 | tf_op jit(solution)/shard_map/prepare/pallas_call | solution.py:327
  4.4 2.0 %collective-permute-start = (f32[2,528,128]{2,1,0:T(8,128)}, f32[2,528,128]{2,1,0:T(8,128)S(1)}, u32[]{:S(2)}, u32[]{:S(2)}) collective-permute-start(f32[2,528,128]{2,1,0:T(8,128)} %get-tuple-element.35), channel_id=1, source_target_pairs={{0,8},{8,16},{16,24},{24,32},{32,40},{40,48},{48,56},{56,64},{64,7... | collective-permute-start | bytes 1622024 | tf_op jit(solution)/shard_map/ppermute | solution.py:346
  6.4 6.2 %collective-permute-start.1 = (f32[2,528,128]{2,1,0:T(8,128)}, f32[2,528,128]{2,1,0:T(8,128)S(1)}, u32[]{:S(2)}, u32[]{:S(2)}) collective-permute-start(f32[2,528,128]{2,1,0:T(8,128)} %get-tuple-element.37), channel_id=1, source_target_pairs={{8,0},{16,8},{24,16},{32,24},{40,32},{48,40},{56,48},{64,56},{72,6... | collective-permute-start | bytes 1622024 | tf_op jit(solution)/shard_map/ppermute | solution.py:347
  12.7 2.1 %prepare.3 = (f32[2,528,128]{2,1,0:T(8,128)S(1)}, f32[2,528,128]{2,1,0:T(8,128)S(1)}) custom-call(s32[1]{0:T(128)} %bitcast.refs_0_.position_ref, bf16[128,2048]{1,0:T(8,128)(2,1)S(1)} %bitcast.19, f32[64,128]{1,0:T(8,128)S(1)} %bitcast.39, f32[1,64]{1,0:T(1,128)S(1)} %bitcast.45, bf16[128,512]{1,0:T(8,128)(2,1)S(1)} %bitcast.28, ...), custom_call_target="tpu_custom_call" | custom-call | flops 500000000 | bytes 2500000 | tf_op jit(solution)/shard_map/prepare/pallas_call | solution.py:327
  14.8 10.3 %collective-permute-done.refs_1_.refs_4_ = f32[2,528,128]{2,1,0:T(8,128)S(1)} collective-permute-done((f32[2,528,128]{2,1,0:T(8,128)}, f32[2,528,128]{2,1,0:T(8,128)S(1)}, u32[]{:S(2)}, u32[]{:S(2)}) %collective-permute-start) | collective-permute-done | bytes 540704 | tf_op jit(solution)/shard_map/ppermute | solution.py:346
  25.1 1.1 combine.1
  26.1 5.9 %all-to-all-start = ((f32[16,136,128]{2,1,0:T(8,128)}), f32[16,136,128]{2,1,0:T(8,128)S(1)}, u32[]{:S(2)}, u32[]{:S(2)}) async-start(f32[16,136,128]{2,1,0:T(8,128)} %combine.1), calls=%async_computation | async-start | bytes 2228224 | tf_op jit(solution)/shard_map/all_to_all | solution.py:365
  32.1 1.0 copy-done.3
  33.1 1.0 copy-done.6
  34.2 0.8 copy-done.11
  34.9 0.8 copy-done.15
  35.7 2.3 %moments.1 = (f32[2048,128]{1,0:T(8,128)S(1)}, f32[2048,128]{1,0:T(8,128)S(1)}, f32[64,128]{1,0:T(8,128)S(1)}) custom-call(bf16[128,2048]{1,0:T(8,128)(2,1)S(1)} %bitcast.20, bf16[128,2048]{1,0:T(8,128)(2,1)S(1)} %bitcast.24, f32[64,128]{1,0:T(8,128)S(1)} %bitcast.41, f32[2,2,16,128]{3,2,1,0:T(8,128)S(1)} %copy-done.15, f32[1,64]{1,0:T(1,128)S(1)} %bitcast.46, ...), custom_call_target="tpu_custom_call" | custom-call | flops 1000000000 | bytes 4000000 | tf_op jit(solution)/shard_map/moments/pallas_call | solution.py:367
  38.0 1.0 copy-done
  39.0 24.4 %all-to-all-done.recv_ref = f32[16,136,128]{2,1,0:T(8,128)S(1)} async-done(((f32[16,136,128]{2,1,0:T(8,128)}), f32[16,136,128]{2,1,0:T(8,128)S(1)}, u32[]{:S(2)}, u32[]{:S(2)}) %all-to-all-start) | async-done | bytes 1114144 | tf_op jit(solution)/shard_map/all_to_all | solution.py:365
  63.4 0.1 scan.1
  63.6 24.4 %all_to_all.15.refs_1_ = f32[16,128,128]{2,1,0:T(8,128)S(1)} all-to-all(f32[16,128,128]{2,1,0:T(8,128)S(1)} %scan.1), channel_id=1, replica_groups={{0,16,32,48,64,80,96,112,128,144,160,176,192,208,224,240},{8,24,40,56,7..., dimensions={0} | all-to-all | bytes 2097152 | tf_op jit(solution)/shard_map/all_to_all | solution.py:393
  87.9 0.1 fusion
  88.0 7.5 %collective-permute-start.3 = (f32[16,64,128]{2,1,0:T(8,128)S(1)}, f32[16,64,128]{2,1,0:T(8,128)S(1)}, u32[]{:S(2)}, u32[]{:S(2)}) collective-permute-start(f32[16,64,128]{2,1,0:T(8,128)S(1)} %get-tuple-element.64), channel_id=1, source_target_pairs={{0,8},{8,16},{16,24},{24,32},{32,40},{40,48},{48,56},{56,64},{64,7... | collective-permute-start | bytes 1572872 | tf_op jit(solution)/shard_map/ppermute | solution.py:395
  95.5 0.4 collective-permute-start.2
  95.9 8.6 %intra.1 = (bf16[2048,128]{1,0:T(8,128)(2,1)}, bf16[2048,128]{1,0:T(8,128)(2,1)}, f32[2048,128]{1,0:T(8,128)}, f32[128,512]{1,0:T(8,128)}, f32[128,512]{1,0:T(8,...) custom-call(bf16[128,2048]{1,0:T(8,128)(2,1)S(1)} %bitcast.21, bf16[128,2048]{1,0:T(8,128)(2,1)S(1)} %bitcast.25, ...), custom_call_target="tpu_custom_call" | custom-call | flops 4000000000 | bytes 5000000 | tf_op jit(solution)/shard_map/intra/pallas_call | solution.py:397
  104.5 3.4 %collective-permute-done.3.refs_3_ = f32[16,64,128]{2,1,0:T(8,128)S(1)} collective-permute-done((f32[16,64,128]{2,1,0:T(8,128)S(1)}, f32[16,64,128]{2,1,0:T(8,128)S(1)}, u32[]{:S(2)}, u32[]{:S(2)}) %collective-permute-start.3) | collective-permute-done | bytes 524320 | tf_op jit(solution)/shard_map/ppermute | solution.py:395
  107.9 2.4 %rates.1 = (f32[64,128]{1,0:T(8,128)}, f32[32,1,128]{2,1,0:T(1,128)}, bf16[2048,128]{1,0:T(8,128)(2,1)}, bf16[2048,128]{1,0:T(8,128)(2,1)}) custom-call(s32[1]{0:T(128)} %bitcast.refs_0_.position_ref, f32[16,128,128]{2,1,0:T(8,128)S(1)} %all_to_all.15.refs_1_, f32[16,64,128]{2,1,0:T(8,128)S(1)} %collective-permute-done.2.refs_2_, ...), custom_call_target="tpu_custom_call" | custom-call | flops 10000000 | bytes 6000000 | tf_op jit(solution)/shard_map/rates/pallas_call | solution.py:413
  110.3 6.7 %all-to-all-start.2 = ((f32[32,1,128]{2,1,0:T(1,128)}), f32[32,1,128]{2,1,0:T(1,128)S(1)}, u32[]{:S(2)}, u32[]{:S(2)}) async-start(f32[32,1,128]{2,1,0:T(1,128)} %get-tuple-element.62), calls=%async_computation.2 | async-start | bytes 32768 | tf_op jit(solution)/shard_map/all_to_all | solution.py:266
  117.0 5.4 %finish.1 = (bf16[128,2048]{1,0:T(8,128)(2,1)}, bf16[128,512]{1,0:T(8,128)(2,1)}, bf16[128,512]{1,0:T(8,128)(2,1)}, f32[64,128]{1,0:T(8,128)}) custom-call(bf16[2048,128]{1,0:T(8,128)(2,1)} %get-tuple-element.48.state_low_ref, bf16[2048,128]{1,0:T(8,128)(2,1)} %get-tuple-element.49.adjoint_low_ref, f32[64,128]{1,0:T(8,128)} %get-tuple-element.50.cross_ref, ...), custom_call_target="tpu_custom_call" | custom-call | flops 1500000000 | bytes 5000000 | tf_op jit(solution)/shard_map/finish/pallas_call | solution.py:433
  122.4 4.4 %all-to-all-done.2 = f32[32,1,128]{2,1,0:T(1,128)S(1)} async-done(((f32[32,1,128]{2,1,0:T(1,128)}), f32[32,1,128]{2,1,0:T(1,128)S(1)}, u32[]{:S(2)}, u32[]{:S(2)}) %all-to-all-start.2) | async-done | bytes 16416 | tf_op jit(solution)/shard_map/all_to_all | solution.py:266
  126.8 0.1 collective-permute-start.4
  126.9 1.1 collective-permute-done.4
  128.0 1.3 collective-permute-start.5
  129.3 2.3 %collective-permute-done.5 = f32[1,128]{1,0:T(1,128)S(1)} collective-permute-done((f32[1,128]{1,0:T(1,128)S(1)}, f32[1,128]{1,0:T(1,128)S(1)}, u32[]{:S(2)}, u32[]{:S(2)}) %collective-permute-start.5) | collective-permute-done | bytes 544 | tf_op jit(solution)/shard_map/ppermute | solution.py:270
  131.6 0.3 collective-permute-start.6
  131.9 4.7 %collective-permute-done.6 = f32[1,128]{1,0:T(1,128)S(1)} collective-permute-done((f32[1,128]{1,0:T(1,128)S(1)}, f32[1,128]{1,0:T(1,128)S(1)}, u32[]{:S(2)}, u32[]{:S(2)}) %collective-permute-start.6) | collective-permute-done | bytes 544 | tf_op jit(solution)/shard_map/ppermute | solution.py:270
  136.6 0.6 slice_bitcast_fusion
  (35 shorter events, 0.1 us)
Async XLA Ops:
  0.6 12.0 %copy-start.13 = (f32[1,128]{1,0:T(1,128)S(1)}, f32[1,128]{1,0:T(1,128)}, u32[]{:S(2)}) copy-start(f32[1,128]{1,0:T(1,128)} %refs_7_.3) | copy-start | bytes 1540
  0.6 12.0 %copy-start.5 = (bf16[1,128,2048]{2,1,0:T(8,128)(2,1)S(1)}, bf16[1,128,2048]{2,1,0:T(8,128)(2,1)}, u32[]{:S(2)}) copy-start(bf16[1,128,2048]{2,1,0:T(8,128)(2,1)} %param.15) | copy-start | bytes 1572868
  0.7 12.0 %copy-start.9 = (bf16[1,128,512]{2,1,0:T(8,128)(2,1)S(1)}, bf16[1,128,512]{2,1,0:T(8,128)(2,1)}, u32[]{:S(2)}) copy-start(bf16[1,128,512]{2,1,0:T(8,128)(2,1)} %param.14) | copy-start | bytes 393220
  0.7 12.0 %copy-start.8 = (bf16[1,128,512]{2,1,0:T(8,128)(2,1)S(1)}, bf16[1,128,512]{2,1,0:T(8,128)(2,1)}, u32[]{:S(2)}) copy-start(bf16[1,128,512]{2,1,0:T(8,128)(2,1)} %param.13) | copy-start | bytes 393220
  0.7 12.0 %copy-start.14 = (f32[64]{0:T(128)S(1)}, f32[64]{0:T(128)}, u32[]{:S(2)}) copy-start(f32[64]{0:T(128)} %param.11) | copy-start | bytes 772
  0.7 12.0 %copy-start.10 = (f32[1,64,128]{2,1,0:T(8,128)S(1)}, f32[1,64,128]{2,1,0:T(8,128)}, u32[]{:S(2)}) copy-start(f32[1,64,128]{2,1,0:T(8,128)} %param.9) | copy-start | bytes 98308
  0.7 12.0 %copy-start.2 = (bf16[1,128,2048]{2,1,0:T(8,128)(2,1)S(1)}, bf16[1,128,2048]{2,1,0:T(8,128)(2,1)}, u32[]{:S(2)}) copy-start(bf16[1,128,2048]{2,1,0:T(8,128)(2,1)} %param.8) | copy-start | bytes 1572868
  4.4 20.6 %collective-permute-start = (f32[2,528,128]{2,1,0:T(8,128)}, f32[2,528,128]{2,1,0:T(8,128)S(1)}, u32[]{:S(2)}, u32[]{:S(2)}) collective-permute-start(f32[2,528,128]{2,1,0:T(8,128)} %get-tuple-element.35), channel_id=1, source_target_pairs={{0,8},{8,16},{16,24},{24,32},{32,40},{40,48},{48,56},{56,64},{64,7... | collective-permute-start | bytes 1622024 | tf_op jit(solution)/shard_map/ppermute | solution.py:346
  6.4 18.6 %collective-permute-start.1 = (f32[2,528,128]{2,1,0:T(8,128)}, f32[2,528,128]{2,1,0:T(8,128)S(1)}, u32[]{:S(2)}, u32[]{:S(2)}) collective-permute-start(f32[2,528,128]{2,1,0:T(8,128)} %get-tuple-element.37), channel_id=1, source_target_pairs={{8,0},{16,8},{24,16},{32,24},{40,32},{48,40},{56,48},{64,56},{72,6... | collective-permute-start | bytes 1622024 | tf_op jit(solution)/shard_map/ppermute | solution.py:347
  26.1 37.3 %all-to-all-start = ((f32[16,136,128]{2,1,0:T(8,128)}), f32[16,136,128]{2,1,0:T(8,128)S(1)}, u32[]{:S(2)}, u32[]{:S(2)}) async-start(f32[16,136,128]{2,1,0:T(8,128)} %combine.1), calls=%async_computation | async-start | bytes 2228224 | tf_op jit(solution)/shard_map/all_to_all | solution.py:365
  32.1 1.0 copy-start.3
  33.1 1.0 copy-start.6
  34.2 0.8 copy-start.11
  34.9 0.8 copy-start.15
  38.0 1.0 copy-start
  87.9 8.0 %copy-start.4 = (bf16[1,128,2048]{2,1,0:T(8,128)(2,1)S(1)}, bf16[1,128,2048]{2,1,0:T(8,128)(2,1)}, u32[]{:S(2)}) copy-start(bf16[1,128,2048]{2,1,0:T(8,128)(2,1)} %param.8) | copy-start | bytes 1572868
  87.9 8.0 %copy-start.7 = (bf16[1,128,2048]{2,1,0:T(8,128)(2,1)S(1)}, bf16[1,128,2048]{2,1,0:T(8,128)(2,1)}, u32[]{:S(2)}) copy-start(bf16[1,128,2048]{2,1,0:T(8,128)(2,1)} %param.15) | copy-start | bytes 1572868
  87.9 8.0 %copy-start.12 = (f32[1,64,128]{2,1,0:T(8,128)S(1)}, f32[1,64,128]{2,1,0:T(8,128)}, u32[]{:S(2)}) copy-start(f32[1,64,128]{2,1,0:T(8,128)} %param.9) | copy-start | bytes 98308
  87.9 8.0 %copy-start.16 = (f32[2,2,16,128]{3,2,1,0:T(8,128)S(1)}, f32[2,2,16,128]{3,2,1,0:T(8,128)}, u32[]{:S(2)}) copy-start(f32[2,2,16,128]{3,2,1,0:T(8,128)} %get-tuple-element.41.cum_ref) | copy-start | bytes 98308
  88.0 19.8 %collective-permute-start.3 = (f32[16,64,128]{2,1,0:T(8,128)S(1)}, f32[16,64,128]{2,1,0:T(8,128)S(1)}, u32[]{:S(2)}, u32[]{:S(2)}) collective-permute-start(f32[16,64,128]{2,1,0:T(8,128)S(1)} %get-tuple-element.64), channel_id=1, source_target_pairs={{0,8},{8,16},{16,24},{24,32},{32,40},{40,48},{48,56},{56,64},{64,7... | collective-permute-start | bytes 1572872 | tf_op jit(solution)/shard_map/ppermute | solution.py:395
  95.5 12.4 %copy-start.1 = (f32[2048,128]{1,0:T(8,128)S(1)}, f32[2048,128]{1,0:T(8,128)}, u32[]{:S(2)}) copy-start(f32[2048,128]{1,0:T(8,128)} %copy-done) | copy-start | bytes 3145732
  95.5 12.4 %collective-permute-start.2 = (f32[16,64,128]{2,1,0:T(8,128)S(1)}, f32[16,64,128]{2,1,0:T(8,128)S(1)}, u32[]{:S(2)}, u32[]{:S(2)}) collective-permute-start(f32[16,64,128]{2,1,0:T(8,128)S(1)} %get-tuple-element.65), channel_id=1, source_target_pairs={{8,0},{16,8},{24,16},{32,24},{40,32},{48,40},{56,48},{64,56},{72,6... | collective-permute-start | bytes 1572872 | tf_op jit(solution)/shard_map/ppermute | solution.py:394
  110.3 16.5 %all-to-all-start.2 = ((f32[32,1,128]{2,1,0:T(1,128)}), f32[32,1,128]{2,1,0:T(1,128)S(1)}, u32[]{:S(2)}, u32[]{:S(2)}) async-start(f32[32,1,128]{2,1,0:T(1,128)} %get-tuple-element.62), calls=%async_computation.2 | async-start | bytes 32768 | tf_op jit(solution)/shard_map/all_to_all | solution.py:266
  126.8 1.2 collective-permute-start.4
  128.0 3.5 %collective-permute-start.5 = (f32[1,128]{1,0:T(1,128)S(1)}, f32[1,128]{1,0:T(1,128)S(1)}, u32[]{:S(2)}, u32[]{:S(2)}) collective-permute-start(f32[1,128]{1,0:T(1,128)S(1)} %bitcast_add_fusion), channel_id=1, source_target_pairs={{0,2},{1,3},{2,0},{3,1},{4,6},{5,7},{6,4},{7,5},{8,10},{9,11},{10,... | collective-permute-start | bytes 1544 | tf_op jit(solution)/shard_map/ppermute | solution.py:270
  131.6 5.0 %collective-permute-start.6 = (f32[1,128]{1,0:T(1,128)S(1)}, f32[1,128]{1,0:T(1,128)S(1)}, u32[]{:S(2)}, u32[]{:S(2)}) collective-permute-start(f32[1,128]{1,0:T(1,128)S(1)} %add.10), channel_id=1, source_target_pairs={{0,4},{1,5},{2,6},{3,7},{4,0},{5,1},{6,2},{7,3},{8,12},{9,13},{10,... | collective-permute-start | bytes 1544 | tf_op jit(solution)/shard_map/ppermute | solution.py:270

commit v9 on v8

--- a/solution.py
+++ b/solution.py
@@ -265,10 +265,11 @@
 def total_over_devices(copies, beside):
     row, _ = lax.optimization_barrier((lax.all_to_all(copies, "seq", 0, 0), beside))
     row = jnp.sum(row, axis=0)
-    size, reach = lax.axis_size("dp"), 1
-    while reach < size:
-        row = row + lax.ppermute(row, "dp", [(i, i ^ reach) for i in range(size)])
-        reach *= 2
+    size, cores = lax.axis_size("dp"), 2
+    row = row + lax.ppermute(row, "dp", [(i, i ^ 1) for i in range(size)])
+    assert size == 4 * cores
+    around = [lax.ppermute(row, "dp", [(i, (i + hop * cores) % size) for i in range(size)]) for hop in (1, 2, 3)]
+    row = (row + around[1]) + (around[0] + around[2])
     return row
 
 
@@ -320,7 +321,7 @@
     def prepare(first):
         other = 1 - first
         kept = pltpu.VMEM(message.shape, f32)
-        out_specs, out_shape = [one_message] * 2, [message if first == 0 else kept] * 2
+        out_specs, out_shape = [one_message] * 2, [kept] * 2
         if first == 0:
             out_specs.append(block((PAIR, 1, K, length), lambda s: (0, s, 0, 0)))
             out_shape.append(cums)
@@ -347,6 +348,8 @@
     recv_seed = lax.ppermute(second_seeds, "seq", back)
     second_states, first_seeds = prepare(1)
 
+    recv_seed, later_cum = lax.optimization_barrier((recv_seed, cum))
+
     slot = 2 * half + 8
     send = pl.pallas_call(
         lambda *refs: combine_kernel(*refs, blocks=blocks),
@@ -361,7 +364,6 @@
         cost_estimate=pl.CostEstimate(flops=1_000_000, bytes_accessed=3_300_000, transcendentals=0),
         name="combine",
     )(position, recv_state, second_states, recv_seed, first_seeds)
-    send, later_cum = lax.optimization_barrier((send, cum))
     recv = lax.all_to_all(send, "seq", 0, 0, axis_index_groups=parities)
     low_rows = ((GP, N), lambda g: (g, 0))
     state_moment, adjoint_moment, cross_weight = pl.pallas_call(

time: 138 us -> 140 us (1.014)
  blocking collectives: 24.4 us -> 31.4 us
  starting transfers between devices: 30.5 us -> 27.2 us
  waiting for transfers between devices: 50.6 us -> 48 us
    ppermute x1, waiting for transfers between devices: 0.01 us -> 9.41 us  [on_device(): recv_seed = lax.ppermute(second_seeds, 'seq', back)]
    ppermute x1, starting transfers between devices: 7.48 us -> 0.08 us  [on_device(): adjoint_in = lax.ppermute(carries[:, half:], 'seq', around)]
    all_to_all x1, blocking collectives: 24.4 us -> 31.4 us  [on_device(): carries = lax.all_to_all(scanned, 'seq', 0, 0, axis_index_groups=parities)]
    ppermute x1, starting transfers between devices: 0.39 us -> 5.32 us  [on_device(): state_in = lax.ppermute(carries[:, :half], 'seq', back)]
    ppermute x1, waiting for transfers between devices: 10.3 us -> 5.52 us  [on_device(): recv_state = lax.ppermute(first_states, 'seq', around)]
    ppermute x3 -> x4, waiting for transfers between devices: 8.08 us -> 4.82 us  [the longest x3 3.72 us: total_over_devices(): lax.ppermute(row, 'dp', [(i, (i + hop * cores) % size) for i in range(siz...]
    all_to_all x1, starting transfers between devices: 5.93 us -> 3.7 us  [on_device(): recv = lax.all_to_all(send, 'seq', 0, 0, axis_index_groups=parities)]
    ppermute x1, waiting for transfers between devices: 3.36 us -> 1.32 us  [on_device(): adjoint_in = lax.ppermute(carries[:, half:], 'seq', around)]
  transfers between devices with their start and end apart: 9 -> 10, of which waited for: 7 -> 9; matrix products, arithmetic and copies ran while one was open for 0% -> 0% of each run, Pallas kernels for 13% -> 13%
where the time goes in v9:
time: 140 us; the launch traced here: 138 us
  waiting for transfers between devices  48 us (34%)
  blocking collectives  31.4 us (22%)
  starting transfers between devices  27.2 us (19%)
  Pallas kernels  25.5 us (18%)
  local copies, waits for them, and re-layouts  5.28 us (4%)
    all_to_all x1, blocking collectives, on_device(): carries = lax.all_to_all(scanned, 'seq', 0, 0, axis_index_groups=parities)  31.4 us
    all_to_all x1, waiting for transfers between devices, on_device(): recv = lax.all_to_all(send, 'seq', 0, 0, axis_index_groups=parities)  22.5 us
    ppermute x1, waiting for transfers between devices, on_device(): recv_seed = lax.ppermute(second_seeds, 'seq', back)  9.41 us
    pallas_call x1, Pallas kernels, on_device(): pl.pallas_call(intra_kernel, grid=(G,), in_specs=[block(*tokens), block(*...  8.61 us
    ppermute x1, starting transfers between devices, on_device(): recv_seed = lax.ppermute(second_seeds, 'seq', back)  8.05 us
    all_to_all x1, starting transfers between devices, total_over_devices(): lax.all_to_all(copies, 'seq', 0, 0)  6.65 us
    pallas_call x2, Pallas kernels, prepare(): pl.pallas_call(lambda *refs: prepare_kernel(first, *refs), grid_spec=pltp...  5.66 us
    ppermute x1, waiting for transfers between devices, on_device(): recv_state = lax.ppermute(first_states, 'seq', around)  5.52 us
  transfers between devices with their start and end apart: 10, of which 9 were waited for; matrix products, arithmetic and copies ran while one was open for 0% of the time, Pallas kernels for 13%

profile of v9, /device:TPU:16, one launch (start us, length us, event | category | flops | bytes accessed | tf_op | source)
XLA Modules:
  0.0 138.3 jit_solution(16088445152806885101)
XLA Ops:
  0.7 3.6 %prepare.2 = (f32[2,528,128]{2,1,0:T(8,128)S(1)}, f32[2,528,128]{2,1,0:T(8,128)S(1)}, f32[2,2,16,128]{3,2,1,0:T(8,128)}) custom-call(s32[1]{0:T(128)} %bitcast.refs_0_.position_ref, bf16[128,2048]{1,0:T(8,128)(2,1)} %bitcast.18, f32[64,128]{1,0:T(8,128)} %bitcast.36, f32[1,64]{1,0:T(1,128)} %bitcast.43, bf16[128,512]{1,0:T(8,128)(2,1)} %bitcast.26, ...), custom_call_target="tpu_custom_call" | custom-call | flops 500000000 | bytes 2500000 | tf_op jit(solution)/shard_map/prepare/pallas_call | solution.py:328
  4.3 8.1 %collective-permute-start.1 = (f32[2,528,128]{2,1,0:T(8,128)S(1)}, f32[2,528,128]{2,1,0:T(8,128)S(1)}, u32[]{:S(2)}, u32[]{:S(2)}) collective-permute-start(f32[2,528,128]{2,1,0:T(8,128)S(1)} %get-tuple-element.37), channel_id=1, source_target_pairs={{8,0},{16,8},{24,16},{32,24},{40,32},{48,40},{56,48},{64,56},{72,6... | collective-permute-start | bytes 1622024 | tf_op jit(solution)/shard_map/ppermute | solution.py:348
  12.4 2.1 %prepare.3 = (f32[2,528,128]{2,1,0:T(8,128)S(1)}, f32[2,528,128]{2,1,0:T(8,128)S(1)}) custom-call(s32[1]{0:T(128)} %bitcast.refs_0_.position_ref, bf16[128,2048]{1,0:T(8,128)(2,1)S(1)} %bitcast.19, f32[64,128]{1,0:T(8,128)S(1)} %bitcast.39, f32[1,64]{1,0:T(1,128)S(1)} %bitcast.45, bf16[128,512]{1,0:T(8,128)(2,1)S(1)} %bitcast.28, ...), custom_call_target="tpu_custom_call" | custom-call | flops 500000000 | bytes 2500000 | tf_op jit(solution)/shard_map/prepare/pallas_call | solution.py:328
  14.5 9.4 %collective-permute-done.1.refs_3_.refs_5_ = f32[2,528,128]{2,1,0:T(8,128)S(1)} collective-permute-done((f32[2,528,128]{2,1,0:T(8,128)S(1)}, f32[2,528,128]{2,1,0:T(8,128)S(1)}, u32[]{:S(2)}, u32[]{:S(2)}) %collective-permute-start.1) | collective-permute-done | bytes 540704 | tf_op jit(solution)/shard_map/ppermute | solution.py:348
  23.9 5.5 %collective-permute-done.refs_1_.refs_4_ = f32[2,528,128]{2,1,0:T(8,128)S(1)} collective-permute-done((f32[2,528,128]{2,1,0:T(8,128)S(1)}, f32[2,528,128]{2,1,0:T(8,128)S(1)}, u32[]{:S(2)}, u32[]{:S(2)}) %collective-permute-start) | collective-permute-done | bytes 540704 | tf_op jit(solution)/shard_map/ppermute | solution.py:347
  29.4 1.1 combine.1
  30.5 3.7 %all-to-all-start = ((f32[16,136,128]{2,1,0:T(8,128)}), f32[16,136,128]{2,1,0:T(8,128)S(1)}, u32[]{:S(2)}, u32[]{:S(2)}) async-start(f32[16,136,128]{2,1,0:T(8,128)} %combine.1), calls=%async_computation | async-start | bytes 2228224 | tf_op jit(solution)/shard_map/all_to_all | solution.py:367
  34.2 1.0 copy-done.3
  35.3 1.0 copy-done.6
  36.3 0.8 copy-done.11
  37.1 0.8 copy-done.15
  37.8 2.3 %moments.1 = (f32[2048,128]{1,0:T(8,128)S(1)}, f32[2048,128]{1,0:T(8,128)S(1)}, f32[64,128]{1,0:T(8,128)S(1)}) custom-call(bf16[128,2048]{1,0:T(8,128)(2,1)S(1)} %bitcast.20, bf16[128,2048]{1,0:T(8,128)(2,1)S(1)} %bitcast.24, f32[64,128]{1,0:T(8,128)S(1)} %bitcast.41, f32[2,2,16,128]{3,2,1,0:T(8,128)S(1)} %copy-done.15, f32[1,64]{1,0:T(1,128)S(1)} %bitcast.46, ...), custom_call_target="tpu_custom_call" | custom-call | flops 1000000000 | bytes 4000000 | tf_op jit(solution)/shard_map/moments/pallas_call | solution.py:369
  40.2 1.0 copy-done
  41.1 22.5 %all-to-all-done.recv_ref = f32[16,136,128]{2,1,0:T(8,128)S(1)} async-done(((f32[16,136,128]{2,1,0:T(8,128)}), f32[16,136,128]{2,1,0:T(8,128)S(1)}, u32[]{:S(2)}, u32[]{:S(2)}) %all-to-all-start) | async-done | bytes 1114144 | tf_op jit(solution)/shard_map/all_to_all | solution.py:367
  63.6 0.1 scan.1
  63.7 31.4 %all_to_all.15.refs_1_ = f32[16,128,128]{2,1,0:T(8,128)S(1)} all-to-all(f32[16,128,128]{2,1,0:T(8,128)S(1)} %scan.1), channel_id=1, replica_groups={{0,16,32,48,64,80,96,112,128,144,160,176,192,208,224,240},{8,24,40,56,7..., dimensions={0} | all-to-all | bytes 2097152 | tf_op jit(solution)/shard_map/all_to_all | solution.py:395
  95.2 0.1 collective-permute-start.3
  95.3 5.3 %collective-permute-start.2 = (f32[16,64,128]{2,1,0:T(8,128)S(1)}, f32[16,64,128]{2,1,0:T(8,128)S(1)}, u32[]{:S(2)}, u32[]{:S(2)}) collective-permute-start(f32[16,64,128]{2,1,0:T(8,128)S(1)} %get-tuple-element.65), channel_id=1, source_target_pairs={{8,0},{16,8},{24,16},{32,24},{40,32},{48,40},{56,48},{64,56},{72,6... | collective-permute-start | bytes 1572872 | tf_op jit(solution)/shard_map/ppermute | solution.py:396
  100.6 8.6 %intra.1 = (bf16[2048,128]{1,0:T(8,128)(2,1)}, bf16[2048,128]{1,0:T(8,128)(2,1)}, f32[2048,128]{1,0:T(8,128)}, f32[128,512]{1,0:T(8,128)}, f32[128,512]{1,0:T(8,...) custom-call(bf16[128,2048]{1,0:T(8,128)(2,1)S(1)} %bitcast.21, bf16[128,2048]{1,0:T(8,128)(2,1)S(1)} %bitcast.25, ...), custom_call_target="tpu_custom_call" | custom-call | flops 4000000000 | bytes 5000000 | tf_op jit(solution)/shard_map/intra/pallas_call | solution.py:399
  109.3 1.3 collective-permute-done.3.refs_3_
  110.6 2.4 %rates.1 = (f32[64,128]{1,0:T(8,128)}, f32[32,1,128]{2,1,0:T(1,128)}, bf16[2048,128]{1,0:T(8,128)(2,1)}, bf16[2048,128]{1,0:T(8,128)(2,1)}) custom-call(s32[1]{0:T(128)} %bitcast.refs_0_.position_ref, f32[16,128,128]{2,1,0:T(8,128)S(1)} %all_to_all.15.refs_1_, f32[16,64,128]{2,1,0:T(8,128)S(1)} %collective-permute-done.2.refs_2_, ...), custom_call_target="tpu_custom_call" | custom-call | flops 10000000 | bytes 6000000 | tf_op jit(solution)/shard_map/rates/pallas_call | solution.py:415
  113.0 6.7 %all-to-all-start.2 = ((f32[32,1,128]{2,1,0:T(1,128)}), f32[32,1,128]{2,1,0:T(1,128)S(1)}, u32[]{:S(2)}, u32[]{:S(2)}) async-start(f32[32,1,128]{2,1,0:T(1,128)} %get-tuple-element.62), calls=%async_computation.2 | async-start | bytes 32768 | tf_op jit(solution)/shard_map/all_to_all | solution.py:266
  119.6 5.4 %finish.1 = (bf16[128,2048]{1,0:T(8,128)(2,1)}, bf16[128,512]{1,0:T(8,128)(2,1)}, bf16[128,512]{1,0:T(8,128)(2,1)}, f32[64,128]{1,0:T(8,128)}) custom-call(bf16[2048,128]{1,0:T(8,128)(2,1)} %get-tuple-element.48.state_low_ref, bf16[2048,128]{1,0:T(8,128)(2,1)} %get-tuple-element.49.adjoint_low_ref, f32[64,128]{1,0:T(8,128)} %get-tuple-element.50.cross_ref, ...), custom_call_target="tpu_custom_call" | custom-call | flops 1500000000 | bytes 5000000 | tf_op jit(solution)/shard_map/finish/pallas_call | solution.py:435
  125.0 4.4 %all-to-all-done.2 = f32[32,1,128]{2,1,0:T(1,128)S(1)} async-done(((f32[32,1,128]{2,1,0:T(1,128)}), f32[32,1,128]{2,1,0:T(1,128)S(1)}, u32[]{:S(2)}, u32[]{:S(2)}) %all-to-all-start.2) | async-done | bytes 16416 | tf_op jit(solution)/shard_map/all_to_all | solution.py:266
  129.6 1.1 collective-permute-done.4
  130.7 0.4 collective-permute-start.7
  131.1 1.6 %collective-permute-start.6 = (f32[1,128]{1,0:T(1,128)S(1)}, f32[1,128]{1,0:T(1,128)S(1)}, u32[]{:S(2)}, u32[]{:S(2)}) collective-permute-start(f32[1,128]{1,0:T(1,128)S(1)} %bitcast_add_fusion), channel_id=1, source_target_pairs={{0,2},{1,3},{2,4},{3,5},{4,6},{5,7},{6,0},{7,1},{8,10},{9,11},{10,... | collective-permute-start | bytes 1544 | tf_op jit(solution)/shard_map/ppermute | solution.py:271
  132.7 1.3 collective-permute-start.5
  134.0 0.2 collective-permute-done.7
  134.2 0.4 collective-permute-done.6
  134.7 3.1 %collective-permute-done.5 = f32[1,128]{1,0:T(1,128)S(1)} collective-permute-done((f32[1,128]{1,0:T(1,128)S(1)}, f32[1,128]{1,0:T(1,128)S(1)}, u32[]{:S(2)}, u32[]{:S(2)}) %collective-permute-start.5) | collective-permute-done | bytes 544 | tf_op jit(solution)/shard_map/ppermute | solution.py:271
  137.7 0.6 slice_bitcast_fusion
  (36 shorter events, 0.3 us)
Async XLA Ops:
  0.6 11.7 %copy-start.13 = (f32[1,128]{1,0:T(1,128)S(1)}, f32[1,128]{1,0:T(1,128)}, u32[]{:S(2)}) copy-start(f32[1,128]{1,0:T(1,128)} %refs_7_.3) | copy-start | bytes 1540
  0.6 11.7 %copy-start.5 = (bf16[1,128,2048]{2,1,0:T(8,128)(2,1)S(1)}, bf16[1,128,2048]{2,1,0:T(8,128)(2,1)}, u32[]{:S(2)}) copy-start(bf16[1,128,2048]{2,1,0:T(8,128)(2,1)} %param.15) | copy-start | bytes 1572868
  0.7 11.7 %copy-start.9 = (bf16[1,128,512]{2,1,0:T(8,128)(2,1)S(1)}, bf16[1,128,512]{2,1,0:T(8,128)(2,1)}, u32[]{:S(2)}) copy-start(bf16[1,128,512]{2,1,0:T(8,128)(2,1)} %param.14) | copy-start | bytes 393220
  0.7 11.7 %copy-start.8 = (bf16[1,128,512]{2,1,0:T(8,128)(2,1)S(1)}, bf16[1,128,512]{2,1,0:T(8,128)(2,1)}, u32[]{:S(2)}) copy-start(bf16[1,128,512]{2,1,0:T(8,128)(2,1)} %param.13) | copy-start | bytes 393220
  0.7 11.7 %copy-start.14 = (f32[64]{0:T(128)S(1)}, f32[64]{0:T(128)}, u32[]{:S(2)}) copy-start(f32[64]{0:T(128)} %param.11) | copy-start | bytes 772
  0.7 11.7 %copy-start.10 = (f32[1,64,128]{2,1,0:T(8,128)S(1)}, f32[1,64,128]{2,1,0:T(8,128)}, u32[]{:S(2)}) copy-start(f32[1,64,128]{2,1,0:T(8,128)} %param.9) | copy-start | bytes 98308
  0.7 11.7 %copy-start.2 = (bf16[1,128,2048]{2,1,0:T(8,128)(2,1)S(1)}, bf16[1,128,2048]{2,1,0:T(8,128)(2,1)}, u32[]{:S(2)}) copy-start(bf16[1,128,2048]{2,1,0:T(8,128)(2,1)} %param.8) | copy-start | bytes 1572868
  4.3 19.6 %collective-permute-start.1 = (f32[2,528,128]{2,1,0:T(8,128)S(1)}, f32[2,528,128]{2,1,0:T(8,128)S(1)}, u32[]{:S(2)}, u32[]{:S(2)}) collective-permute-start(f32[2,528,128]{2,1,0:T(8,128)S(1)} %get-tuple-element.37), channel_id=1, source_target_pairs={{8,0},{16,8},{24,16},{32,24},{40,32},{48,40},{56,48},{64,56},{72,6... | collective-permute-start | bytes 1622024 | tf_op jit(solution)/shard_map/ppermute | solution.py:348
  12.4 17.1 %collective-permute-start = (f32[2,528,128]{2,1,0:T(8,128)S(1)}, f32[2,528,128]{2,1,0:T(8,128)S(1)}, u32[]{:S(2)}, u32[]{:S(2)}) collective-permute-start(f32[2,528,128]{2,1,0:T(8,128)S(1)} %get-tuple-element.35), channel_id=1, source_target_pairs={{0,8},{8,16},{16,24},{24,32},{32,40},{40,48},{48,56},{56,64},{64,7... | collective-permute-start | bytes 1622024 | tf_op jit(solution)/shard_map/ppermute | solution.py:347
  30.5 33.1 %all-to-all-start = ((f32[16,136,128]{2,1,0:T(8,128)}), f32[16,136,128]{2,1,0:T(8,128)S(1)}, u32[]{:S(2)}, u32[]{:S(2)}) async-start(f32[16,136,128]{2,1,0:T(8,128)} %combine.1), calls=%async_computation | async-start | bytes 2228224 | tf_op jit(solution)/shard_map/all_to_all | solution.py:367
  34.2 1.0 copy-start.3
  35.3 1.0 copy-start.6
  36.3 0.8 copy-start.11
  37.1 0.8 copy-start.15
  40.2 1.0 copy-start
  95.1 5.5 %copy-start.4 = (bf16[1,128,2048]{2,1,0:T(8,128)(2,1)S(1)}, bf16[1,128,2048]{2,1,0:T(8,128)(2,1)}, u32[]{:S(2)}) copy-start(bf16[1,128,2048]{2,1,0:T(8,128)(2,1)} %param.8) | copy-start | bytes 1572868
  95.1 5.5 %copy-start.7 = (bf16[1,128,2048]{2,1,0:T(8,128)(2,1)S(1)}, bf16[1,128,2048]{2,1,0:T(8,128)(2,1)}, u32[]{:S(2)}) copy-start(bf16[1,128,2048]{2,1,0:T(8,128)(2,1)} %param.15) | copy-start | bytes 1572868
  95.1 5.5 %copy-start.12 = (f32[1,64,128]{2,1,0:T(8,128)S(1)}, f32[1,64,128]{2,1,0:T(8,128)}, u32[]{:S(2)}) copy-start(f32[1,64,128]{2,1,0:T(8,128)} %param.9) | copy-start | bytes 98308
  95.1 5.5 %copy-start.16 = (f32[2,2,16,128]{3,2,1,0:T(8,128)S(1)}, f32[2,2,16,128]{3,2,1,0:T(8,128)}, u32[]{:S(2)}) copy-start(f32[2,2,16,128]{3,2,1,0:T(8,128)} %get-tuple-element.41.cum_ref) | copy-start | bytes 98308
  95.2 15.4 %collective-permute-start.3 = (f32[16,64,128]{2,1,0:T(8,128)S(1)}, f32[16,64,128]{2,1,0:T(8,128)S(1)}, u32[]{:S(2)}, u32[]{:S(2)}) collective-permute-start(f32[16,64,128]{2,1,0:T(8,128)S(1)} %get-tuple-element.64), channel_id=1, source_target_pairs={{0,8},{8,16},{16,24},{24,32},{32,40},{40,48},{48,56},{56,64},{64,7... | collective-permute-start | bytes 1572872 | tf_op jit(solution)/shard_map/ppermute | solution.py:397
  95.3 15.3 %copy-start.1 = (f32[2048,128]{1,0:T(8,128)S(1)}, f32[2048,128]{1,0:T(8,128)}, u32[]{:S(2)}) copy-start(f32[2048,128]{1,0:T(8,128)} %copy-done) | copy-start | bytes 3145732
  95.3 15.3 %collective-permute-start.2 = (f32[16,64,128]{2,1,0:T(8,128)S(1)}, f32[16,64,128]{2,1,0:T(8,128)S(1)}, u32[]{:S(2)}, u32[]{:S(2)}) collective-permute-start(f32[16,64,128]{2,1,0:T(8,128)S(1)} %get-tuple-element.65), channel_id=1, source_target_pairs={{8,0},{16,8},{24,16},{32,24},{40,32},{48,40},{56,48},{64,56},{72,6... | collective-permute-start | bytes 1572872 | tf_op jit(solution)/shard_map/ppermute | solution.py:396
  113.0 16.4 %all-to-all-start.2 = ((f32[32,1,128]{2,1,0:T(1,128)}), f32[32,1,128]{2,1,0:T(1,128)S(1)}, u32[]{:S(2)}, u32[]{:S(2)}) async-start(f32[32,1,128]{2,1,0:T(1,128)} %get-tuple-element.62), calls=%async_computation.2 | async-start | bytes 32768 | tf_op jit(solution)/shard_map/all_to_all | solution.py:266
  129.5 1.2 collective-permute-start.4
  130.7 3.5 %collective-permute-start.7 = (f32[1,128]{1,0:T(1,128)S(1)}, f32[1,128]{1,0:T(1,128)S(1)}, u32[]{:S(2)}, u32[]{:S(2)}) collective-permute-start(f32[1,128]{1,0:T(1,128)S(1)} %bitcast_add_fusion), channel_id=1, source_target_pairs={{0,6},{1,7},{2,0},{3,1},{4,2},{5,3},{6,4},{7,5},{8,14},{9,15},{10,... | collective-permute-start | bytes 1544 | tf_op jit(solution)/shard_map/ppermute | solution.py:271
  131.1 3.5 %collective-permute-start.6 = (f32[1,128]{1,0:T(1,128)S(1)}, f32[1,128]{1,0:T(1,128)S(1)}, u32[]{:S(2)}, u32[]{:S(2)}) collective-permute-start(f32[1,128]{1,0:T(1,128)S(1)} %bitcast_add_fusion), channel_id=1, source_target_pairs={{0,2},{1,3},{2,4},{3,5},{4,6},{5,7},{6,0},{7,1},{8,10},{9,11},{10,... | collective-permute-start | bytes 1544 | tf_op jit(solution)/shard_map/ppermute | solution.py:271
  132.7 5.0 %collective-permute-start.5 = (f32[1,128]{1,0:T(1,128)S(1)}, f32[1,128]{1,0:T(1,128)S(1)}, u32[]{:S(2)}, u32[]{:S(2)}) collective-permute-start(f32[1,128]{1,0:T(1,128)S(1)} %bitcast_add_fusion), channel_id=1, source_target_pairs={{0,4},{1,5},{2,6},{3,7},{4,0},{5,1},{6,2},{7,3},{8,12},{9,13},{10,... | collective-permute-start | bytes 1544 | tf_op jit(solution)/shard_map/ppermute | solution.py:271

commit v10 on v9

--- a/solution.py
+++ b/solution.py
@@ -348,7 +348,7 @@
     recv_seed = lax.ppermute(second_seeds, "seq", back)
     second_states, first_seeds = prepare(1)
 
-    recv_seed, later_cum = lax.optimization_barrier((recv_seed, cum))
+    recv_state, later_cum = lax.optimization_barrier((recv_state, cum))
 
     slot = 2 * half + 8
     send = pl.pallas_call(

time: 140 us -> 137 us (0.979)
  blocking collectives: 31.4 us -> 24.4 us
  starting transfers between devices: 27.2 us -> 32.1 us
    ppermute x1, waiting for transfers between devices: 9.41 us -> 0.01 us  [on_device(): recv_seed = lax.ppermute(second_seeds, 'seq', back)]
    ppermute x1, starting transfers between devices: 0.08 us -> 7.48 us  [on_device(): adjoint_in = lax.ppermute(carries[:, half:], 'seq', around)]
    all_to_all x1, blocking collectives: 31.4 us -> 24.4 us  [on_device(): carries = lax.all_to_all(scanned, 'seq', 0, 0, axis_index_groups=parities)]
    ppermute x1, starting transfers between devices: 5.32 us -> 0.39 us  [on_device(): state_in = lax.ppermute(carries[:, :half], 'seq', back)]
    ppermute x1, waiting for transfers between devices: 5.52 us -> 10.1 us  [on_device(): recv_state = lax.ppermute(first_states, 'seq', around)]
    all_to_all x1, starting transfers between devices: 3.7 us -> 5.93 us  [on_device(): recv = lax.all_to_all(send, 'seq', 0, 0, axis_index_groups=parities)]
    ppermute x1, waiting for transfers between devices: 1.32 us -> 3.35 us  [on_device(): adjoint_in = lax.ppermute(carries[:, half:], 'seq', around)]
    all_to_all x1, waiting for transfers between devices: 22.5 us -> 24.4 us  [on_device(): recv = lax.all_to_all(send, 'seq', 0, 0, axis_index_groups=parities)]
  transfers between devices with their start and end apart: 10 -> 10, of which waited for: 9 -> 8; matrix products, arithmetic and copies ran while one was open for 0% -> 0% of each run, Pallas kernels for 13% -> 14%
where the time goes in v10:
time: 137 us; the launch traced here: 135 us
  waiting for transfers between devices  47.1 us (34%)
  starting transfers between devices  32.1 us (23%)
  Pallas kernels  25.5 us (19%)
  blocking collectives  24.4 us (18%)
  local copies, waits for them, and re-layouts  5.28 us (4%)
    all_to_all x1, waiting for transfers between devices, on_device(): recv = lax.all_to_all(send, 'seq', 0, 0, axis_index_groups=parities)  24.4 us
    all_to_all x1, blocking collectives, on_device(): carries = lax.all_to_all(scanned, 'seq', 0, 0, axis_index_groups=parities)  24.4 us
    ppermute x1, waiting for transfers between devices, on_device(): recv_state = lax.ppermute(first_states, 'seq', around)  10.1 us
    pallas_call x1, Pallas kernels, on_device(): pl.pallas_call(intra_kernel, grid=(G,), in_specs=[block(*tokens), block(*...  8.61 us
    ppermute x1, starting transfers between devices, on_device(): adjoint_in = lax.ppermute(carries[:, half:], 'seq', around)  7.48 us
    all_to_all x1, starting transfers between devices, total_over_devices(): lax.all_to_all(copies, 'seq', 0, 0)  6.74 us
    ppermute x1, starting transfers between devices, on_device(): recv_seed = lax.ppermute(second_seeds, 'seq', back)  6.22 us
    all_to_all x1, starting transfers between devices, on_device(): recv = lax.all_to_all(send, 'seq', 0, 0, axis_index_groups=parities)  5.93 us
  transfers between devices with their start and end apart: 10, of which 8 were waited for; matrix products, arithmetic and copies ran while one was open for 0% of the time, Pallas kernels for 14%

profile of v10, /device:TPU:16, one launch (start us, length us, event | category | flops | bytes accessed | tf_op | source)
XLA Modules:
  0.0 135.3 jit_solution(1198804550701917339)
XLA Ops:
  0.7 3.6 %prepare.2 = (f32[2,528,128]{2,1,0:T(8,128)S(1)}, f32[2,528,128]{2,1,0:T(8,128)S(1)}, f32[2,2,16,128]{3,2,1,0:T(8,128)}) custom-call(s32[1]{0:T(128)} %bitcast.refs_0_.position_ref, bf16[128,2048]{1,0:T(8,128)(2,1)} %bitcast.18, f32[64,128]{1,0:T(8,128)} %bitcast.36, f32[1,64]{1,0:T(1,128)} %bitcast.43, bf16[128,512]{1,0:T(8,128)(2,1)} %bitcast.26, ...), custom_call_target="tpu_custom_call" | custom-call | flops 500000000 | bytes 2500000 | tf_op jit(solution)/shard_map/prepare/pallas_call | solution.py:328
  4.3 1.9 %collective-permute-start = (f32[2,528,128]{2,1,0:T(8,128)S(1)}, f32[2,528,128]{2,1,0:T(8,128)S(1)}, u32[]{:S(2)}, u32[]{:S(2)}) collective-permute-start(f32[2,528,128]{2,1,0:T(8,128)S(1)} %get-tuple-element.35), channel_id=1, source_target_pairs={{0,8},{8,16},{16,24},{24,32},{32,40},{40,48},{48,56},{56,64},{64,7... | collective-permute-start | bytes 1622024 | tf_op jit(solution)/shard_map/ppermute | solution.py:347
  6.2 6.2 %collective-permute-start.1 = (f32[2,528,128]{2,1,0:T(8,128)S(1)}, f32[2,528,128]{2,1,0:T(8,128)S(1)}, u32[]{:S(2)}, u32[]{:S(2)}) collective-permute-start(f32[2,528,128]{2,1,0:T(8,128)S(1)} %get-tuple-element.39), channel_id=1, source_target_pairs={{8,0},{16,8},{24,16},{32,24},{40,32},{48,40},{56,48},{64,56},{72,6... | collective-permute-start | bytes 1622024 | tf_op jit(solution)/shard_map/ppermute | solution.py:348
  12.5 2.1 %prepare.3 = (f32[2,528,128]{2,1,0:T(8,128)S(1)}, f32[2,528,128]{2,1,0:T(8,128)S(1)}) custom-call(s32[1]{0:T(128)} %bitcast.refs_0_.position_ref, bf16[128,2048]{1,0:T(8,128)(2,1)S(1)} %bitcast.19, f32[64,128]{1,0:T(8,128)S(1)} %bitcast.39, f32[1,64]{1,0:T(1,128)S(1)} %bitcast.45, bf16[128,512]{1,0:T(8,128)(2,1)S(1)} %bitcast.28, ...), custom_call_target="tpu_custom_call" | custom-call | flops 500000000 | bytes 2500000 | tf_op jit(solution)/shard_map/prepare/pallas_call | solution.py:328
  14.6 10.1 %collective-permute-done.refs_1_.refs_4_ = f32[2,528,128]{2,1,0:T(8,128)S(1)} collective-permute-done((f32[2,528,128]{2,1,0:T(8,128)S(1)}, f32[2,528,128]{2,1,0:T(8,128)S(1)}, u32[]{:S(2)}, u32[]{:S(2)}) %collective-permute-start) | collective-permute-done | bytes 540704 | tf_op jit(solution)/shard_map/ppermute | solution.py:347
  24.6 1.1 combine.1
  25.7 5.9 %all-to-all-start = ((f32[16,136,128]{2,1,0:T(8,128)}), f32[16,136,128]{2,1,0:T(8,128)S(1)}, u32[]{:S(2)}, u32[]{:S(2)}) async-start(f32[16,136,128]{2,1,0:T(8,128)} %combine.1), calls=%async_computation | async-start | bytes 2228224 | tf_op jit(solution)/shard_map/all_to_all | solution.py:367
  31.7 1.0 copy-done.3
  32.7 1.0 copy-done.6
  33.8 0.8 copy-done.11
  34.5 0.8 copy-done.15
  35.3 2.3 %moments.1 = (f32[2048,128]{1,0:T(8,128)S(1)}, f32[2048,128]{1,0:T(8,128)S(1)}, f32[64,128]{1,0:T(8,128)S(1)}) custom-call(bf16[128,2048]{1,0:T(8,128)(2,1)S(1)} %bitcast.20, bf16[128,2048]{1,0:T(8,128)(2,1)S(1)} %bitcast.24, f32[64,128]{1,0:T(8,128)S(1)} %bitcast.41, f32[2,2,16,128]{3,2,1,0:T(8,128)S(1)} %copy-done.15, f32[1,64]{1,0:T(1,128)S(1)} %bitcast.46, ...), custom_call_target="tpu_custom_call" | custom-call | flops 1000000000 | bytes 4000000 | tf_op jit(solution)/shard_map/moments/pallas_call | solution.py:369
  37.6 1.0 copy-done
  38.6 24.4 %all-to-all-done.recv_ref = f32[16,136,128]{2,1,0:T(8,128)S(1)} async-done(((f32[16,136,128]{2,1,0:T(8,128)}), f32[16,136,128]{2,1,0:T(8,128)S(1)}, u32[]{:S(2)}, u32[]{:S(2)}) %all-to-all-start) | async-done | bytes 1114144 | tf_op jit(solution)/shard_map/all_to_all | solution.py:367
  63.0 0.1 scan.1
  63.2 24.4 %all_to_all.15.refs_1_ = f32[16,128,128]{2,1,0:T(8,128)S(1)} all-to-all(f32[16,128,128]{2,1,0:T(8,128)S(1)} %scan.1), channel_id=1, replica_groups={{0,16,32,48,64,80,96,112,128,144,160,176,192,208,224,240},{8,24,40,56,7..., dimensions={0} | all-to-all | bytes 2097152 | tf_op jit(solution)/shard_map/all_to_all | solution.py:395
  87.6 7.5 %collective-permute-start.3 = (f32[16,64,128]{2,1,0:T(8,128)S(1)}, f32[16,64,128]{2,1,0:T(8,128)S(1)}, u32[]{:S(2)}, u32[]{:S(2)}) collective-permute-start(f32[16,64,128]{2,1,0:T(8,128)S(1)} %get-tuple-element.64), channel_id=1, source_target_pairs={{0,8},{8,16},{16,24},{24,32},{32,40},{40,48},{48,56},{56,64},{64,7... | collective-permute-start | bytes 1572872 | tf_op jit(solution)/shard_map/ppermute | solution.py:397
  95.1 0.4 collective-permute-start.2
  95.5 8.6 %intra.1 = (bf16[2048,128]{1,0:T(8,128)(2,1)}, bf16[2048,128]{1,0:T(8,128)(2,1)}, f32[2048,128]{1,0:T(8,128)}, f32[128,512]{1,0:T(8,128)}, f32[128,512]{1,0:T(8,...) custom-call(bf16[128,2048]{1,0:T(8,128)(2,1)S(1)} %bitcast.21, bf16[128,2048]{1,0:T(8,128)(2,1)S(1)} %bitcast.25, ...), custom_call_target="tpu_custom_call" | custom-call | flops 4000000000 | bytes 5000000 | tf_op jit(solution)/shard_map/intra/pallas_call | solution.py:399
  104.1 3.3 %collective-permute-done.3.refs_3_ = f32[16,64,128]{2,1,0:T(8,128)S(1)} collective-permute-done((f32[16,64,128]{2,1,0:T(8,128)S(1)}, f32[16,64,128]{2,1,0:T(8,128)S(1)}, u32[]{:S(2)}, u32[]{:S(2)}) %collective-permute-start.3) | collective-permute-done | bytes 524320 | tf_op jit(solution)/shard_map/ppermute | solution.py:397
  107.5 2.4 %rates.1 = (f32[64,128]{1,0:T(8,128)}, f32[32,1,128]{2,1,0:T(1,128)}, bf16[2048,128]{1,0:T(8,128)(2,1)}, bf16[2048,128]{1,0:T(8,128)(2,1)}) custom-call(s32[1]{0:T(128)} %bitcast.refs_0_.position_ref, f32[16,128,128]{2,1,0:T(8,128)S(1)} %all_to_all.15.refs_1_, f32[16,64,128]{2,1,0:T(8,128)S(1)} %collective-permute-done.2.refs_2_, ...), custom_call_target="tpu_custom_call" | custom-call | flops 10000000 | bytes 6000000 | tf_op jit(solution)/shard_map/rates/pallas_call | solution.py:415
  109.8 6.7 %all-to-all-start.2 = ((f32[32,1,128]{2,1,0:T(1,128)}), f32[32,1,128]{2,1,0:T(1,128)S(1)}, u32[]{:S(2)}, u32[]{:S(2)}) async-start(f32[32,1,128]{2,1,0:T(1,128)} %get-tuple-element.62), calls=%async_computation.2 | async-start | bytes 32768 | tf_op jit(solution)/shard_map/all_to_all | solution.py:266
  116.6 5.4 %finish.1 = (bf16[128,2048]{1,0:T(8,128)(2,1)}, bf16[128,512]{1,0:T(8,128)(2,1)}, bf16[128,512]{1,0:T(8,128)(2,1)}, f32[64,128]{1,0:T(8,128)}) custom-call(bf16[2048,128]{1,0:T(8,128)(2,1)} %get-tuple-element.48.state_low_ref, bf16[2048,128]{1,0:T(8,128)(2,1)} %get-tuple-element.49.adjoint_low_ref, f32[64,128]{1,0:T(8,128)} %get-tuple-element.50.cross_ref, ...), custom_call_target="tpu_custom_call" | custom-call | flops 1500000000 | bytes 5000000 | tf_op jit(solution)/shard_map/finish/pallas_call | solution.py:435
  122.0 4.4 %all-to-all-done.2 = f32[32,1,128]{2,1,0:T(1,128)S(1)} async-done(((f32[32,1,128]{2,1,0:T(1,128)}), f32[32,1,128]{2,1,0:T(1,128)S(1)}, u32[]{:S(2)}, u32[]{:S(2)}) %all-to-all-start.2) | async-done | bytes 16416 | tf_op jit(solution)/shard_map/all_to_all | solution.py:266
  126.5 1.1 collective-permute-done.4
  127.6 0.4 collective-permute-start.7
  128.1 1.6 %collective-permute-start.6 = (f32[1,128]{1,0:T(1,128)S(1)}, f32[1,128]{1,0:T(1,128)S(1)}, u32[]{:S(2)}, u32[]{:S(2)}) collective-permute-start(f32[1,128]{1,0:T(1,128)S(1)} %bitcast_add_fusion), channel_id=1, source_target_pairs={{0,2},{1,3},{2,4},{3,5},{4,6},{5,7},{6,0},{7,1},{8,10},{9,11},{10,... | collective-permute-start | bytes 1544 | tf_op jit(solution)/shard_map/ppermute | solution.py:271
  129.7 1.3 collective-permute-start.5
  131.0 0.2 collective-permute-done.7
  131.2 0.4 collective-permute-done.6
  131.6 3.1 %collective-permute-done.5 = f32[1,128]{1,0:T(1,128)S(1)} collective-permute-done((f32[1,128]{1,0:T(1,128)S(1)}, f32[1,128]{1,0:T(1,128)S(1)}, u32[]{:S(2)}, u32[]{:S(2)}) %collective-permute-start.5) | collective-permute-done | bytes 544 | tf_op jit(solution)/shard_map/ppermute | solution.py:271
  134.7 0.6 slice_bitcast_fusion
  (36 shorter events, 0.3 us)
Async XLA Ops:
  0.6 11.8 %copy-start.13 = (f32[1,128]{1,0:T(1,128)S(1)}, f32[1,128]{1,0:T(1,128)}, u32[]{:S(2)}) copy-start(f32[1,128]{1,0:T(1,128)} %refs_7_.3) | copy-start | bytes 1540
  0.6 11.8 %copy-start.5 = (bf16[1,128,2048]{2,1,0:T(8,128)(2,1)S(1)}, bf16[1,128,2048]{2,1,0:T(8,128)(2,1)}, u32[]{:S(2)}) copy-start(bf16[1,128,2048]{2,1,0:T(8,128)(2,1)} %param.15) | copy-start | bytes 1572868
  0.7 11.8 %copy-start.9 = (bf16[1,128,512]{2,1,0:T(8,128)(2,1)S(1)}, bf16[1,128,512]{2,1,0:T(8,128)(2,1)}, u32[]{:S(2)}) copy-start(bf16[1,128,512]{2,1,0:T(8,128)(2,1)} %param.14) | copy-start | bytes 393220
  0.7 11.8 %copy-start.8 = (bf16[1,128,512]{2,1,0:T(8,128)(2,1)S(1)}, bf16[1,128,512]{2,1,0:T(8,128)(2,1)}, u32[]{:S(2)}) copy-start(bf16[1,128,512]{2,1,0:T(8,128)(2,1)} %param.13) | copy-start | bytes 393220
  0.7 11.8 %copy-start.14 = (f32[64]{0:T(128)S(1)}, f32[64]{0:T(128)}, u32[]{:S(2)}) copy-start(f32[64]{0:T(128)} %param.11) | copy-start | bytes 772
  0.7 11.8 %copy-start.10 = (f32[1,64,128]{2,1,0:T(8,128)S(1)}, f32[1,64,128]{2,1,0:T(8,128)}, u32[]{:S(2)}) copy-start(f32[1,64,128]{2,1,0:T(8,128)} %param.9) | copy-start | bytes 98308
  0.7 11.8 %copy-start.2 = (bf16[1,128,2048]{2,1,0:T(8,128)(2,1)S(1)}, bf16[1,128,2048]{2,1,0:T(8,128)(2,1)}, u32[]{:S(2)}) copy-start(bf16[1,128,2048]{2,1,0:T(8,128)(2,1)} %param.8) | copy-start | bytes 1572868
  4.3 20.3 %collective-permute-start = (f32[2,528,128]{2,1,0:T(8,128)S(1)}, f32[2,528,128]{2,1,0:T(8,128)S(1)}, u32[]{:S(2)}, u32[]{:S(2)}) collective-permute-start(f32[2,528,128]{2,1,0:T(8,128)S(1)} %get-tuple-element.35), channel_id=1, source_target_pairs={{0,8},{8,16},{16,24},{24,32},{32,40},{40,48},{48,56},{56,64},{64,7... | collective-permute-start | bytes 1622024 | tf_op jit(solution)/shard_map/ppermute | solution.py:347
  6.2 18.4 %collective-permute-start.1 = (f32[2,528,128]{2,1,0:T(8,128)S(1)}, f32[2,528,128]{2,1,0:T(8,128)S(1)}, u32[]{:S(2)}, u32[]{:S(2)}) collective-permute-start(f32[2,528,128]{2,1,0:T(8,128)S(1)} %get-tuple-element.39), channel_id=1, source_target_pairs={{8,0},{16,8},{24,16},{32,24},{40,32},{48,40},{56,48},{64,56},{72,6... | collective-permute-start | bytes 1622024 | tf_op jit(solution)/shard_map/ppermute | solution.py:348
  25.7 37.3 %all-to-all-start = ((f32[16,136,128]{2,1,0:T(8,128)}), f32[16,136,128]{2,1,0:T(8,128)S(1)}, u32[]{:S(2)}, u32[]{:S(2)}) async-start(f32[16,136,128]{2,1,0:T(8,128)} %combine.1), calls=%async_computation | async-start | bytes 2228224 | tf_op jit(solution)/shard_map/all_to_all | solution.py:367
  31.7 1.0 copy-start.3
  32.7 1.0 copy-start.6
  33.8 0.8 copy-start.11
  34.5 0.8 copy-start.15
  37.6 1.0 copy-start
  87.5 8.0 %copy-start.4 = (bf16[1,128,2048]{2,1,0:T(8,128)(2,1)S(1)}, bf16[1,128,2048]{2,1,0:T(8,128)(2,1)}, u32[]{:S(2)}) copy-start(bf16[1,128,2048]{2,1,0:T(8,128)(2,1)} %param.8) | copy-start | bytes 1572868
  87.5 8.0 %copy-start.7 = (bf16[1,128,2048]{2,1,0:T(8,128)(2,1)S(1)}, bf16[1,128,2048]{2,1,0:T(8,128)(2,1)}, u32[]{:S(2)}) copy-start(bf16[1,128,2048]{2,1,0:T(8,128)(2,1)} %param.15) | copy-start | bytes 1572868
  87.5 8.0 %copy-start.12 = (f32[1,64,128]{2,1,0:T(8,128)S(1)}, f32[1,64,128]{2,1,0:T(8,128)}, u32[]{:S(2)}) copy-start(f32[1,64,128]{2,1,0:T(8,128)} %param.9) | copy-start | bytes 98308
  87.5 8.0 %copy-start.16 = (f32[2,2,16,128]{3,2,1,0:T(8,128)S(1)}, f32[2,2,16,128]{3,2,1,0:T(8,128)}, u32[]{:S(2)}) copy-start(f32[2,2,16,128]{3,2,1,0:T(8,128)} %get-tuple-element.41.cum_ref) | copy-start | bytes 98308
  87.6 19.8 %collective-permute-start.3 = (f32[16,64,128]{2,1,0:T(8,128)S(1)}, f32[16,64,128]{2,1,0:T(8,128)S(1)}, u32[]{:S(2)}, u32[]{:S(2)}) collective-permute-start(f32[16,64,128]{2,1,0:T(8,128)S(1)} %get-tuple-element.64), channel_id=1, source_target_pairs={{0,8},{8,16},{16,24},{24,32},{32,40},{40,48},{48,56},{56,64},{64,7... | collective-permute-start | bytes 1572872 | tf_op jit(solution)/shard_map/ppermute | solution.py:397
  95.1 12.4 %copy-start.1 = (f32[2048,128]{1,0:T(8,128)S(1)}, f32[2048,128]{1,0:T(8,128)}, u32[]{:S(2)}) copy-start(f32[2048,128]{1,0:T(8,128)} %copy-done) | copy-start | bytes 3145732
  95.1 12.4 %collective-permute-start.2 = (f32[16,64,128]{2,1,0:T(8,128)S(1)}, f32[16,64,128]{2,1,0:T(8,128)S(1)}, u32[]{:S(2)}, u32[]{:S(2)}) collective-permute-start(f32[16,64,128]{2,1,0:T(8,128)S(1)} %get-tuple-element.65), channel_id=1, source_target_pairs={{8,0},{16,8},{24,16},{32,24},{40,32},{48,40},{56,48},{64,56},{72,6... | collective-permute-start | bytes 1572872 | tf_op jit(solution)/shard_map/ppermute | solution.py:396
  109.8 16.5 %all-to-all-start.2 = ((f32[32,1,128]{2,1,0:T(1,128)}), f32[32,1,128]{2,1,0:T(1,128)S(1)}, u32[]{:S(2)}, u32[]{:S(2)}) async-start(f32[32,1,128]{2,1,0:T(1,128)} %get-tuple-element.62), calls=%async_computation.2 | async-start | bytes 32768 | tf_op jit(solution)/shard_map/all_to_all | solution.py:266
  126.4 1.2 collective-permute-start.4
  127.6 3.5 %collective-permute-start.7 = (f32[1,128]{1,0:T(1,128)S(1)}, f32[1,128]{1,0:T(1,128)S(1)}, u32[]{:S(2)}, u32[]{:S(2)}) collective-permute-start(f32[1,128]{1,0:T(1,128)S(1)} %bitcast_add_fusion), channel_id=1, source_target_pairs={{0,6},{1,7},{2,0},{3,1},{4,2},{5,3},{6,4},{7,5},{8,14},{9,15},{10,... | collective-permute-start | bytes 1544 | tf_op jit(solution)/shard_map/ppermute | solution.py:271
  128.1 3.5 %collective-permute-start.6 = (f32[1,128]{1,0:T(1,128)S(1)}, f32[1,128]{1,0:T(1,128)S(1)}, u32[]{:S(2)}, u32[]{:S(2)}) collective-permute-start(f32[1,128]{1,0:T(1,128)S(1)} %bitcast_add_fusion), channel_id=1, source_target_pairs={{0,2},{1,3},{2,4},{3,5},{4,6},{5,7},{6,0},{7,1},{8,10},{9,11},{10,... | collective-permute-start | bytes 1544 | tf_op jit(solution)/shard_map/ppermute | solution.py:271
  129.7 5.0 %collective-permute-start.5 = (f32[1,128]{1,0:T(1,128)S(1)}, f32[1,128]{1,0:T(1,128)S(1)}, u32[]{:S(2)}, u32[]{:S(2)}) collective-permute-start(f32[1,128]{1,0:T(1,128)S(1)} %bitcast_add_fusion), channel_id=1, source_target_pairs={{0,4},{1,5},{2,6},{3,7},{4,0},{5,1},{6,2},{7,3},{8,12},{9,13},{10,... | collective-permute-start | bytes 1544 | tf_op jit(solution)/shard_map/ppermute | solution.py:271

commit v11 on v10

--- a/solution.py
+++ b/solution.py
@@ -195,7 +195,7 @@
     accumulate(sums_ref, jnp.zeros(sums_ref.shape, f32), parts)
 
 
-def rates_kernel(position_ref, carry_ref, state_in_ref, adjoint_in_ref, recv_state_ref, recv_seed_ref,
+def rates_kernel(position_ref, carry_ref, adjoint_in_ref, state_in_ref, recv_state_ref, recv_seed_ref,
                  state_moment_ref, adjoint_moment_ref, cross_weight_ref, sums_in_ref,
                  cross_ref, sums_ref, state_low_ref, adjoint_low_ref,
                  state_scratch, adjoint_scratch, sums_scratch, *, blocks):
@@ -419,7 +419,7 @@
             grid=(G,),
             in_specs=[
                 block((owners, 2 * half, N), lambda s: (lax.rem(s, PG), 0, 0)),
-                stepped((owners, half, N), 0), stepped((owners, half, N), 1),
+                stepped((owners, half, N), 1), stepped((owners, half, N), 0),
                 stepped((1, MSG, N), 1), stepped((1, MSG, N), 0),
                 ordered(*low_rows), ordered(*low_rows), ordered((K, N), lambda g: (g, 0)), sums_row],
             out_specs=[ordered((K, N), lambda g: (g, 0)), block((blocks, 1, 2 * H), lambda s: (0, 0, 0)),
@@ -430,7 +430,7 @@
         compiler_params=small,
         cost_estimate=pl.CostEstimate(flops=10_000_000, bytes_accessed=6_000_000, transcendentals=0),
         name="rates",
-    )(position, carries, state_in, adjoint_in, recv_state, recv_seed, state_moment, adjoint_moment, cross_weight, sums)
+    )(position, carries, adjoint_in, state_in, recv_state, recv_seed, state_moment, adjoint_moment, cross_weight, sums)
 
     d_inputs, d_keys, d_queries, d_steps = pl.pallas_call(
         finish_kernel,

time: 137 us -> 139 us (1.015)
  waiting for transfers between devices: 47.1 us -> 52 us
  starting transfers between devices: 32.1 us -> 29.1 us
    ppermute x1, starting transfers between devices: 7.48 us -> 0.01 us  [on_device(): adjoint_in = lax.ppermute(carries[:, half:], 'seq', around)]
    ppermute x1, starting transfers between devices: 0.39 us -> 7.78 us  [on_device(): state_in = lax.ppermute(carries[:, :half], 'seq', back)]
    all_to_all x1, starting transfers between devices: 6.74 us -> 3.83 us  [total_over_devices(): lax.all_to_all(copies, 'seq', 0, 0)]
    ppermute x1, waiting for transfers between devices: 0.01 us -> 2.69 us  [on_device(): state_in = lax.ppermute(carries[:, :half], 'seq', back)]
    ppermute x1, waiting for transfers between devices: 3.35 us -> 5.52 us  [on_device(): adjoint_in = lax.ppermute(carries[:, half:], 'seq', around)]
  transfers between devices with their start and end apart: 10 -> 10, of which waited for: 8 -> 9; matrix products, arithmetic and copies ran while one was open for 0% -> 0% of each run, Pallas kernels for 14% -> 13%
where the time goes in v11:
time: 139 us; the launch traced here: 137 us
  waiting for transfers between devices  52 us (37%)
  starting transfers between devices  29.1 us (21%)
  Pallas kernels  25.5 us (18%)
  blocking collectives  24.4 us (18%)
  local copies, waits for them, and re-layouts  5.28 us (4%)
    all_to_all x1, waiting for transfers between devices, on_device(): recv = lax.all_to_all(send, 'seq', 0, 0, axis_index_groups=parities)  24.4 us
    all_to_all x1, blocking collectives, on_device(): carries = lax.all_to_all(scanned, 'seq', 0, 0, axis_index_groups=parities)  24.4 us
    ppermute x1, waiting for transfers between devices, on_device(): recv_state = lax.ppermute(first_states, 'seq', around)  10.1 us
    pallas_call x1, Pallas kernels, on_device(): pl.pallas_call(intra_kernel, grid=(G,), in_specs=[block(*tokens), block(*...  8.61 us
    ppermute x1, starting transfers between devices, on_device(): state_in = lax.ppermute(carries[:, :half], 'seq', back)  7.78 us
    ppermute x1, starting transfers between devices, on_device(): recv_seed = lax.ppermute(second_seeds, 'seq', back)  6.22 us
    all_to_all x1, starting transfers between devices, on_device(): recv = lax.all_to_all(send, 'seq', 0, 0, axis_index_groups=parities)  5.93 us
    pallas_call x2, Pallas kernels, prepare(): pl.pallas_call(lambda *refs: prepare_kernel(first, *refs), grid_spec=pltp...  5.66 us
  transfers between devices with their start and end apart: 10, of which 9 were waited for; matrix products, arithmetic and copies ran while one was open for 0% of the time, Pallas kernels for 13%

profile of v11, /device:TPU:16, one launch (start us, length us, event | category | flops | bytes accessed | tf_op | source)
XLA Modules:
  0.0 137.1 jit_solution(13379601965344964360)
XLA Ops:
  0.7 3.6 %prepare.2 = (f32[2,528,128]{2,1,0:T(8,128)S(1)}, f32[2,528,128]{2,1,0:T(8,128)S(1)}, f32[2,2,16,128]{3,2,1,0:T(8,128)}) custom-call(s32[1]{0:T(128)} %bitcast.refs_0_.position_ref, bf16[128,2048]{1,0:T(8,128)(2,1)} %bitcast.18, f32[64,128]{1,0:T(8,128)} %bitcast.36, f32[1,64]{1,0:T(1,128)} %bitcast.43, bf16[128,512]{1,0:T(8,128)(2,1)} %bitcast.26, ...), custom_call_target="tpu_custom_call" | custom-call | flops 500000000 | bytes 2500000 | tf_op jit(solution)/shard_map/prepare/pallas_call | solution.py:328
  4.3 1.9 %collective-permute-start = (f32[2,528,128]{2,1,0:T(8,128)S(1)}, f32[2,528,128]{2,1,0:T(8,128)S(1)}, u32[]{:S(2)}, u32[]{:S(2)}) collective-permute-start(f32[2,528,128]{2,1,0:T(8,128)S(1)} %get-tuple-element.35), channel_id=1, source_target_pairs={{0,8},{8,16},{16,24},{24,32},{32,40},{40,48},{48,56},{56,64},{64,7... | collective-permute-start | bytes 1622024 | tf_op jit(solution)/shard_map/ppermute | solution.py:347
  6.2 6.2 %collective-permute-start.1 = (f32[2,528,128]{2,1,0:T(8,128)S(1)}, f32[2,528,128]{2,1,0:T(8,128)S(1)}, u32[]{:S(2)}, u32[]{:S(2)}) collective-permute-start(f32[2,528,128]{2,1,0:T(8,128)S(1)} %get-tuple-element.39), channel_id=1, source_target_pairs={{8,0},{16,8},{24,16},{32,24},{40,32},{48,40},{56,48},{64,56},{72,6... | collective-permute-start | bytes 1622024 | tf_op jit(solution)/shard_map/ppermute | solution.py:348
  12.5 2.1 %prepare.3 = (f32[2,528,128]{2,1,0:T(8,128)S(1)}, f32[2,528,128]{2,1,0:T(8,128)S(1)}) custom-call(s32[1]{0:T(128)} %bitcast.refs_0_.position_ref, bf16[128,2048]{1,0:T(8,128)(2,1)S(1)} %bitcast.19, f32[64,128]{1,0:T(8,128)S(1)} %bitcast.39, f32[1,64]{1,0:T(1,128)S(1)} %bitcast.45, bf16[128,512]{1,0:T(8,128)(2,1)S(1)} %bitcast.28, ...), custom_call_target="tpu_custom_call" | custom-call | flops 500000000 | bytes 2500000 | tf_op jit(solution)/shard_map/prepare/pallas_call | solution.py:328
  14.6 10.1 %collective-permute-done.refs_1_.refs_4_ = f32[2,528,128]{2,1,0:T(8,128)S(1)} collective-permute-done((f32[2,528,128]{2,1,0:T(8,128)S(1)}, f32[2,528,128]{2,1,0:T(8,128)S(1)}, u32[]{:S(2)}, u32[]{:S(2)}) %collective-permute-start) | collective-permute-done | bytes 540704 | tf_op jit(solution)/shard_map/ppermute | solution.py:347
  24.6 1.1 combine.1
  25.7 5.9 %all-to-all-start = ((f32[16,136,128]{2,1,0:T(8,128)}), f32[16,136,128]{2,1,0:T(8,128)S(1)}, u32[]{:S(2)}, u32[]{:S(2)}) async-start(f32[16,136,128]{2,1,0:T(8,128)} %combine.1), calls=%async_computation | async-start | bytes 2228224 | tf_op jit(solution)/shard_map/all_to_all | solution.py:367
  31.7 1.0 copy-done.3
  32.7 1.0 copy-done.6
  33.8 0.8 copy-done.11
  34.5 0.8 copy-done.15
  35.3 2.3 %moments.1 = (f32[2048,128]{1,0:T(8,128)S(1)}, f32[2048,128]{1,0:T(8,128)S(1)}, f32[64,128]{1,0:T(8,128)S(1)}) custom-call(bf16[128,2048]{1,0:T(8,128)(2,1)S(1)} %bitcast.20, bf16[128,2048]{1,0:T(8,128)(2,1)S(1)} %bitcast.24, f32[64,128]{1,0:T(8,128)S(1)} %bitcast.41, f32[2,2,16,128]{3,2,1,0:T(8,128)S(1)} %copy-done.15, f32[1,64]{1,0:T(1,128)S(1)} %bitcast.46, ...), custom_call_target="tpu_custom_call" | custom-call | flops 1000000000 | bytes 4000000 | tf_op jit(solution)/shard_map/moments/pallas_call | solution.py:369
  37.6 1.0 copy-done
  38.6 24.4 %all-to-all-done.recv_ref = f32[16,136,128]{2,1,0:T(8,128)S(1)} async-done(((f32[16,136,128]{2,1,0:T(8,128)}), f32[16,136,128]{2,1,0:T(8,128)S(1)}, u32[]{:S(2)}, u32[]{:S(2)}) %all-to-all-start) | async-done | bytes 1114144 | tf_op jit(solution)/shard_map/all_to_all | solution.py:367
  63.0 0.1 scan.1
  63.2 24.4 %all_to_all.15.refs_1_ = f32[16,128,128]{2,1,0:T(8,128)S(1)} all-to-all(f32[16,128,128]{2,1,0:T(8,128)S(1)} %scan.1), channel_id=1, replica_groups={{0,16,32,48,64,80,96,112,128,144,160,176,192,208,224,240},{8,24,40,56,7..., dimensions={0} | all-to-all | bytes 2097152 | tf_op jit(solution)/shard_map/all_to_all | solution.py:395
  87.6 7.8 %collective-permute-start.3 = (f32[16,64,128]{2,1,0:T(8,128)S(1)}, f32[16,64,128]{2,1,0:T(8,128)S(1)}, u32[]{:S(2)}, u32[]{:S(2)}) collective-permute-start(f32[16,64,128]{2,1,0:T(8,128)S(1)} %get-tuple-element.64), channel_id=1, source_target_pairs={{8,0},{16,8},{24,16},{32,24},{40,32},{48,40},{56,48},{64,56},{72,6... | collective-permute-start | bytes 1572872 | tf_op jit(solution)/shard_map/ppermute | solution.py:396
  95.4 8.6 %intra.1 = (bf16[2048,128]{1,0:T(8,128)(2,1)}, bf16[2048,128]{1,0:T(8,128)(2,1)}, f32[2048,128]{1,0:T(8,128)}, f32[128,512]{1,0:T(8,128)}, f32[128,512]{1,0:T(8,...) custom-call(bf16[128,2048]{1,0:T(8,128)(2,1)S(1)} %bitcast.21, bf16[128,2048]{1,0:T(8,128)(2,1)S(1)} %bitcast.25, ...), custom_call_target="tpu_custom_call" | custom-call | flops 4000000000 | bytes 5000000 | tf_op jit(solution)/shard_map/intra/pallas_call | solution.py:399
  104.0 2.7 %collective-permute-done.3.refs_3_ = f32[16,64,128]{2,1,0:T(8,128)S(1)} collective-permute-done((f32[16,64,128]{2,1,0:T(8,128)S(1)}, f32[16,64,128]{2,1,0:T(8,128)S(1)}, u32[]{:S(2)}, u32[]{:S(2)}) %collective-permute-start.3) | collective-permute-done | bytes 524320 | tf_op jit(solution)/shard_map/ppermute | solution.py:396
  106.7 5.5 %collective-permute-done.2.refs_2_ = f32[16,64,128]{2,1,0:T(8,128)S(1)} collective-permute-done((f32[16,64,128]{2,1,0:T(8,128)S(1)}, f32[16,64,128]{2,1,0:T(8,128)S(1)}, u32[]{:S(2)}, u32[]{:S(2)}) %collective-permute-start.2) | collective-permute-done | bytes 524320 | tf_op jit(solution)/shard_map/ppermute | solution.py:397
  112.2 2.3 %rates.1 = (f32[64,128]{1,0:T(8,128)}, f32[32,1,128]{2,1,0:T(1,128)}, bf16[2048,128]{1,0:T(8,128)(2,1)}, bf16[2048,128]{1,0:T(8,128)(2,1)}) custom-call(s32[1]{0:T(128)} %bitcast.refs_0_.position_ref, f32[16,128,128]{2,1,0:T(8,128)S(1)} %all_to_all.15.refs_1_, f32[16,64,128]{2,1,0:T(8,128)S(1)} %collective-permute-done.2.refs_2_, ...), custom_call_target="tpu_custom_call" | custom-call | flops 10000000 | bytes 6000000 | tf_op jit(solution)/shard_map/rates/pallas_call | solution.py:415
  114.5 3.8 %all-to-all-start.2 = ((f32[32,1,128]{2,1,0:T(1,128)}), f32[32,1,128]{2,1,0:T(1,128)S(1)}, u32[]{:S(2)}, u32[]{:S(2)}) async-start(f32[32,1,128]{2,1,0:T(1,128)} %get-tuple-element.62), calls=%async_computation.2 | async-start | bytes 32768 | tf_op jit(solution)/shard_map/all_to_all | solution.py:266
  118.4 5.4 %finish.1 = (bf16[128,2048]{1,0:T(8,128)(2,1)}, bf16[128,512]{1,0:T(8,128)(2,1)}, bf16[128,512]{1,0:T(8,128)(2,1)}, f32[64,128]{1,0:T(8,128)}) custom-call(bf16[2048,128]{1,0:T(8,128)(2,1)} %get-tuple-element.48.state_low_ref, bf16[2048,128]{1,0:T(8,128)(2,1)} %get-tuple-element.49.adjoint_low_ref, f32[64,128]{1,0:T(8,128)} %get-tuple-element.50.cross_ref, ...), custom_call_target="tpu_custom_call" | custom-call | flops 1500000000 | bytes 5000000 | tf_op jit(solution)/shard_map/finish/pallas_call | solution.py:435
  123.7 4.4 %all-to-all-done.2 = f32[32,1,128]{2,1,0:T(1,128)S(1)} async-done(((f32[32,1,128]{2,1,0:T(1,128)}), f32[32,1,128]{2,1,0:T(1,128)S(1)}, u32[]{:S(2)}, u32[]{:S(2)}) %all-to-all-start.2) | async-done | bytes 16416 | tf_op jit(solution)/shard_map/all_to_all | solution.py:266
  128.3 1.1 collective-permute-done.4
  129.4 0.4 collective-permute-start.7
  129.9 1.6 %collective-permute-start.6 = (f32[1,128]{1,0:T(1,128)S(1)}, f32[1,128]{1,0:T(1,128)S(1)}, u32[]{:S(2)}, u32[]{:S(2)}) collective-permute-start(f32[1,128]{1,0:T(1,128)S(1)} %bitcast_add_fusion), channel_id=1, source_target_pairs={{0,2},{1,3},{2,4},{3,5},{4,6},{5,7},{6,0},{7,1},{8,10},{9,11},{10,... | collective-permute-start | bytes 1544 | tf_op jit(solution)/shard_map/ppermute | solution.py:271
  131.4 1.3 collective-permute-start.5
  132.8 0.2 collective-permute-done.7
  133.0 0.4 collective-permute-done.6
  133.4 3.1 %collective-permute-done.5 = f32[1,128]{1,0:T(1,128)S(1)} collective-permute-done((f32[1,128]{1,0:T(1,128)S(1)}, f32[1,128]{1,0:T(1,128)S(1)}, u32[]{:S(2)}, u32[]{:S(2)}) %collective-permute-start.5) | collective-permute-done | bytes 544 | tf_op jit(solution)/shard_map/ppermute | solution.py:271
  136.5 0.6 slice_bitcast_fusion
  (36 shorter events, 0.3 us)
Async XLA Ops:
  0.6 11.8 %copy-start.13 = (f32[1,128]{1,0:T(1,128)S(1)}, f32[1,128]{1,0:T(1,128)}, u32[]{:S(2)}) copy-start(f32[1,128]{1,0:T(1,128)} %refs_7_.3) | copy-start | bytes 1540
  0.6 11.8 %copy-start.5 = (bf16[1,128,2048]{2,1,0:T(8,128)(2,1)S(1)}, bf16[1,128,2048]{2,1,0:T(8,128)(2,1)}, u32[]{:S(2)}) copy-start(bf16[1,128,2048]{2,1,0:T(8,128)(2,1)} %param.15) | copy-start | bytes 1572868
  0.7 11.8 %copy-start.9 = (bf16[1,128,512]{2,1,0:T(8,128)(2,1)S(1)}, bf16[1,128,512]{2,1,0:T(8,128)(2,1)}, u32[]{:S(2)}) copy-start(bf16[1,128,512]{2,1,0:T(8,128)(2,1)} %param.14) | copy-start | bytes 393220
  0.7 11.8 %copy-start.8 = (bf16[1,128,512]{2,1,0:T(8,128)(2,1)S(1)}, bf16[1,128,512]{2,1,0:T(8,128)(2,1)}, u32[]{:S(2)}) copy-start(bf16[1,128,512]{2,1,0:T(8,128)(2,1)} %param.13) | copy-start | bytes 393220
  0.7 11.8 %copy-start.14 = (f32[64]{0:T(128)S(1)}, f32[64]{0:T(128)}, u32[]{:S(2)}) copy-start(f32[64]{0:T(128)} %param.11) | copy-start | bytes 772
  0.7 11.8 %copy-start.10 = (f32[1,64,128]{2,1,0:T(8,128)S(1)}, f32[1,64,128]{2,1,0:T(8,128)}, u32[]{:S(2)}) copy-start(f32[1,64,128]{2,1,0:T(8,128)} %param.9) | copy-start | bytes 98308
  0.7 11.8 %copy-start.2 = (bf16[1,128,2048]{2,1,0:T(8,128)(2,1)S(1)}, bf16[1,128,2048]{2,1,0:T(8,128)(2,1)}, u32[]{:S(2)}) copy-start(bf16[1,128,2048]{2,1,0:T(8,128)(2,1)} %param.8) | copy-start | bytes 1572868
  4.3 20.3 %collective-permute-start = (f32[2,528,128]{2,1,0:T(8,128)S(1)}, f32[2,528,128]{2,1,0:T(8,128)S(1)}, u32[]{:S(2)}, u32[]{:S(2)}) collective-permute-start(f32[2,528,128]{2,1,0:T(8,128)S(1)} %get-tuple-element.35), channel_id=1, source_target_pairs={{0,8},{8,16},{16,24},{24,32},{32,40},{40,48},{48,56},{56,64},{64,7... | collective-permute-start | bytes 1622024 | tf_op jit(solution)/shard_map/ppermute | solution.py:347
  6.2 18.4 %collective-permute-start.1 = (f32[2,528,128]{2,1,0:T(8,128)S(1)}, f32[2,528,128]{2,1,0:T(8,128)S(1)}, u32[]{:S(2)}, u32[]{:S(2)}) collective-permute-start(f32[2,528,128]{2,1,0:T(8,128)S(1)} %get-tuple-element.39), channel_id=1, source_target_pairs={{8,0},{16,8},{24,16},{32,24},{40,32},{48,40},{56,48},{64,56},{72,6... | collective-permute-start | bytes 1622024 | tf_op jit(solution)/shard_map/ppermute | solution.py:348
  25.7 37.3 %all-to-all-start = ((f32[16,136,128]{2,1,0:T(8,128)}), f32[16,136,128]{2,1,0:T(8,128)S(1)}, u32[]{:S(2)}, u32[]{:S(2)}) async-start(f32[16,136,128]{2,1,0:T(8,128)} %combine.1), calls=%async_computation | async-start | bytes 2228224 | tf_op jit(solution)/shard_map/all_to_all | solution.py:367
  31.7 1.0 copy-start.3
  32.7 1.0 copy-start.6
  33.8 0.8 copy-start.11
  34.5 0.8 copy-start.15
  37.6 1.0 copy-start
  87.5 7.9 %copy-start.4 = (bf16[1,128,2048]{2,1,0:T(8,128)(2,1)S(1)}, bf16[1,128,2048]{2,1,0:T(8,128)(2,1)}, u32[]{:S(2)}) copy-start(bf16[1,128,2048]{2,1,0:T(8,128)(2,1)} %param.8) | copy-start | bytes 1572868
  87.5 7.9 %copy-start.7 = (bf16[1,128,2048]{2,1,0:T(8,128)(2,1)S(1)}, bf16[1,128,2048]{2,1,0:T(8,128)(2,1)}, u32[]{:S(2)}) copy-start(bf16[1,128,2048]{2,1,0:T(8,128)(2,1)} %param.15) | copy-start | bytes 1572868
  87.5 7.9 %copy-start.12 = (f32[1,64,128]{2,1,0:T(8,128)S(1)}, f32[1,64,128]{2,1,0:T(8,128)}, u32[]{:S(2)}) copy-start(f32[1,64,128]{2,1,0:T(8,128)} %param.9) | copy-start | bytes 98308
  87.5 7.9 %copy-start.16 = (f32[2,2,16,128]{3,2,1,0:T(8,128)S(1)}, f32[2,2,16,128]{3,2,1,0:T(8,128)}, u32[]{:S(2)}) copy-start(f32[2,2,16,128]{3,2,1,0:T(8,128)} %get-tuple-element.41.cum_ref) | copy-start | bytes 98308
  87.6 19.1 %collective-permute-start.3 = (f32[16,64,128]{2,1,0:T(8,128)S(1)}, f32[16,64,128]{2,1,0:T(8,128)S(1)}, u32[]{:S(2)}, u32[]{:S(2)}) collective-permute-start(f32[16,64,128]{2,1,0:T(8,128)S(1)} %get-tuple-element.64), channel_id=1, source_target_pairs={{8,0},{16,8},{24,16},{32,24},{40,32},{48,40},{56,48},{64,56},{72,6... | collective-permute-start | bytes 1572872 | tf_op jit(solution)/shard_map/ppermute | solution.py:396
  95.4 16.9 %copy-start.1 = (f32[2048,128]{1,0:T(8,128)S(1)}, f32[2048,128]{1,0:T(8,128)}, u32[]{:S(2)}) copy-start(f32[2048,128]{1,0:T(8,128)} %copy-done) | copy-start | bytes 3145732
  95.4 16.9 %collective-permute-start.2 = (f32[16,64,128]{2,1,0:T(8,128)S(1)}, f32[16,64,128]{2,1,0:T(8,128)S(1)}, u32[]{:S(2)}, u32[]{:S(2)}) collective-permute-start(f32[16,64,128]{2,1,0:T(8,128)S(1)} %get-tuple-element.65), channel_id=1, source_target_pairs={{0,8},{8,16},{16,24},{24,32},{32,40},{40,48},{48,56},{56,64},{64,7... | collective-permute-start | bytes 1572872 | tf_op jit(solution)/shard_map/ppermute | solution.py:397
  114.5 13.6 %all-to-all-start.2 = ((f32[32,1,128]{2,1,0:T(1,128)}), f32[32,1,128]{2,1,0:T(1,128)S(1)}, u32[]{:S(2)}, u32[]{:S(2)}) async-start(f32[32,1,128]{2,1,0:T(1,128)} %get-tuple-element.62), calls=%async_computation.2 | async-start | bytes 32768 | tf_op jit(solution)/shard_map/all_to_all | solution.py:266
  128.2 1.2 collective-permute-start.4
  129.4 3.5 %collective-permute-start.7 = (f32[1,128]{1,0:T(1,128)S(1)}, f32[1,128]{1,0:T(1,128)S(1)}, u32[]{:S(2)}, u32[]{:S(2)}) collective-permute-start(f32[1,128]{1,0:T(1,128)S(1)} %bitcast_add_fusion), channel_id=1, source_target_pairs={{0,6},{1,7},{2,0},{3,1},{4,2},{5,3},{6,4},{7,5},{8,14},{9,15},{10,... | collective-permute-start | bytes 1544 | tf_op jit(solution)/shard_map/ppermute | solution.py:271
  129.9 3.5 %collective-permute-start.6 = (f32[1,128]{1,0:T(1,128)S(1)}, f32[1,128]{1,0:T(1,128)S(1)}, u32[]{:S(2)}, u32[]{:S(2)}) collective-permute-start(f32[1,128]{1,0:T(1,128)S(1)} %bitcast_add_fusion), channel_id=1, source_target_pairs={{0,2},{1,3},{2,4},{3,5},{4,6},{5,7},{6,0},{7,1},{8,10},{9,11},{10,... | collective-permute-start | bytes 1544 | tf_op jit(solution)/shard_map/ppermute | solution.py:271
  131.4 5.0 %collective-permute-start.5 = (f32[1,128]{1,0:T(1,128)S(1)}, f32[1,128]{1,0:T(1,128)S(1)}, u32[]{:S(2)}, u32[]{:S(2)}) collective-permute-start(f32[1,128]{1,0:T(1,128)S(1)} %bitcast_add_fusion), channel_id=1, source_target_pairs={{0,4},{1,5},{2,6},{3,7},{4,0},{5,1},{6,2},{7,3},{8,12},{9,13},{10,... | collective-permute-start | bytes 1544 | tf_op jit(solution)/shard_map/ppermute | solution.py:271
